TPU v7x, 512 devices: a whole 4x4x16 slice. The times are simulated.
512 devices in a mesh: surf: 64 (over x, y, z_lo), field: 8 (over z_hi, core).
Axes of the slice: x: 4, y: 4, z: 16 (z_hi: 4, z_lo: 4; z = z_hi * 4 + z_lo), core: 2. Of those that a mesh axis runs over, the one named last changes fastest.
Arguments:
- forces: bfloat16 [4, 2, 512, 128], P(None, None, 'surf'), may hold values from -6 to 6
- response: bfloat16 [4, 2, 65536, 512], P(None, None, ('surf', 'field'))
- panel_plane: float32 [2, 65536], P(None, 'surf'), may hold values from -1 to 1
- panel_area: float32 [65536], P('surf'), may hold values from 0.002 to 0.008
- field_points: float32 [3, 4096], P(None, 'field'), may hold values from -1.1 to 1.1, as said below
- wavenumber: float32 [4], replicated, may hold values from 2 to 8
Outputs:
- pressure: bfloat16 [4096, 4, 2, 128], P(('field', 'surf'))
- efficiency: float32 [4, 128], replicated
Inputs may be any that keep to these rules, and one draw needn't show every extreme that they name: `field_points`: rows are x, y and height; heights lie between 0.02 and 0.7.
All inputs are finite; a program needn't handle non-finite values.
Results may differ from a plain program's by a relative error of at most 0.0058.
Values may be sent and summed in bfloat16 or wider, within the bound.
No kernel may reach another device: no remote copies, remote signals or barrier semaphores. Data moves between devices by JAX's collectives and lax.ppermute only.
A program may use at most 64 MiB of HBM per device.

v0:
```python
import math

import jax
import jax.numpy as jnp
from jax import lax
from jax.sharding import PartitionSpec as P


def complex_matrix(real_part, imag_part):
    upper = jnp.concatenate([real_part, imag_part], axis=-1)
    lower = jnp.concatenate([-imag_part, real_part], axis=-1)
    return jnp.concatenate([upper, lower], axis=0)


def plane_distance(points, panel_plane):
    offset_x = points[0][:, None] - panel_plane[0][None, :]
    offset_y = points[1][:, None] - panel_plane[1][None, :]
    height = points[2][:, None]
    return jnp.sqrt(offset_x * offset_x + offset_y * offset_y + height * height)


def kernel_tiles(distance, panel_area, wave):
    phase = wave * distance
    sine_part = panel_area[None, :] * jnp.sin(phase) / distance
    cosine_part = panel_area[None, :] * jnp.cos(phase) / distance
    return jnp.concatenate([sine_part, cosine_part], axis=1).astype(jnp.bfloat16)


def shards(forces, response, panel_plane, panel_area, field_points, wavenumber):
    lines = response.shape[0]
    cases = forces.shape[3]
    all_forces = lax.all_gather(forces, "surf", axis=2, tiled=True)
    velocity_list = []
    for line in range(lines):
        operand = jnp.concatenate([response[line, 0], response[line, 1]], axis=1)
        driving = complex_matrix(all_forces[line, 0], all_forces[line, 1])
        velocity_list.append(
            jnp.dot(operand, driving, preferred_element_type=jnp.float32).astype(jnp.bfloat16)
        )
    velocity = jnp.stack(velocity_list)
    squares = jnp.sum(jnp.square(velocity.astype(jnp.float32)), axis=1)
    energy_part = squares[:, :cases] + squares[:, cases:]
    energy_total = lax.psum(energy_part, ("surf", "field"))
    shard_velocity = lax.all_gather(velocity, "field", axis=1, tiled=True)
    stacked = [
        complex_matrix(shard_velocity[line, :, :cases], shard_velocity[line, :, cases:])
        for line in range(lines)
    ]
    rows = field_points.shape[1] // lax.axis_size("surf")

    def line_term(distance, line):
        tiles = kernel_tiles(distance, panel_area, wavenumber[line])
        summed = jnp.dot(tiles, stacked[line], preferred_element_type=jnp.float32)
        return wavenumber[line] / (2.0 * math.pi) * summed

    distance = plane_distance(field_points, panel_plane)
    summed_total = lax.psum_scatter(
        jnp.stack([line_term(distance, line) for line in range(lines)], axis=1),
        "surf",
        scatter_dimension=0,
        tiled=True,
    )
    pressure = summed_total.astype(jnp.bfloat16).reshape(rows, lines, 2, cases)
    power_part = jnp.sum(jnp.square(pressure.astype(jnp.float32)), axis=(0, 2))
    power_total = lax.psum(power_part, ("surf", "field"))
    point_total = field_points.shape[1] * lax.axis_size("field")
    panel_total = velocity.shape[1] * lax.axis_size("surf") * lax.axis_size("field")
    efficiency = power_total / point_total / (energy_total / panel_total + 1e-06)
    return (pressure, efficiency)


def solution(mesh):
    return jax.shard_map(
        shards,
        mesh=mesh,
        in_specs=(
            P(None, None, "surf", None),
            P(None, None, ("surf", "field"), None),
            P(None, "surf"),
            P("surf"),
            P(None, "field"),
            P(),
        ),
        out_specs=(P(("field", "surf"), None, None, None), P()),
        check_vma=False,
    )
```

profile of v0, /device:TPU:1, one launch (start us, length us, event | category | flops | bytes accessed | tf_op | source)
XLA Modules:
  0.0 849.1 jit_solution(3231261848175256884)
XLA Ops:
  7.2 0.7 all-gather.3.cloned.1.call-update
  7.9 1.4 slice_bitcast_fusion.23
  9.3 242.3 %all-gather.3.cloned.1.call-done = bf16[4,2,512,128]{3,2,1,0:T(8,128)(2,1)} async-done(((bf16[4,2,8,128]{3,2,1,0:T(8,128)(2,1)}), bf16[4,2,512,128]{3,2,1,0:T(8,128)(2,1)}) %all-gather.3.cloned.1.call-update) | async-done | bytes 1048592 | tf_op jit(solution)/shard_map/all_gather | solution.py:32
  251.6 1.2 fusion.124
  252.8 1.4 slice_bitcast_fusion.14
  254.2 0.2 fusion.47
  254.4 0.2 fusion.45
  254.6 0.2 fusion.44
  254.9 0.2 fusion.46
  255.2 0.7 multiply_reduce_fusion
  255.9 0.0 reduce-scatter.2.cloned.1.call-start
  256.0 0.6 fusion.134
  259.2 36.1 %divide_convert_fusion.7 = (bf16[512,1024]{1,0:T(8,128)(2,1)S(1)}, bf16[512,1024]{1,0:T(8,128)(2,1)S(1)}, bf16[512,1024]{1,0:T(8,128)(2,1)S(1)}, bf16[512,1024]{...) fusion(f32[512]{0:T(512)S(1)} %bitcast.96, ...), kind=kLoop, calls=%fused_computation.24 | loop fusion | flops 17825792 | bytes 8407056 | tf_op jit(solution)/shard_map/convert.6
  295.2 58.9 %all-gather.5.cloned.1.call-done = bf16[4,1024,256]{2,1,0:T(8,128)(2,1)} async-done(((bf16[4,128,256]{2,1,0:T(8,128)(2,1)}), bf16[4,1024,256]{2,1,0:T(8,128)(2,1)}) %all-gather.5.cloned.1.call-update) | async-done | bytes 2097168 | tf_op jit(solution)/shard_map/all_gather | solution.py:44
  354.1 1.5 fusion.128
  355.6 0.4 copy-done
  356.0 0.4 slice_bitcast_fusion.6
  356.4 0.8 copy-done.8
  357.2 0.3 copy-done.9
  357.5 0.7 fusion.29
  358.3 0.5 copy-done.6
  358.8 0.3 copy-done.7
  359.1 0.7 fusion.35
  359.8 0.5 copy-done.5
  360.3 0.7 fusion.41
  361.0 0.7 fusion.23
  361.8 1.5 pad_maximum_fusion
  363.3 327.7 %reduce-scatter.2.cloned.1.call-done = f32[8,4,256]{2,0,1:T(8,128)} async-done(((f32[512,4,256]{2,0,1:T(8,128)}), f32[8,4,256]{2,0,1:T(8,128)}) %reduce-scatter.2.cloned.1.call-update) | async-done | bytes 32784 | tf_op jit(solution)/shard_map/reduce_scatter | solution.py:57
  691.0 0.8 multiply_reduce_fusion.1
  691.8 0.6 copy.9
  692.4 149.6 %all-reduce = (f32[4,128]{1,0:T(4,128)S(1)}, f32[4,128]{1,0:T(4,128)S(1)}) all-reduce(f32[4,128]{1,0:T(4,128)S(1)} %slice_add_fusion, f32[4,128]{1,0:T(4,128)S(1)} %bitcast_reduce_fusion), channel_id=1, replica_groups=mesh['surf'=64,'field'=8] {'surf','field'}, use_global_device_ids=true, to_apply=%region_5.6 | all-reduce | flops 1024 | bytes 8192 | tf_op jit(solution)/shard_map/psum | solution.py:43
  842.0 0.6 add_divide_fusion
  (22 shorter events, 0.2 us)
Async XLA Ops:
  7.2 244.5 %all-gather.3.cloned.1.call-start = ((), (), s32[]{:S(2)}) async-start(), calls=%async_computation.1 | async-start | bytes 1064960 | tf_op jit(solution)/shard_map/all_gather | solution.py:32
  7.9 346.2 %all-gather.5.cloned.1.call-start = ((), (), s32[]{:S(2)}) async-start(), calls=%async_computation.2 | async-start | bytes 2359296 | tf_op jit(solution)/shard_map/all_gather | solution.py:44
  254.9 1.1 copy-start.2
  254.9 4.2 copy-start.3
  254.9 4.2 copy-start.1
  254.9 4.2 copy-start.4
  255.9 435.0 %reduce-scatter.2.cloned.1.call-start = ((), (), s32[]{:S(2)}) async-start(), calls=%async_computation.3 | async-start | bytes 2129920 | tf_op jit(solution)/shard_map/reduce_scatter | solution.py:57
  354.1 1.9 copy-start
  356.0 1.2 copy-start.8
  356.0 1.5 copy-start.9
  357.5 1.2 copy-start.6
  357.5 1.5 copy-start.7
  359.1 1.2 copy-start.5
Sparse Core Ops, SparseCore 0:
  10.0 241.6 all-gather.2
  256.1 97.9 all-gather.4
  363.4 327.5 reduce-scatter.1
where the time goes:
time: 850 us; the launch traced here: 849 us
  waiting for transfers between devices  630 us (74%)
  blocking collectives  150 us (18%)
  other arithmetic  42.3 us (5%)
  between operations  16.4 us (2%)
    reduce_scatter x1, waiting for transfers between devices, shards(): lax.psum_scatter(jnp.stack([line_term(distance, line) for line in range(l...  328 us
    all_gather x1, waiting for transfers between devices, shards(): all_forces = lax.all_gather(forces, 'surf', axis=2, tiled=True)  242 us
    psum x1, blocking collectives, shards(): energy_total = lax.psum(energy_part, ('surf', 'field'))  150 us
    all_gather x1, waiting for transfers between devices, shards(): shard_velocity = lax.all_gather(velocity, 'field', axis=1, tiled=True)  58.9 us
    another operation x1, other arithmetic  36.1 us
  transfers between devices with their start and end apart: 3, of which 3 were waited for; matrix products, arithmetic and copies ran while one was open for 4% of the time, Pallas kernels for 0%

commit v1 on v0

v1 whole, which is shorter than its diff:
```python
import math

import jax
import jax.numpy as jnp
import numpy as np
from jax import lax
from jax.sharding import Mesh, PartitionSpec as P

SURF = ("x", "y", "zl")
FIELD = ("zh", "c")
DEPTH = ("zh", "zl")
SWAP = [(0, 1), (1, 0)]


def complex_matrix(real_part, imag_part):
    upper = jnp.concatenate([real_part, imag_part], axis=-1)
    lower = jnp.concatenate([-imag_part, real_part], axis=-1)
    return jnp.concatenate([upper, lower], axis=0)


def plane_distance(points, panel_plane):
    offset_x = points[0][:, None] - panel_plane[0][None, :]
    offset_y = points[1][:, None] - panel_plane[1][None, :]
    height = points[2][:, None]
    return jnp.sqrt(offset_x * offset_x + offset_y * offset_y + height * height)


def kernel_tiles(distance, panel_area, wave):
    phase = wave * distance
    sine_part = panel_area[None, :] * jnp.sin(phase) / distance
    cosine_part = panel_area[None, :] * jnp.cos(phase) / distance
    return jnp.concatenate([sine_part, cosine_part], axis=1).astype(jnp.bfloat16)


def exchange(array, axes):
    return lax.all_to_all(array, axes, 0, 0, tiled=True)


def gather(array, axes):
    size = lax.axis_size(axes)
    return exchange(jnp.broadcast_to(array[None], (size,) + array.shape), axes)


def ring_gather(array, axis):
    size = lax.axis_size(axis)
    me = lax.axis_index(axis)
    parts = [array]
    for step in range(1, size):
        parts.append(lax.ppermute(array, axis, [(i, (i - step) % size) for i in range(size)]))
    twice = jnp.stack(parts + parts)
    return lax.dynamic_slice_in_dim(twice, (size - me) % size, size, 0)


def shards(forces, response, panel_plane, panel_area, field_points, wavenumber):
    lines, _, channels, cases = forces.shape
    own = response.shape[2]
    x_size, y_size = lax.axis_size("x"), lax.axis_size("y")
    depth_size = lax.axis_size(DEPTH)
    core = lax.axis_index("c")
    rows = field_points.shape[1] // lax.axis_size(SURF)
    share = rows * y_size * lax.axis_size("zl")

    my_points = lax.dynamic_slice_in_dim(field_points, lax.axis_index("x") * share, share, 1)
    all_points = ring_gather(my_points, "zh")
    points = all_points.reshape(-1, 3, y_size, share // y_size).transpose(1, 2, 0, 3).reshape(3, -1)

    panels = jnp.concatenate([panel_plane, panel_area[None]], axis=0)
    my_panels = lax.dynamic_slice_in_dim(panels, lax.axis_index("zh") * 2 * own, 2 * own, 1)
    panels = gather(my_panels, "x")
    panels = panels.reshape(x_size, 3, 2, own).transpose(1, 2, 0, 3)
    panels = jnp.where(core == 0, panels, panels[:, ::-1]).reshape(3, -1)

    part = jnp.where(core == 0, forces[:, 0], forces[:, 1])
    part = gather(part, SURF)
    part = part.transpose(1, 0, 2, 3).reshape(lines, -1, cases)
    other = lax.ppermute(part, "c", SWAP)
    real_part = jnp.where(core == 0, part, other)
    imag_part = jnp.where(core == 0, other, part)

    velocity_list = []
    for line in range(lines):
        operand = jnp.concatenate([response[line, 0], response[line, 1]], axis=1)
        driving = complex_matrix(real_part[line], imag_part[line])
        velocity_list.append(
            jnp.dot(operand, driving, preferred_element_type=jnp.float32).astype(jnp.bfloat16)
        )
    velocity = jnp.stack(velocity_list)
    squares = jnp.sum(jnp.square(velocity.astype(jnp.float32)), axis=1)
    energy_part = squares[:, :cases] + squares[:, cases:]

    near = gather(velocity, "x")
    shared = jnp.stack([near, lax.ppermute(near, "c", SWAP)])
    shared = shared.transpose(2, 0, 1, 3, 4).reshape(lines, -1, 2 * cases)

    distance = plane_distance(points, panels)
    partial = []
    for line in range(lines):
        tiles = kernel_tiles(distance, panels[2], wavenumber[line])
        stacked = complex_matrix(shared[line, :, :cases], shared[line, :, cases:])
        summed = jnp.dot(tiles, stacked, preferred_element_type=jnp.float32)
        partial.append(summed.astype(jnp.bfloat16).reshape(y_size, -1, 2 * cases))
    partial = jnp.stack(partial, axis=1)

    beside = exchange(partial, "y")
    level = jnp.sum(beside.astype(jnp.float32), axis=0).astype(jnp.bfloat16)
    level = level.reshape(lines, depth_size, rows, 2 * cases).transpose(1, 0, 2, 3)
    column = exchange(level, DEPTH)
    total = jnp.sum(column.astype(jnp.float32), axis=0)
    total = total * (wavenumber / (2.0 * math.pi))[:, None, None]
    pressure = total.astype(jnp.bfloat16)
    power = jnp.sum(jnp.square(pressure.astype(jnp.float32)), axis=1)
    power_part = power[:, :cases] + power[:, cases:]

    sums = jnp.concatenate([energy_part, power_part], axis=0)
    sums = jnp.sum(gather(sums, ("x", "y")), axis=0)
    sums = jnp.sum(gather(sums, DEPTH + ("c",)), axis=0)
    point_total = field_points.shape[1] * lax.axis_size(FIELD)
    panel_total = own * lax.axis_size(SURF + FIELD)
    efficiency = sums[lines:] / point_total / (sums[:lines] / panel_total + 1e-06)
    pressure = pressure.transpose(1, 0, 2).reshape(rows, lines, 2, cases)
    return (pressure, efficiency)


def solution(mesh):
    grid = Mesh(np.asarray(mesh.devices).reshape(4, 4, 4, 4, 2), SURF + FIELD)
    return jax.shard_map(
        shards,
        mesh=grid,
        in_specs=(
            P(None, None, SURF, None),
            P(None, None, SURF + FIELD, None),
            P(None, SURF),
            P(SURF),
            P(None, FIELD),
            P(),
        ),
        out_specs=(P(FIELD + SURF, None, None, None), P()),
        check_vma=False,
    )
```

time: 850 us -> 195 us (0.23)
  waiting for transfers between devices: 630 us -> 44.9 us
  blocking collectives: 150 us -> 27.9 us
  starting transfers between devices: 0.12 us -> 71 us
  between operations: 16.4 us -> 1 us
    reduce_scatter x1 -> x0, waiting for transfers between devices: 328 us -> none  [shards(): lax.psum_scatter(jnp.stack([line_term(distance, line) for line in range(l...]
    all_gather x2 -> x0, waiting for transfers between devices: 301 us -> none  [the longest x1 242 us: shards(): all_forces = lax.all_gather(forces, 'surf', axis=2, tiled=True)]
    psum x1 -> x0, blocking collectives: 150 us -> none  [shards(): energy_total = lax.psum(energy_part, ('surf', 'field'))]
    all_to_all x0 -> x5, waiting for transfers between devices: none -> 42.1 us  [exchange(): return lax.all_to_all(array, axes, 0, 0, tiled=True)]
    all_to_all x0 -> x5, starting transfers between devices: none -> 40.3 us  [exchange(): return lax.all_to_all(array, axes, 0, 0, tiled=True)]
    ppermute x0 -> x5, starting transfers between devices: none -> 30.7 us  [the longest x3 21.9 us: ring_gather(): lax.ppermute(array, axis, [(i, (i - step) % size) for i in range(size)])]
    all_to_all x0 -> x2, blocking collectives: none -> 27.9 us  [exchange(): return lax.all_to_all(array, axes, 0, 0, tiled=True)]
    another operation x2 -> x3, other arithmetic: 37.6 us -> 35.4 us
  transfers between devices with their start and end apart: 3 -> 10, of which waited for: 3 -> 5; matrix products, arithmetic and copies ran while one was open for 4% -> 20% of each run, Pallas kernels for 0% -> 0%
where the time goes in v1:
time: 195 us; the launch traced here: 194 us
  starting transfers between devices  71 us (36%)
  waiting for transfers between devices  44.9 us (23%)
  other arithmetic  37.7 us (19%)
  blocking collectives  27.9 us (14%)
  local copies, waits for them, and re-layouts  7.87 us (4%)
  matrix products  3.81 us (2%)
    all_to_all x5, waiting for transfers between devices, exchange(): return lax.all_to_all(array, axes, 0, 0, tiled=True)  42.1 us
    all_to_all x5, starting transfers between devices, exchange(): return lax.all_to_all(array, axes, 0, 0, tiled=True)  40.3 us
    another operation x1, other arithmetic  35 us
    all_to_all x2, blocking collectives, exchange(): return lax.all_to_all(array, axes, 0, 0, tiled=True)  27.9 us
    ppermute x3, starting transfers between devices, ring_gather(): lax.ppermute(array, axis, [(i, (i - step) % size) for i in range(size)])  21.9 us
    ppermute x1, starting transfers between devices, shards(): other = lax.ppermute(part, 'c', SWAP)  5.13 us
  transfers between devices with their start and end apart: 10, of which 5 were waited for; matrix products, arithmetic and copies ran while one was open for 20% of the time, Pallas kernels for 0%

profile of v1, /device:TPU:1, one launch (start us, length us, event | category | flops | bytes accessed | tf_op | source)
XLA Modules:
  0.0 194.2 jit_solution(16038369326351164146)
XLA Ops:
  0.7 0.8 select_bitcast_fusion
  1.5 0.9 broadcast_in_dim.14
  2.3 12.5 %all-to-all-start.1 = ((bf16[64,4,8,128]{3,2,1,0:T(8,128)(2,1)}), bf16[64,4,8,128]{3,2,1,0:T(8,128)(2,1)S(1)}, u32[]{:S(2)}, u32[]{:S(2)}) async-start(bf16[64,4,8,128]{3,2,1,0:T(8,128)(2,1)} %broadcast_in_dim.14), calls=%async_computation.1 | async-start | bytes 1048576 | tf_op jit(solution)/shard_map/all_to_all | solution.py:36
  14.9 0.7 constant_dynamic-update-slice_fusion.7
  15.6 8.8 %collective-permute-start.2 = (f32[3,128]{1,0:T(4,128)S(1)}, f32[3,128]{1,0:T(4,128)S(1)}, u32[]{:S(2)}, u32[]{:S(2)}) collective-permute-start(f32[3,128]{1,0:T(4,128)S(1)} %get-tuple-element.9), channel_id=1, source_target_pairs={{0,2},{2,4},{4,6},{6,0},{1,3},{3,5},{5,7},{7,1},{8,10},{10,12},{12... | collective-permute-start | bytes 4616 | tf_op jit(solution)/shard_map/ppermute | solution.py:49
  24.4 7.9 %collective-permute-start.1 = (f32[3,128]{1,0:T(4,128)S(1)}, f32[3,128]{1,0:T(4,128)S(1)}, u32[]{:S(2)}, u32[]{:S(2)}) collective-permute-start(f32[3,128]{1,0:T(4,128)S(1)} %get-tuple-element.9), channel_id=1, source_target_pairs={{0,4},{2,6},{4,0},{6,2},{1,5},{3,7},{5,1},{7,3},{8,12},{10,14},{12... | collective-permute-start | bytes 4616 | tf_op jit(solution)/shard_map/ppermute | solution.py:49
  32.3 5.2 %collective-permute-start = (f32[3,128]{1,0:T(4,128)S(1)}, f32[3,128]{1,0:T(4,128)S(1)}, u32[]{:S(2)}, u32[]{:S(2)}) collective-permute-start(f32[3,128]{1,0:T(4,128)S(1)} %get-tuple-element.9), channel_id=1, source_target_pairs={{0,6},{2,0},{4,2},{6,4},{1,7},{3,1},{5,3},{7,5},{8,14},{10,8},{12,... | collective-permute-start | bytes 4616 | tf_op jit(solution)/shard_map/ppermute | solution.py:49
  37.5 1.5 fusion.124
  39.2 1.4 collective-permute-done
  40.6 0.6 broadcast_in_dim.13
  41.2 3.9 %all-to-all-start = ((f32[4,3,256]{2,1,0:T(4,128)}), f32[4,3,256]{2,1,0:T(4,128)S(1)}, u32[]{:S(2)}, u32[]{:S(2)}) async-start(f32[4,3,256]{2,1,0:T(4,128)} %broadcast_in_dim.13), calls=%async_computation | async-start | bytes 32768 | tf_op jit(solution)/shard_map/all_to_all | solution.py:36
  45.2 5.1 %collective-permute-start.3 = (bf16[4,512,128]{2,1,0:T(8,128)(2,1)S(1)}, bf16[4,512,128]{2,1,0:T(8,128)(2,1)S(1)}, u32[]{:S(2)}, u32[]{:S(2)}) collective-permute-start(bf16[4,512,128]{2,1,0:T(8,128)(2,1)S(1)} %bitcast.142), channel_id=1, source_target_pairs={{0,1},{1,0},{2,3},{3,2},{4,5},{5,4},{6,7},{7,6},{8,9},{9,8},{10,11... | collective-permute-start | bytes 1572872 | tf_op jit(solution)/shard_map/ppermute | solution.py:76
  50.4 1.5 collective-permute-done.3
  53.2 1.1 broadcast_in_dim.15
  54.3 4.5 %all-to-all-start.2 = ((bf16[4,4,128,256]{3,2,1,0:T(8,128)(2,1)}), bf16[4,4,128,256]{3,2,1,0:T(8,128)(2,1)S(1)}, u32[]{:S(2)}, u32[]{:S(2)}) async-start(bf16[4,4,128,256]{3,2,1,0:T(8,128)(2,1)} %broadcast_in_dim.15), calls=%async_computation.2 | async-start | bytes 2097152 | tf_op jit(solution)/shard_map/all_to_all | solution.py:36
  59.2 14.1 %all-to-all-done.2 = bf16[4,4,128,256]{3,2,1,0:T(8,128)(2,1)S(1)} async-done(((bf16[4,4,128,256]{3,2,1,0:T(8,128)(2,1)}), bf16[4,4,128,256]{3,2,1,0:T(8,128)(2,1)S(1)}, u32[]{:S(2)}, u32[]{:S(2)}) %all-to-all-start.2) | async-done | bytes 1048608 | tf_op jit(solution)/shard_map/all_to_all | solution.py:36
  73.4 3.6 %collective-permute-start.4 = (bf16[4,4,128,256]{3,2,0,1:T(8,128)(2,1)S(1)}, bf16[4,4,128,256]{3,2,0,1:T(8,128)(2,1)S(1)}, u32[]{:S(2)}, u32[]{:S(2)}) collective-permute-start(bf16[4,4,128,256]{3,2,0,1:T(8,128)(2,1)S(1)} %copy.75), channel_id=1, source_target_pairs={{0,1},{1,0},{2,3},{3,2},{4,5},{5,4},{6,7},{7,6},{8,9},{9,8},{10,11... | collective-permute-start | bytes 3145736 | tf_op jit(solution)/shard_map/ppermute | solution.py:92
  77.0 35.0 %divide_convert_fusion.7 = (bf16[512,1024]{1,0:T(8,128)(2,1)S(1)}, bf16[512,1024]{1,0:T(8,128)(2,1)S(1)}, bf16[512,1024]{1,0:T(8,128)(2,1)S(1)}, bf16[512,1024]{...) fusion(f32[512]{0:T(512)S(1)} %mul.118, ...), kind=kLoop, calls=%fused_computation.24 | loop fusion | flops 17825792 | bytes 8407056 | tf_op jit(solution)/shard_map/convert.7
  112.8 0.7 fusion.23
  113.6 0.7 fusion.26
  114.3 0.7 fusion.29
  115.0 0.7 fusion.20
  115.9 18.7 %all_to_all.35 = bf16[4,4,128,256]{3,2,1,0:T(8,128)(2,1)S(1)} all-to-all(bf16[4,4,128,256]{3,2,1,0:T(8,128)(2,1)S(1)} %pad_maximum_fusion.1), channel_id=1, replica_groups=mesh['x'=4,'y'=4,'zl'=4,'zh'=4,'c'=2] {'y'}, dimensions={0} | all-to-all | bytes 2097152 | tf_op jit(solution)/shard_map/all_to_all | solution.py:36
  134.8 0.7 copy.63
  135.5 5.5 %all-to-all-start.4 = ((bf16[16,4,8,256]{3,2,1,0:T(8,128)(2,1)}), bf16[16,4,8,256]{3,2,1,0:T(8,128)(2,1)S(1)}, u32[]{:S(2)}, u32[]{:S(2)}) async-start(bf16[16,4,8,256]{3,2,1,0:T(8,128)(2,1)} %copy.63), calls=%async_computation.4 | async-start | bytes 524288 | tf_op jit(solution)/shard_map/all_to_all | solution.py:36
  141.1 12.7 %all-to-all-done.4 = bf16[16,4,8,256]{3,2,1,0:T(8,128)(2,1)S(1)} async-done(((bf16[16,4,8,256]{3,2,1,0:T(8,128)(2,1)}), bf16[16,4,8,256]{3,2,1,0:T(8,128)(2,1)S(1)}, u32[]{:S(2)}, u32[]{:S(2)}) %all-to-all-start.4) | async-done | bytes 262176 | tf_op jit(solution)/shard_map/all_to_all | solution.py:36
  154.0 9.2 %all_to_all.36 = f32[16,8,128]{2,1,0:T(8,128)S(1)} all-to-all(f32[16,8,128]{2,1,0:T(8,128)S(1)} %broadcast_in_dim.16), channel_id=1, replica_groups=mesh['x'=4,'y'=4,'zl'=4,'zh'=4,'c'=2] {'x','y'}, dimensions={0} | all-to-all | bytes 131072 | tf_op jit(solution)/shard_map/all_to_all | solution.py:36
  163.2 0.7 broadcast_in_dim.17
  163.9 13.9 %all-to-all-start.6 = ((f32[32,8,128]{2,1,0:T(8,128)}), f32[32,8,128]{2,1,0:T(8,128)S(1)}, u32[]{:S(2)}, u32[]{:S(2)}) async-start(f32[32,8,128]{2,1,0:T(8,128)} %broadcast_in_dim.17), calls=%async_computation.6 | async-start | bytes 262144 | tf_op jit(solution)/shard_map/all_to_all | solution.py:36
  177.7 0.6 copy.64
  178.3 15.2 %all-to-all-done.6 = f32[32,8,128]{2,1,0:T(8,128)S(1)} async-done(((f32[32,8,128]{2,1,0:T(8,128)}), f32[32,8,128]{2,1,0:T(8,128)S(1)}, u32[]{:S(2)}, u32[]{:S(2)}) %all-to-all-start.6) | async-done | bytes 131104 | tf_op jit(solution)/shard_map/all_to_all | solution.py:36
  193.6 0.6 add_divide_fusion
  (59 shorter events, 3.3 us)
Async XLA Ops:
  0.6 38.4 %copy-start = (bf16[4,2,128,512]{3,2,1,0:T(8,128)(2,1)S(1)}, bf16[4,2,128,512]{3,2,1,0:T(8,128)(2,1)}, u32[]{:S(2)}) copy-start(bf16[4,2,128,512]{3,2,1,0:T(8,128)(2,1)} %param.7) | copy-start | bytes 3145732
  0.6 38.4 %copy-start.3 = (f32[1024]{0:T(1024)S(1)}, f32[1024]{0:T(1024)}, u32[]{:S(2)}) copy-start(f32[1024]{0:T(1024)} %param.9) | copy-start | bytes 12292
  0.7 38.4 %copy-start.1 = (f32[2,1024]{1,0:T(2,128)S(1)}, f32[2,1024]{1,0:T(2,128)}, u32[]{:S(2)}) copy-start(f32[2,1024]{1,0:T(2,128)} %param.8) | copy-start | bytes 24580
  2.3 38.3 %all-to-all-start.1 = ((bf16[64,4,8,128]{3,2,1,0:T(8,128)(2,1)}), bf16[64,4,8,128]{3,2,1,0:T(8,128)(2,1)S(1)}, u32[]{:S(2)}, u32[]{:S(2)}) async-start(bf16[64,4,8,128]{3,2,1,0:T(8,128)(2,1)} %broadcast_in_dim.14), calls=%async_computation.1 | async-start | bytes 1048576 | tf_op jit(solution)/shard_map/all_to_all | solution.py:36
  15.6 25.0 %collective-permute-start.2 = (f32[3,128]{1,0:T(4,128)S(1)}, f32[3,128]{1,0:T(4,128)S(1)}, u32[]{:S(2)}, u32[]{:S(2)}) collective-permute-start(f32[3,128]{1,0:T(4,128)S(1)} %get-tuple-element.9), channel_id=1, source_target_pairs={{0,2},{2,4},{4,6},{6,0},{1,3},{3,5},{5,7},{7,1},{8,10},{10,12},{12... | collective-permute-start | bytes 4616 | tf_op jit(solution)/shard_map/ppermute | solution.py:49
  24.4 16.2 %collective-permute-start.1 = (f32[3,128]{1,0:T(4,128)S(1)}, f32[3,128]{1,0:T(4,128)S(1)}, u32[]{:S(2)}, u32[]{:S(2)}) collective-permute-start(f32[3,128]{1,0:T(4,128)S(1)} %get-tuple-element.9), channel_id=1, source_target_pairs={{0,4},{2,6},{4,0},{6,2},{1,5},{3,7},{5,1},{7,3},{8,12},{10,14},{12... | collective-permute-start | bytes 4616 | tf_op jit(solution)/shard_map/ppermute | solution.py:49
  32.3 8.2 %collective-permute-start = (f32[3,128]{1,0:T(4,128)S(1)}, f32[3,128]{1,0:T(4,128)S(1)}, u32[]{:S(2)}, u32[]{:S(2)}) collective-permute-start(f32[3,128]{1,0:T(4,128)S(1)} %get-tuple-element.9), channel_id=1, source_target_pairs={{0,6},{2,0},{4,2},{6,4},{1,7},{3,1},{5,3},{7,5},{8,14},{10,8},{12,... | collective-permute-start | bytes 4616 | tf_op jit(solution)/shard_map/ppermute | solution.py:49
  41.2 11.9 %all-to-all-start = ((f32[4,3,256]{2,1,0:T(4,128)}), f32[4,3,256]{2,1,0:T(4,128)S(1)}, u32[]{:S(2)}, u32[]{:S(2)}) async-start(f32[4,3,256]{2,1,0:T(4,128)} %broadcast_in_dim.13), calls=%async_computation | async-start | bytes 32768 | tf_op jit(solution)/shard_map/all_to_all | solution.py:36
  45.2 6.7 %collective-permute-start.3 = (bf16[4,512,128]{2,1,0:T(8,128)(2,1)S(1)}, bf16[4,512,128]{2,1,0:T(8,128)(2,1)S(1)}, u32[]{:S(2)}, u32[]{:S(2)}) collective-permute-start(bf16[4,512,128]{2,1,0:T(8,128)(2,1)S(1)} %bitcast.142), channel_id=1, source_target_pairs={{0,1},{1,0},{2,3},{3,2},{4,5},{5,4},{6,7},{7,6},{8,9},{9,8},{10,11... | collective-permute-start | bytes 1572872 | tf_op jit(solution)/shard_map/ppermute | solution.py:76
  54.3 19.1 %all-to-all-start.2 = ((bf16[4,4,128,256]{3,2,1,0:T(8,128)(2,1)}), bf16[4,4,128,256]{3,2,1,0:T(8,128)(2,1)S(1)}, u32[]{:S(2)}, u32[]{:S(2)}) async-start(bf16[4,4,128,256]{3,2,1,0:T(8,128)(2,1)} %broadcast_in_dim.15), calls=%async_computation.2 | async-start | bytes 2097152 | tf_op jit(solution)/shard_map/all_to_all | solution.py:36
  73.4 38.7 %collective-permute-start.4 = (bf16[4,4,128,256]{3,2,0,1:T(8,128)(2,1)S(1)}, bf16[4,4,128,256]{3,2,0,1:T(8,128)(2,1)S(1)}, u32[]{:S(2)}, u32[]{:S(2)}) collective-permute-start(bf16[4,4,128,256]{3,2,0,1:T(8,128)(2,1)S(1)} %copy.75), channel_id=1, source_target_pairs={{0,1},{1,0},{2,3},{3,2},{4,5},{5,4},{6,7},{7,6},{8,9},{9,8},{10,11... | collective-permute-start | bytes 3145736 | tf_op jit(solution)/shard_map/ppermute | solution.py:92
  115.9 25.2 %copy-start.2 = (f32[4]{0:T(128)S(1)}, f32[4]{0:T(128)}, u32[]{:S(2)}) copy-start(f32[4]{0:T(128)} %param.11) | copy-start | bytes 52
  135.5 18.3 %all-to-all-start.4 = ((bf16[16,4,8,256]{3,2,1,0:T(8,128)(2,1)}), bf16[16,4,8,256]{3,2,1,0:T(8,128)(2,1)S(1)}, u32[]{:S(2)}, u32[]{:S(2)}) async-start(bf16[16,4,8,256]{3,2,1,0:T(8,128)(2,1)} %copy.63), calls=%async_computation.4 | async-start | bytes 524288 | tf_op jit(solution)/shard_map/all_to_all | solution.py:36
  163.9 29.7 %all-to-all-start.6 = ((f32[32,8,128]{2,1,0:T(8,128)}), f32[32,8,128]{2,1,0:T(8,128)S(1)}, u32[]{:S(2)}, u32[]{:S(2)}) async-start(f32[32,8,128]{2,1,0:T(8,128)} %broadcast_in_dim.17), calls=%async_computation.6 | async-start | bytes 262144 | tf_op jit(solution)/shard_map/all_to_all | solution.py:36

commit v2 on v1

v2 whole, which is shorter than its diff:
```python
import functools
import math

import jax
import jax.numpy as jnp
import numpy as np
from jax import lax
from jax.experimental import pallas as pl
from jax.experimental.pallas import tpu as pltpu
from jax.sharding import Mesh, PartitionSpec as P

SURF = ("x", "y", "zl")
FIELD = ("zh", "c")
DEPTH = ("zh", "zl")
LEVEL = ("x", "y", "c")
SWAP = [(0, 1), (1, 0)]
LANES = 128
STRIP = 32
THIRDS = 16
BF16 = jnp.bfloat16
F32 = jnp.float32


def fitted(function, count):
    top = 0.0625
    nodes = 0.5 * top * (1.0 - np.cos(np.pi * (np.arange(count) + 0.5) / count))
    powers = np.vander(nodes, count, increasing=True)
    return [float(value) for value in np.linalg.solve(powers, function(np.sqrt(nodes)))]


SINE = fitted(lambda b: np.sin(2.0 * np.pi * b) / b, 5)
COSINE = fitted(lambda b: np.cos(2.0 * np.pi * b), 5)


def polynomial(coefficients, u):
    total = u * coefficients[-1] + coefficients[-2]
    for value in coefficients[-3::-1]:
        total = total * u + value
    return total


def tile_kernel(place, wave, own, first, second, third, mine, other, out, px, py, pz):
    lines = out.shape[1]
    depth = 4

    @pl.when((pl.program_id(0) == 0) & (pl.program_id(1) == 0))
    def _():
        for back, block in enumerate((own, first, second, third)):
            slot = lax.rem(place[0] + depth - back, depth)
            for coordinate, target in enumerate((px, py, pz)):
                row = block[coordinate : coordinate + 1, :]
                if coordinate == 2:
                    row = row * row
                column = jnp.broadcast_to(row, (LANES, LANES)).T
                for part in range(4):
                    start = pl.multiple_of(part * LANES + slot * STRIP, STRIP)
                    target[pl.ds(start, STRIP), :] = column[part * STRIP : (part + 1) * STRIP, :]

    thirds = jnp.where(pl.program_id(0) == 0, mine[0].astype(F32), other[0].astype(F32))
    across = thirds[0:1] + thirds[1:2] + thirds[2:3]
    along = thirds[3:4] + thirds[4:5] + thirds[5:6]
    area = thirds[6:7] + thirds[7:8] + thirds[8:9]
    turns = [wave[line] * (0.5 / math.pi) for line in range(lines)]

    def strip(index, carry):
        rows = pl.ds(pl.multiple_of(index * STRIP, STRIP), STRIP)
        dx = px[rows, :] - across
        dy = py[rows, :] - along
        distance = jnp.sqrt(dx * dx + dy * dy + pz[rows, :])
        gain = area / distance
        opposite = -gain
        for line in range(lines):
            turn = distance * turns[line]
            turn = turn - jnp.round(turn)
            b = 0.25 - jnp.abs(turn)
            u = b * b
            cosine = polynomial(SINE, u) * b
            sine = polynomial(COSINE, u)
            signed = jnp.where(turn < 0.0, opposite, gain)
            out[0, line, rows, 0:LANES] = (signed * sine).astype(BF16)
            out[0, line, rows, LANES : 2 * LANES] = (gain * cosine).astype(BF16)
        return carry

    lax.fori_loop(0, out.shape[2] // STRIP, strip, 0)


def make_tiles(place, wave, blocks, mine, other, interpret=False):
    lines = wave.shape[0]
    sources = 4
    points = 4 * LANES
    last = mine.shape[1] // THIRDS - 1
    whole = pl.BlockSpec((3, LANES), lambda h, i, place, wave: (0, 0))
    panel = pl.BlockSpec(
        (1, THIRDS, LANES), lambda h, i, place, wave: (i * sources + place[2], last, 0)
    )
    return pl.pallas_call(
        tile_kernel,
        out_shape=jax.ShapeDtypeStruct((2 * sources, lines, points, 2 * LANES), BF16),
        grid_spec=pltpu.PrefetchScalarGridSpec(
            num_scalar_prefetch=2,
            grid=(2, sources),
            in_specs=[whole] * 4 + [panel] * 2,
            out_specs=pl.BlockSpec(
                (1, lines, points, 2 * LANES),
                lambda h, i, place, wave: (h * sources + i, 0, 0, 0),
            ),
            scratch_shapes=[pltpu.VMEM((points, LANES), F32)] * 3,
        ),
        cost_estimate=pl.CostEstimate(
            flops=8_000_000_000, bytes_accessed=8 << 20, transcendentals=0
        ),
        interpret=interpret,
        name="tiles",
    )(place, wave, *blocks, mine, other)


def velocity_kernel(place, mine, other, response, out, energy):
    a = mine[...].reshape(-1, LANES)
    b = other[...].reshape(-1, LANES)
    first = place[1] == 0
    real = jnp.where(first, a, b)
    imag = jnp.where(first, b, a)
    upper = jnp.concatenate([real, imag], axis=1)
    lower = jnp.concatenate([-imag, real], axis=1)
    total = jnp.dot(response[0, 0], upper, preferred_element_type=F32)
    total = total + jnp.dot(response[0, 1], lower, preferred_element_type=F32)
    rounded = total.astype(BF16)
    for copy in range(out.shape[0]):
        out[copy, 0] = rounded
    wide = rounded.astype(F32)
    squares = jnp.sum(wide * wide, axis=0, keepdims=True)
    energy[0] = squares[:, :LANES] + squares[:, LANES:]


def make_velocity(place, mine, other, response, copies, interpret=False):
    groups, _, cases = mine.shape
    lines, _, own, channels = response.shape
    force_spec = pl.BlockSpec((groups, channels // groups, cases), lambda l, place: (0, l, 0))
    return pl.pallas_call(
        velocity_kernel,
        out_shape=(
            jax.ShapeDtypeStruct((copies, lines, own, 2 * cases), BF16),
            jax.ShapeDtypeStruct((lines, 1, cases), F32),
        ),
        grid_spec=pltpu.PrefetchScalarGridSpec(
            num_scalar_prefetch=1,
            grid=(lines,),
            in_specs=[
                force_spec,
                force_spec,
                pl.BlockSpec((1, 2, own, channels), lambda l, place: (l, 0, 0, 0)),
            ],
            out_specs=(
                pl.BlockSpec((copies, 1, own, 2 * cases), lambda l, place: (0, l, 0, 0)),
                pl.BlockSpec((1, 1, cases), lambda l, place: (l, 0, 0)),
            ),
        ),
        cost_estimate=pl.CostEstimate(
            flops=2 * lines * own * 4 * channels * cases, bytes_accessed=3 << 20, transcendentals=0
        ),
        interpret=interpret,
        name="velocity",
    )(place, mine, other, response)


def pressure_kernel(tiles, near, far, out):
    sources = near.shape[0]
    total = None
    for half, block in enumerate((near, far)):
        for source in range(sources):
            upper = block[source, 0]
            lower = jnp.concatenate([-upper[:, LANES:], upper[:, :LANES]], axis=1)
            stacked = jnp.concatenate([upper, lower], axis=0)
            term = jnp.dot(tiles[half * sources + source, 0], stacked, preferred_element_type=F32)
            total = term if total is None else total + term
    out[:, 0] = total.astype(BF16).reshape(out.shape[0], out.shape[2], out.shape[3])


def make_partial(tiles, near, far, parts, interpret=False):
    chunks, lines, points, depth = tiles.shape
    sources, _, own, columns = near.shape
    spec = pl.BlockSpec((sources, 1, own, columns), lambda l: (0, l, 0, 0))
    return pl.pallas_call(
        pressure_kernel,
        out_shape=jax.ShapeDtypeStruct((parts, lines, points // parts, columns), BF16),
        grid=(lines,),
        in_specs=[pl.BlockSpec((chunks, 1, points, depth), lambda l: (0, l, 0, 0)), spec, spec],
        out_specs=pl.BlockSpec((parts, 1, points // parts, columns), lambda l: (0, l, 0, 0)),
        cost_estimate=pl.CostEstimate(
            flops=2 * lines * chunks * points * depth * columns,
            bytes_accessed=11 << 20,
            transcendentals=0,
        ),
        interpret=interpret,
        name="partial",
    )(tiles, near, far)


def level_kernel(rows, beside, out):
    lines = beside.shape[1]
    levels = []
    for line in range(lines):
        total = beside[0, line].astype(F32)
        for source in range(1, beside.shape[0]):
            total = total + beside[source, line].astype(F32)
        levels.append(total.reshape(-1, rows, total.shape[1]))
    out[...] = jnp.concatenate(levels, axis=1).astype(BF16)


def make_level(beside, rows, interpret=False):
    _, lines, share, columns = beside.shape
    return pl.pallas_call(
        functools.partial(level_kernel, rows),
        out_shape=jax.ShapeDtypeStruct((share // rows, lines * rows, columns), BF16),
        interpret=interpret,
        name="level",
    )(beside)


def finish_kernel(wave, column, energy, pressure, sums):
    lines = energy.shape[0]
    total = column[0].astype(F32)
    for source in range(1, column.shape[0]):
        total = total + column[source].astype(F32)
    rows = total.shape[0] // lines
    parts = [
        total[line * rows : (line + 1) * rows] * (wave[line] * (0.5 / math.pi))
        for line in range(lines)
    ]
    rounded = jnp.concatenate(parts, axis=0).astype(BF16)
    pressure[...] = rounded
    wide = rounded.astype(F32)
    wide = wide * wide
    both = wide[:, :LANES] + wide[:, LANES:]
    power = [
        jnp.sum(both[line * rows : (line + 1) * rows], axis=0, keepdims=True)
        for line in range(lines)
    ]
    table = jnp.concatenate([energy[line] for line in range(lines)] + power, axis=0)
    for copy in range(sums.shape[0]):
        sums[copy] = table


def make_finish(wave, column, energy, copies, interpret=False):
    lines, _, cases = energy.shape
    _, rows, columns = column.shape
    return pl.pallas_call(
        finish_kernel,
        out_shape=(
            jax.ShapeDtypeStruct((rows, columns), BF16),
            jax.ShapeDtypeStruct((copies, 2 * lines, cases), F32),
        ),
        in_specs=[
            pl.BlockSpec(memory_space=pltpu.SMEM),
            pl.BlockSpec(memory_space=pltpu.VMEM),
            pl.BlockSpec(memory_space=pltpu.VMEM),
        ],
        interpret=interpret,
        name="finish",
    )(wave, column, energy)


def fold_kernel(table, out):
    total = table[0]
    for source in range(1, table.shape[0]):
        total = total + table[source]
    for copy in range(out.shape[0]):
        out[copy] = total


def make_fold(table, copies, interpret=False):
    return pl.pallas_call(
        fold_kernel,
        out_shape=jax.ShapeDtypeStruct((copies,) + table.shape[1:], F32),
        interpret=interpret,
        name="fold",
    )(table)


def ratio_kernel(point_total, panel_total, table, out):
    lines = out.shape[0]
    total = table[0]
    for source in range(1, table.shape[0]):
        total = total + table[source]
    out[...] = total[lines:] / point_total / (total[:lines] / panel_total + 1e-06)


def make_ratio(table, point_total, panel_total, interpret=False):
    _, double, cases = table.shape
    return pl.pallas_call(
        functools.partial(ratio_kernel, point_total, panel_total),
        out_shape=jax.ShapeDtypeStruct((double // 2, cases), F32),
        interpret=interpret,
        name="ratio",
    )(table)


def exchange(array, axes):
    return lax.all_to_all(array, axes, 0, 0, tiled=True)


def gather(array, axes):
    size = lax.axis_size(axes)
    return exchange(jnp.broadcast_to(array[None], (size,) + array.shape), axes)


def shards(forces, response, panel_plane, panel_area, field_points, wavenumber):
    lines, _, channels, cases = forces.shape
    own = response.shape[2]
    rows = field_points.shape[1] // lax.axis_size(SURF)
    share = rows * lax.axis_size("y") * lax.axis_size("zl")
    place = jnp.stack([lax.axis_index(axis) for axis in ("zh", "c", "y")]).astype(jnp.int32)
    turn = lax.axis_size("zh")

    first = (lax.axis_index("zh") * 2 + lax.axis_index("c")) * own
    panels = lax.dynamic_slice_in_dim(panel_plane, first, own, 1)
    area = lax.dynamic_slice_in_dim(panel_area, first, own, 0)
    panels = jnp.concatenate([panels, area[None]], axis=0)
    high = lax.reduce_precision(panels, 8, 7)
    middle = lax.reduce_precision(panels - high, 8, 7)
    low = panels - high - middle
    thirds = jnp.stack([high, middle, low], axis=1).reshape(-1, own)
    thirds = jnp.pad(thirds, ((0, THIRDS - thirds.shape[0]), (0, 0))).astype(BF16)
    block = lax.dynamic_slice_in_dim(field_points, lax.axis_index("x") * share, share, 1)

    part = jnp.where(lax.axis_index("c") == 0, forces[:, 0], forces[:, 1])
    part = gather(part, "zl")
    part, block = lax.optimization_barrier((part, block))
    part = jnp.concatenate([part.transpose(1, 0, 2, 3).reshape(-1, cases), thirds], axis=0)
    mine = gather(part, ("x", "y"))
    blocks = [block] + [
        lax.ppermute(block, "zh", [(i, (i + step) % turn) for i in range(turn)])
        for step in range(1, turn)
    ]
    mine, blocks = lax.optimization_barrier((mine, blocks))
    other = lax.ppermute(mine, "c", SWAP)
    velocity, energy = make_velocity(place, mine, other, response, lax.axis_size("x"))
    velocity, tile_mine, tile_other = lax.optimization_barrier((velocity, mine, other))
    near = exchange(velocity, "x")
    tiles = make_tiles(place, wavenumber, blocks, tile_mine, tile_other)
    near, tiles = lax.optimization_barrier((near, tiles))
    far = lax.ppermute(near, "c", SWAP)
    partial = make_partial(tiles, near, far, lax.axis_size("y"))
    level = make_level(exchange(partial, "y"), rows)
    column = exchange(level, DEPTH)
    pressure, sums = make_finish(wavenumber, column, energy, lax.axis_size(LEVEL))
    sums = make_fold(exchange(sums, LEVEL), lax.axis_size(DEPTH))
    sums = exchange(sums, DEPTH)
    point_total = field_points.shape[1] * lax.axis_size(FIELD)
    panel_total = own * lax.axis_size(SURF + FIELD)
    efficiency = make_ratio(sums, point_total, panel_total)
    pressure = pressure.reshape(lines, rows, 2, cases).transpose(1, 0, 2, 3)
    return (pressure, efficiency)


def solution(mesh):
    grid = Mesh(np.asarray(mesh.devices).reshape(4, 4, 4, 4, 2), SURF + FIELD)
    return jax.shard_map(
        shards,
        mesh=grid,
        in_specs=(
            P(None, None, SURF, None),
            P(None, None, SURF + FIELD, None),
            P(None, SURF),
            P(SURF),
            P(None, FIELD),
            P(),
        ),
        out_specs=(P(FIELD + SURF, None, None, None), P()),
        check_vma=False,
    )
```

time: 195 us -> 174 us (0.89)
  other arithmetic: 37.7 us -> 1.36 us
  Pallas kernels: 0 us -> 31.8 us
  blocking collectives: 27.9 us -> 58.4 us
  waiting for transfers between devices: 44.9 us -> 19.4 us
  starting transfers between devices: 71 us -> 54 us
  matrix products: 3.81 us -> 0 us
    another operation x3, other arithmetic: 35.4 us -> 0.63 us  [the longest x1 0.6 us: shards(): jnp.stack([lax.axis_index(axis) for axis in ('zh', 'c', 'y')])]
    pallas_call x0 -> x7, Pallas kernels: none -> 31.8 us  [the longest x1 13.7 us: make_tiles(): pl.pallas_call(tile_kernel, out_shape=jax.ShapeDtypeStruct((2 * sources,...]
    all_to_all x2 -> x3, blocking collectives: 27.9 us -> 58.4 us  [exchange(): return lax.all_to_all(array, axes, 0, 0, tiled=True)]
    all_to_all x5 -> x4, waiting for transfers between devices: 42.1 us -> 14.1 us  [exchange(): return lax.all_to_all(array, axes, 0, 0, tiled=True)]
    all_to_all x5 -> x4, starting transfers between devices: 40.3 us -> 22.6 us  [exchange(): return lax.all_to_all(array, axes, 0, 0, tiled=True)]
    dot_general x8 -> x0, matrix products: 3.81 us -> none  [the longest x4 2.88 us: shards(): summed = jnp.dot(tiles, stacked, preferred_element_type=jnp.float32)]
    ppermute x5, waiting for transfers between devices: 2.88 us -> 5.33 us  [the longest x1 2.26 us: shards(): far = lax.ppermute(near, 'c', SWAP)]
  transfers between devices with their start and end apart: 10 -> 9, of which waited for: 5 -> 7; matrix products, arithmetic and copies ran while one was open for 20% -> 2% of each run, Pallas kernels for 0% -> 8%
where the time goes in v2:
time: 174 us; the launch traced here: 173 us
  blocking collectives  58.4 us (34%)
  starting transfers between devices  54 us (31%)
  Pallas kernels  31.8 us (18%)
  waiting for transfers between devices  19.4 us (11%)
  local copies, waits for them, and re-layouts  6.82 us (4%)
    all_to_all x3, blocking collectives, exchange(): return lax.all_to_all(array, axes, 0, 0, tiled=True)  58.4 us
    all_to_all x4, starting transfers between devices, exchange(): return lax.all_to_all(array, axes, 0, 0, tiled=True)  22.6 us
    ppermute x3, starting transfers between devices, shards(): lax.ppermute(block, 'zh', [(i, (i + step) % turn) for i in range(turn)])  22.3 us
    all_to_all x4, waiting for transfers between devices, exchange(): return lax.all_to_all(array, axes, 0, 0, tiled=True)  14.1 us
    pallas_call x1, Pallas kernels, make_tiles(): pl.pallas_call(tile_kernel, out_shape=jax.ShapeDtypeStruct((2 * sources,...  13.7 us
    pallas_call x1, Pallas kernels, make_partial(): pl.pallas_call(pressure_kernel, out_shape=jax.ShapeDtypeStruct((parts, li...  6.62 us
    ppermute x1, starting transfers between devices, shards(): other = lax.ppermute(mine, 'c', SWAP)  5.7 us
    pallas_call x1, Pallas kernels, make_velocity(): pl.pallas_call(velocity_kernel, out_shape=(jax.ShapeDtypeStruct((copies,...  4.8 us
  transfers between devices with their start and end apart: 9, of which 7 were waited for; matrix products, arithmetic and copies ran while one was open for 2% of the time, Pallas kernels for 8%

profile of v2, /device:TPU:1, one launch (start us, length us, event | category | flops | bytes accessed | tf_op | source)
XLA Modules:
  0.0 172.6 jit_solution(2610138619059928763)
XLA Ops:
  0.7 0.7 select_bitcast_fusion
  2.0 6.4 %all-to-all-start = ((bf16[4,4,8,128]{3,2,1,0:T(8,128)(2,1)}), bf16[4,4,8,128]{3,2,1,0:T(8,128)(2,1)S(1)}, u32[]{:S(2)}, u32[]{:S(2)}) async-start(bf16[4,4,8,128]{3,2,1,0:T(8,128)(2,1)} %broadcast_in_dim.4), calls=%async_computation | async-start | bytes 65536 | tf_op jit(solution)/shard_map/all_to_all | solution.py:299
  8.4 0.8 dynamic-slice_bitcast_fusion
  9.9 3.0 %all-to-all-done = bf16[4,4,8,128]{3,2,1,0:T(8,128)(2,1)S(1)} async-done(((bf16[4,4,8,128]{3,2,1,0:T(8,128)(2,1)}), bf16[4,4,8,128]{3,2,1,0:T(8,128)(2,1)S(1)}, u32[]{:S(2)}, u32[]{:S(2)}) %all-to-all-start) | async-done | bytes 32800 | tf_op jit(solution)/shard_map/all_to_all | solution.py:299
  12.9 0.9 broadcast_in_dim.5
  13.9 6.8 %all-to-all-start.1 = ((bf16[16,144,128]{2,1,0:T(8,128)(2,1)}), bf16[16,144,128]{2,1,0:T(8,128)(2,1)S(1)}, u32[]{:S(2)}, u32[]{:S(2)}) async-start(bf16[16,144,128]{2,1,0:T(8,128)(2,1)} %broadcast_in_dim.5), calls=%async_computation.1 | async-start | bytes 1179648 | tf_op jit(solution)/shard_map/all_to_all | solution.py:299
  20.6 10.1 %collective-permute-start.2 = (f32[3,128]{1,0:T(4,128)S(1)}, f32[3,128]{1,0:T(4,128)S(1)}, u32[]{:S(2)}, u32[]{:S(2)}) collective-permute-start(f32[3,128]{1,0:T(4,128)S(1)} %constant_dynamic-slice_fusion.1.own), channel_id=1, source_target_pairs={{0,6},{2,0},{4,2},{6,4},{1,7},{3,1},{5,3},{7,5},{8,14},{10,8},{12,... | collective-permute-start | bytes 4616 | tf_op jit(solution)/shard_map/ppermute | solution.py:332
  30.7 5.7 %collective-permute-start.1 = (f32[3,128]{1,0:T(4,128)S(1)}, f32[3,128]{1,0:T(4,128)S(1)}, u32[]{:S(2)}, u32[]{:S(2)}) collective-permute-start(f32[3,128]{1,0:T(4,128)S(1)} %constant_dynamic-slice_fusion.1.own), channel_id=1, source_target_pairs={{0,4},{2,6},{4,0},{6,2},{1,5},{3,7},{5,1},{7,3},{8,12},{10,14},{12... | collective-permute-start | bytes 4616 | tf_op jit(solution)/shard_map/ppermute | solution.py:332
  36.4 6.4 %collective-permute-start = (f32[3,128]{1,0:T(4,128)S(1)}, f32[3,128]{1,0:T(4,128)S(1)}, u32[]{:S(2)}, u32[]{:S(2)}) collective-permute-start(f32[3,128]{1,0:T(4,128)S(1)} %constant_dynamic-slice_fusion.1.own), channel_id=1, source_target_pairs={{0,2},{2,4},{4,6},{6,0},{1,3},{3,5},{5,7},{7,1},{8,10},{10,12},{12... | collective-permute-start | bytes 4616 | tf_op jit(solution)/shard_map/ppermute | solution.py:332
  42.9 0.8 collective-permute-done.1.second
  43.7 1.2 collective-permute-done.first
  45.0 5.7 %collective-permute-start.3 = (bf16[16,144,128]{2,1,0:T(8,128)(2,1)S(1)}, bf16[16,144,128]{2,1,0:T(8,128)(2,1)S(1)}, u32[]{:S(2)}, u32[]{:S(2)}) collective-permute-start(bf16[16,144,128]{2,1,0:T(8,128)(2,1)S(1)} %all-to-all-done.1.mine), channel_id=1, source_target_pairs={{0,1},{1,0},{2,3},{3,2},{4,5},{5,4},{6,7},{7,6},{8,9},{9,8},{10,11... | collective-permute-start | bytes 1769480 | tf_op jit(solution)/shard_map/ppermute | solution.py:336
  51.3 1.0 collective-permute-done.3.other
  52.3 0.8 copy-done.4
  53.2 4.8 %velocity.1 = (bf16[4,4,128,256]{3,2,1,0:T(8,128)(2,1)}, f32[4,1,128]{2,1,0:T(1,128)}) custom-call(s32[3]{0:T(128)} %pad_add_fusion.place, bf16[16,144,128]{2,1,0:T(8,128)(2,1)} %copy-done.2, bf16[16,144,128]{2,1,0:T(8,128)(2,1)} %copy-done.4, bf16[4,2,128,512]{3,2,1,0:T(8,128)(2,1)} %response.1), custom_call_target="tpu_custom_call" | custom-call | flops 268435456 | bytes 3145728 | tf_op jit(solution)/shard_map/velocity/pallas_call | solution.py:139
  58.0 4.4 %all-to-all-start.2 = ((bf16[4,4,128,256]{3,2,1,0:T(8,128)(2,1)}), bf16[4,4,128,256]{3,2,1,0:T(8,128)(2,1)S(1)}, u32[]{:S(2)}, u32[]{:S(2)}) async-start(bf16[4,4,128,256]{3,2,1,0:T(8,128)(2,1)} %get-tuple-element.22), calls=%async_computation.2 | async-start | bytes 2097152 | tf_op jit(solution)/shard_map/all_to_all | solution.py:299
  62.4 13.7 %tiles.1 = bf16[8,4,512,256]{3,2,1,0:T(8,128)(2,1)} custom-call(s32[3]{0:T(128)} %pad_add_fusion.place, f32[4]{0:T(128)} %wave.3, f32[3,128]{1,0:T(4,128)} %copy-done.6, f32[3,128]{1,0:T(4,128)} %copy-done.9, f32[3,128]{1,0:T(4,128)} %copy-done.8, f32[3,128]{1,0:T(4,128)} %copy-done.7, bf16[16,144,128]{2,1,0:T(8,128)(2,1)} %copy-done.2, ...), custom_call_target="tpu_custom_call" | custom-call | flops 8000000000 | bytes 8388608 | tf_op jit(solution)/shard_map/tiles/pallas_call | solution.py:96
  76.1 0.9 all-to-all-done.2.near
  76.9 3.4 %collective-permute-start.4 = (bf16[4,4,128,256]{3,2,1,0:T(8,128)(2,1)S(1)}, bf16[4,4,128,256]{3,2,1,0:T(8,128)(2,1)S(1)}, u32[]{:S(2)}, u32[]{:S(2)}) collective-permute-start(bf16[4,4,128,256]{3,2,1,0:T(8,128)(2,1)S(1)} %all-to-all-done.2.near), channel_id=1, source_target_pairs={{0,1},{1,0},{2,3},{3,2},{4,5},{5,4},{6,7},{7,6},{8,9},{9,8},{10,11... | collective-permute-start | bytes 3145736 | tf_op jit(solution)/shard_map/ppermute | solution.py:342
  80.3 2.3 %collective-permute-done.4.far = bf16[4,4,128,256]{3,2,1,0:T(8,128)(2,1)S(1)} collective-permute-done((bf16[4,4,128,256]{3,2,1,0:T(8,128)(2,1)S(1)}, bf16[4,4,128,256]{3,2,1,0:T(8,128)(2,1)S(1)}, u32[]{:S(2)}, u32[]{:S(2)}) %collective-permute-start.4) | collective-permute-done | bytes 1048608 | tf_op jit(solution)/shard_map/ppermute | solution.py:342
  82.6 1.0 copy-done.3
  83.6 6.6 %partial.1 = bf16[4,4,128,256]{3,2,1,0:T(8,128)(2,1)} custom-call(bf16[8,4,512,256]{3,2,1,0:T(8,128)(2,1)} %tiles.1, bf16[4,4,128,256]{3,2,1,0:T(8,128)(2,1)} %copy-done.1, bf16[4,4,128,256]{3,2,1,0:T(8,128)(2,1)} %copy-done.3), custom_call_target="tpu_custom_call" | custom-call | flops 2147483648 | bytes 11534336 | tf_op jit(solution)/shard_map/partial/pallas_call | solution.py:183
  90.2 19.1 %all_to_all.35.beside = bf16[4,4,128,256]{3,2,1,0:T(8,128)(2,1)} all-to-all(bf16[4,4,128,256]{3,2,1,0:T(8,128)(2,1)} %partial.1), channel_id=1, replica_groups=mesh['x'=4,'y'=4,'zl'=4,'zh'=4,'c'=2] {'y'}, dimensions={0} | all-to-all | bytes 2097152 | tf_op jit(solution)/shard_map/all_to_all | solution.py:299
  109.3 2.0 %level.1 = bf16[16,32,256]{2,1,0:T(8,128)(2,1)} custom-call(bf16[4,4,128,256]{3,2,1,0:T(8,128)(2,1)} %all_to_all.35.beside), custom_call_target="tpu_custom_call" | custom-call | tf_op jit(solution)/shard_map/level/pallas_call | solution.py:212
  111.3 20.3 %all_to_all.36.column = bf16[16,32,256]{2,1,0:T(8,128)(2,1)} all-to-all(bf16[16,32,256]{2,1,0:T(8,128)(2,1)} %level.1), channel_id=1, replica_groups=mesh['x'=4,'y'=4,'zl'=4,'zh'=4,'c'=2] {'zh','zl'}, dimensions={0} | all-to-all | bytes 524288 | tf_op jit(solution)/shard_map/all_to_all | solution.py:299
  131.6 1.7 finish.1
  133.3 19.0 %all_to_all.37.table = f32[32,8,128]{2,1,0:T(8,128)} all-to-all(f32[32,8,128]{2,1,0:T(8,128)} %get-tuple-element.33), channel_id=1, replica_groups=mesh['x'=4,'y'=4,'zl'=4,'zh'=4,'c'=2] {'x','y','c'}, dimensions={0} | all-to-all | bytes 262144 | tf_op jit(solution)/shard_map/all_to_all | solution.py:299
  152.3 1.6 fold.1
  153.9 5.0 %all-to-all-start.6 = ((f32[16,8,128]{2,1,0:T(8,128)}), f32[16,8,128]{2,1,0:T(8,128)S(1)}, u32[]{:S(2)}, u32[]{:S(2)}) async-start(f32[16,8,128]{2,1,0:T(8,128)} %fold.1), calls=%async_computation.6 | async-start | bytes 131072 | tf_op jit(solution)/shard_map/all_to_all | solution.py:299
  158.9 1.3 copy.25
  160.3 10.3 %all-to-all-done.6.table = f32[16,8,128]{2,1,0:T(8,128)S(1)} async-done(((f32[16,8,128]{2,1,0:T(8,128)}), f32[16,8,128]{2,1,0:T(8,128)S(1)}, u32[]{:S(2)}, u32[]{:S(2)}) %all-to-all-start.6) | async-done | bytes 65568 | tf_op jit(solution)/shard_map/all_to_all | solution.py:299
  171.1 1.4 ratio.1
  (29 shorter events, 2.6 us)
Async XLA Ops:
  0.6 9.3 %copy-start = (f32[3,512]{1,0:T(4,128)S(1)}, f32[3,512]{1,0:T(4,128)}, u32[]{:S(2)}) copy-start(f32[3,512]{1,0:T(4,128)} %param.10) | copy-start | bytes 18436
  2.0 10.9 %all-to-all-start = ((bf16[4,4,8,128]{3,2,1,0:T(8,128)(2,1)}), bf16[4,4,8,128]{3,2,1,0:T(8,128)(2,1)S(1)}, u32[]{:S(2)}, u32[]{:S(2)}) async-start(bf16[4,4,8,128]{3,2,1,0:T(8,128)(2,1)} %broadcast_in_dim.4), calls=%async_computation | async-start | bytes 65536 | tf_op jit(solution)/shard_map/all_to_all | solution.py:299
  9.9 52.4 %copy-start.6 = (f32[3,128]{1,0:T(4,128)}, f32[3,128]{1,0:T(4,128)S(1)}, u32[]{:S(2)}) copy-start(f32[3,128]{1,0:T(4,128)S(1)} %constant_dynamic-slice_fusion.1.own) | copy-start | bytes 4612
  13.9 31.1 %all-to-all-start.1 = ((bf16[16,144,128]{2,1,0:T(8,128)(2,1)}), bf16[16,144,128]{2,1,0:T(8,128)(2,1)S(1)}, u32[]{:S(2)}, u32[]{:S(2)}) async-start(bf16[16,144,128]{2,1,0:T(8,128)(2,1)} %broadcast_in_dim.5), calls=%async_computation.1 | async-start | bytes 1179648 | tf_op jit(solution)/shard_map/all_to_all | solution.py:299
  20.6 22.3 %collective-permute-start.2 = (f32[3,128]{1,0:T(4,128)S(1)}, f32[3,128]{1,0:T(4,128)S(1)}, u32[]{:S(2)}, u32[]{:S(2)}) collective-permute-start(f32[3,128]{1,0:T(4,128)S(1)} %constant_dynamic-slice_fusion.1.own), channel_id=1, source_target_pairs={{0,6},{2,0},{4,2},{6,4},{1,7},{3,1},{5,3},{7,5},{8,14},{10,8},{12,... | collective-permute-start | bytes 4616 | tf_op jit(solution)/shard_map/ppermute | solution.py:332
  30.7 13.0 %collective-permute-start.1 = (f32[3,128]{1,0:T(4,128)S(1)}, f32[3,128]{1,0:T(4,128)S(1)}, u32[]{:S(2)}, u32[]{:S(2)}) collective-permute-start(f32[3,128]{1,0:T(4,128)S(1)} %constant_dynamic-slice_fusion.1.own), channel_id=1, source_target_pairs={{0,4},{2,6},{4,0},{6,2},{1,5},{3,7},{5,1},{7,3},{8,12},{10,14},{12... | collective-permute-start | bytes 4616 | tf_op jit(solution)/shard_map/ppermute | solution.py:332
  36.4 8.5 %collective-permute-start = (f32[3,128]{1,0:T(4,128)S(1)}, f32[3,128]{1,0:T(4,128)S(1)}, u32[]{:S(2)}, u32[]{:S(2)}) collective-permute-start(f32[3,128]{1,0:T(4,128)S(1)} %constant_dynamic-slice_fusion.1.own), channel_id=1, source_target_pairs={{0,2},{2,4},{4,6},{6,0},{1,3},{3,5},{5,7},{7,1},{8,10},{10,12},{12... | collective-permute-start | bytes 4616 | tf_op jit(solution)/shard_map/ppermute | solution.py:332
  42.9 19.5 %copy-start.7 = (f32[3,128]{1,0:T(4,128)}, f32[3,128]{1,0:T(4,128)S(1)}, u32[]{:S(2)}) copy-start(f32[3,128]{1,0:T(4,128)S(1)} %collective-permute-done.2.third) | copy-start | bytes 4612
  43.7 18.6 %copy-start.8 = (f32[3,128]{1,0:T(4,128)}, f32[3,128]{1,0:T(4,128)S(1)}, u32[]{:S(2)}) copy-start(f32[3,128]{1,0:T(4,128)S(1)} %collective-permute-done.1.second) | copy-start | bytes 4612
  45.0 17.4 %copy-start.9 = (f32[3,128]{1,0:T(4,128)}, f32[3,128]{1,0:T(4,128)S(1)}, u32[]{:S(2)}) copy-start(f32[3,128]{1,0:T(4,128)S(1)} %collective-permute-done.first) | copy-start | bytes 4612
  45.0 7.3 %copy-start.2 = (bf16[16,144,128]{2,1,0:T(8,128)(2,1)}, bf16[16,144,128]{2,1,0:T(8,128)(2,1)S(1)}, u32[]{:S(2)}) copy-start(bf16[16,144,128]{2,1,0:T(8,128)(2,1)S(1)} %all-to-all-done.1.mine) | copy-start | bytes 1769476
  45.0 7.3 %collective-permute-start.3 = (bf16[16,144,128]{2,1,0:T(8,128)(2,1)S(1)}, bf16[16,144,128]{2,1,0:T(8,128)(2,1)S(1)}, u32[]{:S(2)}, u32[]{:S(2)}) collective-permute-start(bf16[16,144,128]{2,1,0:T(8,128)(2,1)S(1)} %all-to-all-done.1.mine), channel_id=1, source_target_pairs={{0,1},{1,0},{2,3},{3,2},{4,5},{5,4},{6,7},{7,6},{8,9},{9,8},{10,11... | collective-permute-start | bytes 1769480 | tf_op jit(solution)/shard_map/ppermute | solution.py:336
  52.3 0.8 copy-start.4
  58.0 19.0 %all-to-all-start.2 = ((bf16[4,4,128,256]{3,2,1,0:T(8,128)(2,1)}), bf16[4,4,128,256]{3,2,1,0:T(8,128)(2,1)S(1)}, u32[]{:S(2)}, u32[]{:S(2)}) async-start(bf16[4,4,128,256]{3,2,1,0:T(8,128)(2,1)} %get-tuple-element.22), calls=%async_computation.2 | async-start | bytes 2097152 | tf_op jit(solution)/shard_map/all_to_all | solution.py:299
  76.9 5.7 %copy-start.1 = (bf16[4,4,128,256]{3,2,1,0:T(8,128)(2,1)}, bf16[4,4,128,256]{3,2,1,0:T(8,128)(2,1)S(1)}, u32[]{:S(2)}) copy-start(bf16[4,4,128,256]{3,2,1,0:T(8,128)(2,1)S(1)} %all-to-all-done.2.near) | copy-start | bytes 3145732
  76.9 5.7 %collective-permute-start.4 = (bf16[4,4,128,256]{3,2,1,0:T(8,128)(2,1)S(1)}, bf16[4,4,128,256]{3,2,1,0:T(8,128)(2,1)S(1)}, u32[]{:S(2)}, u32[]{:S(2)}) collective-permute-start(bf16[4,4,128,256]{3,2,1,0:T(8,128)(2,1)S(1)} %all-to-all-done.2.near), channel_id=1, source_target_pairs={{0,1},{1,0},{2,3},{3,2},{4,5},{5,4},{6,7},{7,6},{8,9},{9,8},{10,11... | collective-permute-start | bytes 3145736 | tf_op jit(solution)/shard_map/ppermute | solution.py:342
  82.6 1.0 copy-start.3
  153.9 16.6 %all-to-all-start.6 = ((f32[16,8,128]{2,1,0:T(8,128)}), f32[16,8,128]{2,1,0:T(8,128)S(1)}, u32[]{:S(2)}, u32[]{:S(2)}) async-start(f32[16,8,128]{2,1,0:T(8,128)} %fold.1), calls=%async_computation.6 | async-start | bytes 131072 | tf_op jit(solution)/shard_map/all_to_all | solution.py:299
  170.5 0.6 copy-start.5

commit v3 on v1

v3 whole, which is shorter than its diff:
```python
import functools
import math

import jax
import jax.numpy as jnp
import numpy as np
from jax import lax
from jax.experimental import pallas as pl
from jax.experimental.pallas import tpu as pltpu
from jax.sharding import Mesh, PartitionSpec as P

SURF = ("x", "y", "zl")
FIELD = ("zh", "c")
DEPTH = ("zh", "zl")
LEVEL = ("x", "y", "c")
SWAP = [(0, 1), (1, 0)]
LANES = 128
STRIP = 32
GROUP = 16
BF16 = jnp.bfloat16
F32 = jnp.float32
INTERPRET = False


def fitted(function, count):
    top = 0.0625
    nodes = 0.5 * top * (1.0 - np.cos(np.pi * (np.arange(count) + 0.5) / count))
    powers = np.vander(nodes, count, increasing=True)
    return [float(value) for value in np.linalg.solve(powers, function(np.sqrt(nodes)))]


SINE = fitted(lambda b: np.sin(2.0 * np.pi * b) / b, 5)
COSINE = fitted(lambda b: np.cos(2.0 * np.pi * b), 5)


def polynomial(coefficients, u):
    total = u * coefficients[-1] + coefficients[-2]
    for value in coefficients[-3::-1]:
        total = total * u + value
    return total


def call(kernel, out, scalars, arrays, name, scratch=(), cost=None, pinned=9):
    single = not isinstance(out, (list, tuple))
    shapes = (out,) if single else tuple(out)
    if INTERPRET:
        results = tuple(jax.ShapeDtypeStruct(s.shape, s.dtype) for s in shapes)
    else:
        results = tuple(pltpu.VMEM(s.shape, s.dtype) for s in shapes)
        arrays = [
            pltpu.with_memory_space_constraint(array, pltpu.VMEM) if index < pinned else array
            for index, array in enumerate(arrays)
        ]
    outs = pl.pallas_call(
        kernel,
        out_shape=results,
        in_specs=[pl.BlockSpec(memory_space=pltpu.SMEM)] * len(scalars)
        + [
            pl.BlockSpec(memory_space=pltpu.VMEM) if index < pinned else pl.BlockSpec()
            for index in range(len(arrays))
        ],
        out_specs=tuple(pl.BlockSpec(memory_space=pltpu.VMEM) for _ in shapes),
        scratch_shapes=list(scratch),
        cost_estimate=cost,
        interpret=INTERPRET,
        name=name,
    )(*scalars, *arrays)
    return outs[0] if single else outs


def cost(flops, moved):
    return pl.CostEstimate(flops=flops, bytes_accessed=moved, transcendentals=0)


def thirds_of(row):
    high = row.astype(BF16).astype(F32)
    middle = (row - high).astype(BF16).astype(F32)
    return [high, middle, row - high - middle]


def start_kernel(place, forces, panel_plane, panel_area, field_points, out, panel_rows):
    zh, core, x, zl = (place(axis) for axis in ("zh", "c", "x", "zl"))
    lane = pl.multiple_of(x * LANES, LANES)
    row = field_points[2:3, pl.ds(lane, LANES)]
    for coordinate in (0, 1):
        other = field_points[coordinate : coordinate + 1, pl.ds(lane, LANES)]
        row = jnp.where(zl == coordinate, other, row)
    point = jnp.concatenate(thirds_of(row) + [jnp.zeros((5, LANES), F32)], axis=0)
    force = forces[zh, core].astype(F32)
    chunk = jnp.concatenate([force, point], axis=0).astype(BF16)
    for copy in range(out.shape[0]):
        out[copy] = chunk
    field = zh * 2 + core
    lane = pl.multiple_of(field * LANES, LANES)
    rows = thirds_of(panel_plane[0:1, pl.ds(lane, LANES)])
    rows += thirds_of(panel_plane[1:2, pl.ds(lane, LANES)])
    rows += thirds_of(panel_area[pl.ds(field, 1), :])
    rows = jnp.concatenate(rows + [jnp.zeros((GROUP - 9, LANES), F32)], axis=0)
    panel_rows[...] = rows.astype(BF16)


def make_start(place, forces, panel_plane, panel_area, field_points, copies):
    out = (
        jax.ShapeDtypeStruct((copies, GROUP, LANES), BF16),
        jax.ShapeDtypeStruct((GROUP, LANES), BF16),
    )
    arrays = [forces, panel_plane, panel_area, field_points]
    return call(functools.partial(start_kernel, place), out, [], arrays, "start", pinned=0)


def spread_kernel(column, panel_rows, out):
    rows = column[:, 0:8, :].astype(F32).reshape(-1, LANES).astype(BF16)
    rows = jnp.concatenate([rows, panel_rows[...]], axis=0)
    for copy in range(out.shape[0]):
        out[copy] = rows


def make_spread(column, panel_rows, copies):
    rows = column.shape[0] * 8 + GROUP
    out = jax.ShapeDtypeStruct((copies, rows, LANES), BF16)
    return call(spread_kernel, out, [], [column, panel_rows], "spread")


def velocity_kernel(place, mine, other, response, out, energy):
    first = place("c") == 0
    lines = response.shape[0]
    depth = response.shape[3] // mine.shape[0]
    for line in range(lines):
        rows = slice(line * depth, (line + 1) * depth)
        a = mine[:, rows, :].reshape(-1, LANES)
        b = other[:, rows, :].reshape(-1, LANES)
        real = jnp.where(first, a, b)
        imag = jnp.where(first, b, a)
        upper = jnp.concatenate([real, imag], axis=1)
        lower = jnp.concatenate([-imag, real], axis=1)
        total = jnp.dot(response[line, 0], upper, preferred_element_type=F32)
        total = total + jnp.dot(response[line, 1], lower, preferred_element_type=F32)
        rounded = total.astype(BF16)
        for copy in range(out.shape[0]):
            out[copy, line] = rounded
        wide = rounded.astype(F32)
        squares = jnp.sum(wide * wide, axis=0, keepdims=True)
        energy[line : line + 1, :] = squares[:, :LANES] + squares[:, LANES:]


def make_velocity(place, mine, other, response, copies):
    lines, _, own, channels = response.shape
    out = (
        jax.ShapeDtypeStruct((copies, lines, own, 2 * LANES), BF16),
        jax.ShapeDtypeStruct((lines, LANES), F32),
    )
    work = cost(8 * lines * own * channels * LANES, 3 << 20)
    return call(
        functools.partial(velocity_kernel, place),
        out,
        [],
        [mine, other, response],
        "velocity",
        cost=work,
        pinned=2,
    )


def tile_kernel(place, wave, column, mine, other, out, token, px, py, pz):
    lines = out.shape[1]
    sources = 4
    last = mine.shape[1] - GROUP
    half, source = pl.program_id(0), pl.program_id(1)

    @pl.when((half == 0) & (source == 0))
    def _():
        for slot in range(4):
            for coordinate, target in enumerate((px, py, pz)):
                part = column[slot * 4 + coordinate].astype(F32)
                row = part[8:9] + part[9:10] + part[10:11]
                if coordinate == 2:
                    row = row * row
                block = jnp.broadcast_to(row, (LANES, LANES)).T
                for piece in range(4):
                    start = piece * LANES + slot * STRIP
                    target[start : start + STRIP, :] = block[piece * STRIP : (piece + 1) * STRIP, :]
        token[...] = px[0:8, :]

    at = source * sources + place("y")
    thirds = jnp.where(
        half == 0,
        mine[at, last : last + GROUP, :].astype(F32),
        other[at, last : last + GROUP, :].astype(F32),
    )
    across = thirds[0:1] + thirds[1:2] + thirds[2:3]
    along = thirds[3:4] + thirds[4:5] + thirds[5:6]
    area = thirds[6:7] + thirds[7:8] + thirds[8:9]
    turns = [wave[line] * (0.5 / math.pi) for line in range(lines)]

    def strip(index, carry):
        rows = pl.ds(pl.multiple_of(index * STRIP, STRIP), STRIP)
        dx = px[rows, :] - across
        dy = py[rows, :] - along
        distance = jnp.sqrt(dx * dx + dy * dy + pz[rows, :])
        gain = area / distance
        opposite = -gain
        for line in range(lines):
            turn = distance * turns[line]
            turn = turn - jnp.round(turn)
            b = 0.25 - jnp.abs(turn)
            u = b * b
            cosine = polynomial(SINE, u) * b
            sine = polynomial(COSINE, u)
            signed = jnp.where(turn < 0.0, opposite, gain)
            out[0, line, rows, 0:LANES] = (signed * sine).astype(BF16)
            out[0, line, rows, LANES : 2 * LANES] = (gain * cosine).astype(BF16)
        return carry

    lax.fori_loop(0, out.shape[2] // STRIP, strip, 0)


def pinned_to_vmem(array):
    return array if INTERPRET else pltpu.with_memory_space_constraint(array, pltpu.VMEM)


def make_tiles(place, wave, column, mine, other):
    points = 4 * LANES
    lines = wave.shape[0]
    vmem = pl.BlockSpec(memory_space=pltpu.VMEM)
    return pl.pallas_call(
        functools.partial(tile_kernel, place),
        out_shape=(
            jax.ShapeDtypeStruct((8, lines, points, 2 * LANES), BF16),
            jax.ShapeDtypeStruct((8, LANES), F32),
        ),
        grid=(2, 4),
        in_specs=[pl.BlockSpec(memory_space=pltpu.SMEM), vmem, vmem, vmem],
        out_specs=(
            pl.BlockSpec((1, lines, points, 2 * LANES), lambda h, i: (h * 4 + i, 0, 0, 0)),
            pl.BlockSpec((8, LANES), lambda h, i: (0, 0)),
        ),
        scratch_shapes=[pltpu.VMEM((points, LANES), F32)] * 3,
        cost_estimate=cost(8_000_000_000, 8 << 20),
        interpret=INTERPRET,
        name="tiles",
    )(wave, *[pinned_to_vmem(array) for array in (column, mine, other)])


def terms(tiles, block, line):
    total = None
    for source in range(block.shape[0]):
        upper = block[source, line]
        lower = jnp.concatenate([-upper[:, LANES:], upper[:, :LANES]], axis=1)
        stacked = jnp.concatenate([upper, lower], axis=0)
        term = jnp.dot(tiles[source, 0], stacked, preferred_element_type=F32)
        total = term if total is None else total + term
    return total


def near_kernel(tiles, near, token, out):
    out[0] = terms(tiles, near, pl.program_id(0))


def far_kernel(tiles, far, held, out):
    parts, _, share, columns = out.shape
    total = held[0] + terms(tiles, far, pl.program_id(0))
    out[:, 0] = total.astype(BF16).reshape(parts, share, columns)


def make_near(tiles, near, token):
    chunks, lines, points, depth = tiles.shape
    columns = near.shape[3]
    vmem = pl.BlockSpec(memory_space=pltpu.VMEM)
    return pl.pallas_call(
        near_kernel,
        out_shape=jax.ShapeDtypeStruct((lines, points, columns), F32),
        grid=(lines,),
        in_specs=[
            pl.BlockSpec((chunks // 2, 1, points, depth), lambda l: (0, l, 0, 0)),
            vmem,
            vmem,
        ],
        out_specs=pl.BlockSpec((1, points, columns), lambda l: (l, 0, 0)),
        cost_estimate=cost(lines * chunks * points * depth * columns, 7 << 20),
        interpret=INTERPRET,
        name="near",
    )(tiles, pinned_to_vmem(near), pinned_to_vmem(token))


def make_far(tiles, far, held, parts):
    chunks, lines, points, depth = tiles.shape
    columns = far.shape[3]
    return pl.pallas_call(
        far_kernel,
        out_shape=jax.ShapeDtypeStruct((parts, lines, points // parts, columns), BF16),
        grid=(lines,),
        in_specs=[
            pl.BlockSpec((chunks // 2, 1, points, depth), lambda l: (1, l, 0, 0)),
            pl.BlockSpec(memory_space=pltpu.VMEM),
            pl.BlockSpec((1, points, columns), lambda l: (l, 0, 0)),
        ],
        out_specs=pl.BlockSpec((parts, 1, points // parts, columns), lambda l: (0, l, 0, 0)),
        cost_estimate=cost(lines * chunks * points * depth * columns, 8 << 20),
        interpret=INTERPRET,
        name="far",
    )(tiles, pinned_to_vmem(far), held)


def level_kernel(rows, beside, out):
    levels = []
    for line in range(beside.shape[1]):
        total = beside[0, line].astype(F32)
        for source in range(1, beside.shape[0]):
            total = total + beside[source, line].astype(F32)
        levels.append(total.reshape(-1, rows, total.shape[1]))
    out[...] = jnp.concatenate(levels, axis=1).astype(BF16)


def make_level(beside, rows):
    _, lines, share, columns = beside.shape
    out = jax.ShapeDtypeStruct((share // rows, lines * rows, columns), BF16)
    return call(functools.partial(level_kernel, rows), out, [], [beside], "level")


def finish_kernel(wave, column, energy, pressure, sums):
    lines = energy.shape[0]
    total = column[0].astype(F32)
    for source in range(1, column.shape[0]):
        total = total + column[source].astype(F32)
    rows = total.shape[0] // lines
    parts = [
        total[line * rows : (line + 1) * rows] * (wave[line] * (0.5 / math.pi))
        for line in range(lines)
    ]
    rounded = jnp.concatenate(parts, axis=0).astype(BF16)
    pressure[...] = rounded
    wide = rounded.astype(F32)
    wide = wide * wide
    both = wide[:, :LANES] + wide[:, LANES:]
    power = [
        jnp.sum(both[line * rows : (line + 1) * rows], axis=0, keepdims=True)
        for line in range(lines)
    ]
    table = jnp.concatenate([energy[...]] + power, axis=0)
    for copy in range(sums.shape[0]):
        sums[copy] = table


def make_finish(wave, column, energy, copies):
    lines, cases = energy.shape
    _, rows, columns = column.shape
    out = (
        jax.ShapeDtypeStruct((rows, columns), BF16),
        jax.ShapeDtypeStruct((copies, 2 * lines, cases), F32),
    )
    return call(finish_kernel, out, [wave], [column, energy], "finish")


def fold_kernel(table, out):
    total = table[0]
    for source in range(1, table.shape[0]):
        total = total + table[source]
    for copy in range(out.shape[0]):
        out[copy] = total


def make_fold(table, copies):
    out = jax.ShapeDtypeStruct((copies,) + table.shape[1:], F32)
    return call(fold_kernel, out, [], [table], "fold")


def exchange(array, axes):
    return lax.all_to_all(array, axes, 0, 0, tiled=True)


def shards(forces, response, panel_plane, panel_area, field_points, wavenumber):
    lines, _, channels, cases = forces.shape
    own = response.shape[2]
    rows = field_points.shape[1] // lax.axis_size(SURF)
    place = lax.axis_index

    area = panel_area.reshape(-1, own)
    column, panel_rows = make_start(
        place, forces, panel_plane, area, field_points, lax.axis_size(DEPTH)
    )
    column = exchange(column, DEPTH)
    mine = exchange(make_spread(column, panel_rows, lax.axis_size(("x", "y"))), ("x", "y"))
    other = lax.ppermute(mine, "c", SWAP)
    velocity, energy = make_velocity(place, mine, other, response, lax.axis_size("x"))
    energy, column, tile_mine, tile_other = lax.optimization_barrier(
        (energy, column, mine, other)
    )
    near = exchange(velocity, "x")
    tiles, token = make_tiles(place, wavenumber, column, tile_mine, tile_other)
    near, token = lax.optimization_barrier((near, token))
    far = lax.ppermute(near, "c", SWAP)
    partial = make_far(tiles, far, make_near(tiles, near, token), lax.axis_size("y"))
    level = make_level(exchange(partial, "y"), rows)
    column = exchange(level, DEPTH)
    pressure, sums = make_finish(wavenumber, column, energy, lax.axis_size(LEVEL))
    sums = make_fold(exchange(sums, LEVEL), lax.axis_size(DEPTH))
    sums = jnp.sum(exchange(sums, DEPTH), axis=0)
    point_total = field_points.shape[1] * lax.axis_size(FIELD)
    panel_total = own * lax.axis_size(SURF + FIELD)
    efficiency = sums[lines:] / point_total / (sums[:lines] / panel_total + 1e-06)
    pressure = pressure.reshape(lines, rows, 2, cases).transpose(1, 0, 2, 3)
    return (pressure, efficiency)


def solution(mesh):
    grid = Mesh(np.asarray(mesh.devices).reshape(4, 4, 4, 4, 2), SURF + FIELD)
    return jax.shard_map(
        shards,
        mesh=grid,
        in_specs=(
            P(None, None, SURF, None),
            P(None, None, SURF + FIELD, None),
            P(None, SURF),
            P(SURF),
            P(None, FIELD),
            P(),
        ),
        out_specs=(P(FIELD + SURF, None, None, None), P()),
        check_vma=False,
    )
```

time: 195 us -> 158 us (0.81)
  blocking collectives: 27.9 us -> 95 us
  starting transfers between devices: 71 us -> 17.2 us
  other arithmetic: 37.7 us -> 0.61 us
  waiting for transfers between devices: 44.9 us -> 14.5 us
  Pallas kernels: 0 us -> 28.3 us
  local copies, waits for them, and re-layouts: 7.87 us -> 1.3 us
  matrix products: 3.81 us -> 0 us
    all_to_all x2 -> x5, blocking collectives: 27.9 us -> 95 us  [exchange(): return lax.all_to_all(array, axes, 0, 0, tiled=True)]
    another operation x3 -> x0, other arithmetic: 35.4 us -> none
    all_to_all x5 -> x2, starting transfers between devices: 40.3 us -> 8.56 us  [exchange(): return lax.all_to_all(array, axes, 0, 0, tiled=True)]
    all_to_all x5 -> x2, waiting for transfers between devices: 42.1 us -> 12.9 us  [exchange(): return lax.all_to_all(array, axes, 0, 0, tiled=True)]
    pallas_call x0 -> x9, Pallas kernels: none -> 28.3 us  [the longest x1 12.9 us: make_tiles(): pl.pallas_call(functools.partial(tile_kernel, place), out_shape=(jax.Shap...]
    ppermute x5 -> x2, starting transfers between devices: 30.7 us -> 8.64 us  [the longest x1 5.51 us: shards(): other = lax.ppermute(mine, 'c', SWAP)]
    dot_general x8 -> x0, matrix products: 3.81 us -> none  [the longest x4 2.88 us: shards(): summed = jnp.dot(tiles, stacked, preferred_element_type=jnp.float32)]
    broadcast_in_dim x5 -> x0, local copies, waits for them, and re-layouts: 3.23 us -> none  [gather(): return exchange(jnp.broadcast_to(array[None], (size,) + array.shape), axes)]
  transfers between devices with their start and end apart: 10 -> 4, of which waited for: 5 -> 3; matrix products, arithmetic and copies ran while one was open for 20% -> 0% of each run, Pallas kernels for 0% -> 11%
where the time goes in v3:
time: 158 us
  blocking collectives  95 us (60%)
  Pallas kernels  28.3 us (18%)
  starting transfers between devices  17.2 us (11%)
  waiting for transfers between devices  14.5 us (9%)
    all_to_all x5, blocking collectives, exchange(): return lax.all_to_all(array, axes, 0, 0, tiled=True)  95 us
    pallas_call x1, Pallas kernels, make_tiles(): pl.pallas_call(functools.partial(tile_kernel, place), out_shape=(jax.Shap...  12.9 us
    all_to_all x2, waiting for transfers between devices, exchange(): return lax.all_to_all(array, axes, 0, 0, tiled=True)  12.9 us
    all_to_all x2, starting transfers between devices, exchange(): return lax.all_to_all(array, axes, 0, 0, tiled=True)  8.56 us
    ppermute x1, starting transfers between devices, shards(): other = lax.ppermute(mine, 'c', SWAP)  5.51 us
    pallas_call x1, Pallas kernels, make_far(): pl.pallas_call(far_kernel, out_shape=jax.ShapeDtypeStruct((parts, lines,...  5.2 us
    pallas_call x6, Pallas kernels, call(): pl.pallas_call(kernel, out_shape=results, in_specs=[pl.BlockSpec(memory_s...  5.14 us
    pallas_call x1, Pallas kernels, make_near(): pl.pallas_call(near_kernel, out_shape=jax.ShapeDtypeStruct((lines, points...  5.03 us
  transfers between devices with their start and end apart: 4, of which 3 were waited for; matrix products, arithmetic and copies ran while one was open for 0% of the time, Pallas kernels for 11%

profile of v3, /device:TPU:1, one launch (start us, length us, event | category | flops | bytes accessed | tf_op | source)
XLA Modules:
  0.0 157.6 jit_solution(17270374141812600147)
XLA Ops:
  0.6 0.8 start.1
  1.4 27.1 %all_to_all.35.column = bf16[16,16,128]{2,1,0:T(8,128)(2,1)S(1)} all-to-all(bf16[16,16,128]{2,1,0:T(8,128)(2,1)S(1)} %get-tuple-element.16), channel_id=1, replica_groups=mesh['x'=4,'y'=4,'zl'=4,'zh'=4,'c'=2] {'zh','zl'}, dimensions={0} | all-to-all | bytes 131072 | tf_op jit(solution)/shard_map/all_to_all | solution.py:368
  28.5 0.1 spread.1
  28.6 16.1 %all_to_all.36.mine = bf16[16,144,128]{2,1,0:T(8,128)(2,1)S(1)} all-to-all(bf16[16,144,128]{2,1,0:T(8,128)(2,1)S(1)} %spread.1), channel_id=1, replica_groups=mesh['x'=4,'y'=4,'zl'=4,'zh'=4,'c'=2] {'x','y'}, dimensions={0} | all-to-all | bytes 1179648 | tf_op jit(solution)/shard_map/all_to_all | solution.py:368
  44.7 5.5 %collective-permute-start = (bf16[16,144,128]{2,1,0:T(8,128)(2,1)S(1)}, bf16[16,144,128]{2,1,0:T(8,128)(2,1)S(1)}, u32[]{:S(2)}, u32[]{:S(2)}) collective-permute-start(bf16[16,144,128]{2,1,0:T(8,128)(2,1)S(1)} %all_to_all.36.mine), channel_id=1, source_target_pairs={{0,1},{1,0},{2,3},{3,2},{4,5},{5,4},{6,7},{7,6},{8,9},{9,8},{10,11... | collective-permute-start | bytes 1769480 | tf_op jit(solution)/shard_map/ppermute | solution.py:383
  50.2 1.6 %collective-permute-done.other = bf16[16,144,128]{2,1,0:T(8,128)(2,1)S(1)} collective-permute-done((bf16[16,144,128]{2,1,0:T(8,128)(2,1)S(1)}, bf16[16,144,128]{2,1,0:T(8,128)(2,1)S(1)}, u32[]{:S(2)}, u32[]{:S(2)}) %collective-permute-start) | collective-permute-done | bytes 589856 | tf_op jit(solution)/shard_map/ppermute | solution.py:383
  51.8 2.8 %velocity.1 = (bf16[4,4,128,256]{3,2,1,0:T(8,128)(2,1)}, f32[4,128]{1,0:T(4,128)S(1)}) custom-call(bf16[16,144,128]{2,1,0:T(8,128)(2,1)S(1)} %all_to_all.36.mine, bf16[16,144,128]{2,1,0:T(8,128)(2,1)S(1)} %collective-permute-done.other, bf16[4,2,128,512]{3,2,1,0:T(8,128)(2,1)} %response.1), custom_call_target="tpu_custom_call" | custom-call | flops 268435456 | bytes 3145728 | tf_op jit(solution)/shard_map/velocity/pallas_call | solution.py:54
  54.6 3.5 %all-to-all-start.2 = ((bf16[4,4,128,256]{3,2,1,0:T(8,128)(2,1)}), bf16[4,4,128,256]{3,2,1,0:T(8,128)(2,1)S(1)}, u32[]{:S(2)}, u32[]{:S(2)}) async-start(bf16[4,4,128,256]{3,2,1,0:T(8,128)(2,1)} %get-tuple-element.23), calls=%async_computation.2 | async-start | bytes 2097152 | tf_op jit(solution)/shard_map/all_to_all | solution.py:368
  58.1 12.9 %tiles.1 = (bf16[8,4,512,256]{3,2,1,0:T(8,128)(2,1)}, f32[8,128]{1,0:T(8,128)}) custom-call(f32[4]{0:T(128)} %wave.3, bf16[16,16,128]{2,1,0:T(8,128)(2,1)S(1)} %all_to_all.35.column, bf16[16,144,128]{2,1,0:T(8,128)(2,1)S(1)} %all_to_all.36.mine, bf16[16,144,128]{2,1,0:T(8,128)(2,1)S(1)} %collective-permute-done.other), custom_call_target="tpu_custom_call" | custom-call | flops 8000000000 | bytes 8388608 | tf_op jit(solution)/shard_map/tiles/pallas_call | solution.py:225
  71.0 1.9 %all-to-all-done.2.near = bf16[4,4,128,256]{3,2,1,0:T(8,128)(2,1)S(1)} async-done(((bf16[4,4,128,256]{3,2,1,0:T(8,128)(2,1)}), bf16[4,4,128,256]{3,2,1,0:T(8,128)(2,1)S(1)}, u32[]{:S(2)}, u32[]{:S(2)}) %all-to-all-start.2) | async-done | bytes 1048608 | tf_op jit(solution)/shard_map/all_to_all | solution.py:368
  72.9 3.1 %collective-permute-start.1 = (bf16[4,4,128,256]{3,2,1,0:T(8,128)(2,1)S(1)}, bf16[4,4,128,256]{3,2,1,0:T(8,128)(2,1)S(1)}, u32[]{:S(2)}, u32[]{:S(2)}) collective-permute-start(bf16[4,4,128,256]{3,2,1,0:T(8,128)(2,1)S(1)} %all-to-all-done.2.near), channel_id=1, source_target_pairs={{0,1},{1,0},{2,3},{3,2},{4,5},{5,4},{6,7},{7,6},{8,9},{9,8},{10,11... | collective-permute-start | bytes 3145736 | tf_op jit(solution)/shard_map/ppermute | solution.py:391
  76.0 0.0 copy-start
  76.1 0.7 copy-done
  76.7 5.0 %near.1.held = f32[4,512,256]{2,1,0:T(8,128)} custom-call(bf16[8,4,512,256]{3,2,1,0:T(8,128)(2,1)} %get-tuple-element.22.tiles, bf16[4,4,128,256]{3,2,1,0:T(8,128)(2,1)S(1)} %all-to-all-done.2.near, f32[8,128]{1,0:T(8,128)S(1)} %copy-done), custom_call_target="tpu_custom_call" | custom-call | flops 1073741824 | bytes 7340032 | tf_op jit(solution)/shard_map/near/pallas_call | solution.py:269
  81.8 0.0 collective-permute-done.1.far
  81.8 5.2 %far.1 = bf16[4,4,128,256]{3,2,1,0:T(8,128)(2,1)} custom-call(bf16[8,4,512,256]{3,2,1,0:T(8,128)(2,1)} %get-tuple-element.22.tiles, bf16[4,4,128,256]{3,2,1,0:T(8,128)(2,1)S(1)} %collective-permute-done.1.far, f32[4,512,256]{2,1,0:T(8,128)} %near.1.held), custom_call_target="tpu_custom_call" | custom-call | flops 1073741824 | bytes 8388608 | tf_op jit(solution)/shard_map/far/pallas_call | solution.py:288
  87.0 18.4 %all_to_all.37.beside = bf16[4,4,128,256]{3,2,1,0:T(8,128)(2,1)S(1)} all-to-all(bf16[4,4,128,256]{3,2,1,0:T(8,128)(2,1)} %far.1), channel_id=1, replica_groups=mesh['x'=4,'y'=4,'zl'=4,'zh'=4,'c'=2] {'y'}, dimensions={0} | all-to-all | bytes 2097152 | tf_op jit(solution)/shard_map/all_to_all | solution.py:368
  105.3 0.1 level.1
  105.5 15.7 %all_to_all.38.column = bf16[16,32,256]{2,1,0:T(8,128)(2,1)S(1)} all-to-all(bf16[16,32,256]{2,1,0:T(8,128)(2,1)S(1)} %level.1), channel_id=1, replica_groups=mesh['x'=4,'y'=4,'zl'=4,'zh'=4,'c'=2] {'zh','zl'}, dimensions={0} | all-to-all | bytes 524288 | tf_op jit(solution)/shard_map/all_to_all | solution.py:368
  121.2 0.7 finish.1
  121.9 17.7 %all_to_all.39.table = f32[32,8,128]{2,1,0:T(8,128)S(1)} all-to-all(f32[32,8,128]{2,1,0:T(8,128)S(1)} %get-tuple-element.29), channel_id=1, replica_groups=mesh['x'=4,'y'=4,'zl'=4,'zh'=4,'c'=2] {'x','y','c'}, dimensions={0} | all-to-all | bytes 262144 | tf_op jit(solution)/shard_map/all_to_all | solution.py:368
  139.6 0.7 fold.1
  140.3 5.0 %all-to-all-start.6 = ((f32[16,8,128]{2,1,0:T(8,128)}), f32[16,8,128]{2,1,0:T(8,128)S(1)}, u32[]{:S(2)}, u32[]{:S(2)}) async-start(f32[16,8,128]{2,1,0:T(8,128)} %fold.1), calls=%async_computation.6 | async-start | bytes 131072 | tf_op jit(solution)/shard_map/all_to_all | solution.py:368
  145.3 0.6 copy.10
  146.0 11.0 %all-to-all-done.6 = f32[16,8,128]{2,1,0:T(8,128)S(1)} async-done(((f32[16,8,128]{2,1,0:T(8,128)}), f32[16,8,128]{2,1,0:T(8,128)S(1)}, u32[]{:S(2)}, u32[]{:S(2)}) %all-to-all-start.6) | async-done | bytes 65568 | tf_op jit(solution)/shard_map/all_to_all | solution.py:368
  157.0 0.6 add_divide_fusion
  (1 shorter events, 0.0 us)
Async XLA Ops:
  44.7 7.1 %collective-permute-start = (bf16[16,144,128]{2,1,0:T(8,128)(2,1)S(1)}, bf16[16,144,128]{2,1,0:T(8,128)(2,1)S(1)}, u32[]{:S(2)}, u32[]{:S(2)}) collective-permute-start(bf16[16,144,128]{2,1,0:T(8,128)(2,1)S(1)} %all_to_all.36.mine), channel_id=1, source_target_pairs={{0,1},{1,0},{2,3},{3,2},{4,5},{5,4},{6,7},{7,6},{8,9},{9,8},{10,11... | collective-permute-start | bytes 1769480 | tf_op jit(solution)/shard_map/ppermute | solution.py:383
  54.6 18.3 %all-to-all-start.2 = ((bf16[4,4,128,256]{3,2,1,0:T(8,128)(2,1)}), bf16[4,4,128,256]{3,2,1,0:T(8,128)(2,1)S(1)}, u32[]{:S(2)}, u32[]{:S(2)}) async-start(bf16[4,4,128,256]{3,2,1,0:T(8,128)(2,1)} %get-tuple-element.23), calls=%async_computation.2 | async-start | bytes 2097152 | tf_op jit(solution)/shard_map/all_to_all | solution.py:368
  72.9 8.9 %collective-permute-start.1 = (bf16[4,4,128,256]{3,2,1,0:T(8,128)(2,1)S(1)}, bf16[4,4,128,256]{3,2,1,0:T(8,128)(2,1)S(1)}, u32[]{:S(2)}, u32[]{:S(2)}) collective-permute-start(bf16[4,4,128,256]{3,2,1,0:T(8,128)(2,1)S(1)} %all-to-all-done.2.near), channel_id=1, source_target_pairs={{0,1},{1,0},{2,3},{3,2},{4,5},{5,4},{6,7},{7,6},{8,9},{9,8},{10,11... | collective-permute-start | bytes 3145736 | tf_op jit(solution)/shard_map/ppermute | solution.py:391
  76.0 0.7 copy-start
  140.3 16.7 %all-to-all-start.6 = ((f32[16,8,128]{2,1,0:T(8,128)}), f32[16,8,128]{2,1,0:T(8,128)S(1)}, u32[]{:S(2)}, u32[]{:S(2)}) async-start(f32[16,8,128]{2,1,0:T(8,128)} %fold.1), calls=%async_computation.6 | async-start | bytes 131072 | tf_op jit(solution)/shard_map/all_to_all | solution.py:368

commit v4 on v3

--- a/solution.py
+++ b/solution.py
@@ -9,13 +9,19 @@
 from jax.experimental.pallas import tpu as pltpu
 from jax.sharding import Mesh, PartitionSpec as P
 
-SURF = ("x", "y", "zl")
+SURF = ("s", "zl")
 FIELD = ("zh", "c")
 DEPTH = ("zh", "zl")
-LEVEL = ("x", "y", "c")
+LEVEL = ("s", "c")
 SWAP = [(0, 1), (1, 0)]
 LANES = 128
 STRIP = 32
+SIDE = 4
+PAIRS = [(a, b) for a in range(2) for b in range(2)]
+SQUARES = [[(2 * i + a) * SIDE + 2 * j + b for a, b in PAIRS] for i, j in PAIRS]
+SHIFTED = [
+    [(2 * i + a + 3) % SIDE * SIDE + (2 * j + b + 3) % SIDE for a, b in PAIRS] for i, j in PAIRS
+]
 GROUP = 16
 BF16 = jnp.bfloat16
 F32 = jnp.float32
@@ -79,30 +85,39 @@
 
 
 def start_kernel(place, forces, panel_plane, panel_area, field_points, out, panel_rows):
-    zh, core, x, zl = (place(axis) for axis in ("zh", "c", "x", "zl"))
-    lane = pl.multiple_of(x * LANES, LANES)
-    row = field_points[2:3, pl.ds(lane, LANES)]
+    zh, core, zl = (place(axis) for axis in ("zh", "c", "zl"))
+    x, y = lax.div(place("s"), SIDE), lax.rem(place("s"), SIDE)
+    x_first = lax.rem(2 * lax.div(lax.rem(x + 1, SIDE), 2) + 3, SIDE)
+    y_first = lax.rem(2 * lax.div(lax.rem(y + 1, SIDE), 2) + 3, SIDE)
+    piece = lax.broadcasted_iota(jnp.int32, (3, LANES), 1) // STRIP
+    block = jnp.zeros((3, LANES), F32)
+    for index, (a, b) in enumerate(PAIRS):
+        lane = pl.multiple_of(lax.rem(x_first + a, SIDE) * LANES, LANES)
+        shift = lax.rem(index + SIDE - lax.rem(y_first + b, SIDE), SIDE) * STRIP
+        moved = pltpu.roll(field_points[:, pl.ds(lane, LANES)], shift, 1)
+        block = jnp.where(piece == index, moved, block)
+    row = block[2:3]
     for coordinate in (0, 1):
-        other = field_points[coordinate : coordinate + 1, pl.ds(lane, LANES)]
-        row = jnp.where(zl == coordinate, other, row)
+        row = jnp.where(zl == coordinate, block[coordinate : coordinate + 1], row)
     point = jnp.concatenate(thirds_of(row) + [jnp.zeros((5, LANES), F32)], axis=0)
     force = forces[zh, core].astype(F32)
     chunk = jnp.concatenate([force, point], axis=0).astype(BF16)
     for copy in range(out.shape[0]):
         out[copy] = chunk
-    field = zh * 2 + core
-    lane = pl.multiple_of(field * LANES, LANES)
-    rows = thirds_of(panel_plane[0:1, pl.ds(lane, LANES)])
-    rows += thirds_of(panel_plane[1:2, pl.ds(lane, LANES)])
-    rows += thirds_of(panel_area[pl.ds(field, 1), :])
-    rows = jnp.concatenate(rows + [jnp.zeros((GROUP - 9, LANES), F32)], axis=0)
-    panel_rows[...] = rows.astype(BF16)
+    for half in range(2):
+        field = zh * 2 + lax.rem(core + half, 2)
+        lane = pl.multiple_of(field * LANES, LANES)
+        rows = thirds_of(panel_plane[0:1, pl.ds(lane, LANES)])
+        rows += thirds_of(panel_plane[1:2, pl.ds(lane, LANES)])
+        rows += thirds_of(panel_area[pl.ds(field, 1), :])
+        rows = jnp.concatenate(rows + [jnp.zeros((GROUP - 9, LANES), F32)], axis=0)
+        panel_rows[half] = rows.astype(BF16)
 
 
 def make_start(place, forces, panel_plane, panel_area, field_points, copies):
     out = (
         jax.ShapeDtypeStruct((copies, GROUP, LANES), BF16),
-        jax.ShapeDtypeStruct((GROUP, LANES), BF16),
+        jax.ShapeDtypeStruct((2, GROUP, LANES), BF16),
     )
     arrays = [forces, panel_plane, panel_area, field_points]
     return call(functools.partial(start_kernel, place), out, [], arrays, "start", pinned=0)
@@ -110,7 +125,7 @@
 
 def spread_kernel(column, panel_rows, out):
     rows = column[:, 0:8, :].astype(F32).reshape(-1, LANES).astype(BF16)
-    rows = jnp.concatenate([rows, panel_rows[...]], axis=0)
+    rows = jnp.concatenate([rows, panel_rows[0]], axis=0)
     for copy in range(out.shape[0]):
         out[copy] = rows
 
@@ -161,32 +176,54 @@
     )
 
 
-def tile_kernel(place, wave, column, mine, other, out, token, px, py, pz):
-    lines = out.shape[1]
-    sources = 4
+def square_place(place):
+    x, y = lax.div(place("s"), SIDE), lax.rem(place("s"), SIDE)
+    return 2 * lax.rem(x, 2) + lax.rem(y, 2), 2 * lax.div(x, 2) * SIDE + 2 * lax.div(y, 2)
+
+
+def set_points(column, token, px, py, pz):
+    for slot in range(4):
+        for coordinate, target in enumerate((px, py, pz)):
+            part = column[slot * 4 + coordinate].astype(F32)
+            row = part[8:9] + part[9:10] + part[10:11]
+            if coordinate == 2:
+                row = row * row
+            block = jnp.broadcast_to(row, (LANES, LANES)).T
+            for piece in range(4):
+                start = piece * LANES + slot * STRIP
+                target[start : start + STRIP, :] = block[piece * STRIP : (piece + 1) * STRIP, :]
+    token[...] = px[0:8, :]
+
+
+def own_kernel(wave, column, panel_rows, out, token, px, py, pz):
+    @pl.when(pl.program_id(0) == 0)
+    def _():
+        set_points(column, token, px, py, pz)
+
+    fill_tiles(wave, panel_rows[pl.program_id(0)].astype(F32), out, px, py, pz)
+
+
+def rest_kernel(place, wave, column, mine, other, before, out, token, px, py, pz):
     last = mine.shape[1] - GROUP
-    half, source = pl.program_id(0), pl.program_id(1)
-
-    @pl.when((half == 0) & (source == 0))
+    half, step = pl.program_id(0), pl.program_id(1)
+
+    @pl.when((half == 0) & (step == 0))
     def _():
-        for slot in range(4):
-            for coordinate, target in enumerate((px, py, pz)):
-                part = column[slot * 4 + coordinate].astype(F32)
-                row = part[8:9] + part[9:10] + part[10:11]
-                if coordinate == 2:
-                    row = row * row
-                block = jnp.broadcast_to(row, (LANES, LANES)).T
-                for piece in range(4):
-                    start = piece * LANES + slot * STRIP
-                    target[start : start + STRIP, :] = block[piece * STRIP : (piece + 1) * STRIP, :]
-        token[...] = px[0:8, :]
-
-    at = source * sources + place("y")
+        set_points(column, token, px, py, pz)
+
+    own, corner = square_place(place)
+    source = jnp.bitwise_xor(own, step + 1)
+    at = corner + lax.div(source, 2) * SIDE + lax.rem(source, 2)
     thirds = jnp.where(
         half == 0,
         mine[at, last : last + GROUP, :].astype(F32),
         other[at, last : last + GROUP, :].astype(F32),
     )
+    fill_tiles(wave, thirds, out, px, py, pz)
+
+
+def fill_tiles(wave, thirds, out, px, py, pz):
+    lines = out.shape[1]
     across = thirds[0:1] + thirds[1:2] + thirds[2:3]
     along = thirds[3:4] + thirds[4:5] + thirds[5:6]
     area = thirds[6:7] + thirds[7:8] + thirds[8:9]
@@ -218,87 +255,108 @@
     return array if INTERPRET else pltpu.with_memory_space_constraint(array, pltpu.VMEM)
 
 
-def make_tiles(place, wave, column, mine, other):
+def make_tiles(kernel, wave, arrays, grid, name, after=()):
     points = 4 * LANES
     lines = wave.shape[0]
     vmem = pl.BlockSpec(memory_space=pltpu.VMEM)
+    steps = math.prod(grid)
+    inner = grid[1] if len(grid) == 2 else 1
     return pl.pallas_call(
-        functools.partial(tile_kernel, place),
+        kernel,
         out_shape=(
-            jax.ShapeDtypeStruct((8, lines, points, 2 * LANES), BF16),
+            jax.ShapeDtypeStruct((steps, lines, points, 2 * LANES), BF16),
             jax.ShapeDtypeStruct((8, LANES), F32),
         ),
-        grid=(2, 4),
-        in_specs=[pl.BlockSpec(memory_space=pltpu.SMEM), vmem, vmem, vmem],
+        grid=grid,
+        in_specs=[pl.BlockSpec(memory_space=pltpu.SMEM)]
+        + [vmem] * len(arrays)
+        + [pl.BlockSpec(memory_space=pl.ANY)] * len(after),
         out_specs=(
-            pl.BlockSpec((1, lines, points, 2 * LANES), lambda h, i: (h * 4 + i, 0, 0, 0)),
-            pl.BlockSpec((8, LANES), lambda h, i: (0, 0)),
+            pl.BlockSpec(
+                (1, lines, points, 2 * LANES),
+                lambda h, i=0: (h * inner + i, 0, 0, 0),
+            ),
+            pl.BlockSpec((8, LANES), lambda *_: (0, 0)),
         ),
         scratch_shapes=[pltpu.VMEM((points, LANES), F32)] * 3,
-        cost_estimate=cost(8_000_000_000, 8 << 20),
+        cost_estimate=cost(steps * 1_000_000_000, steps << 20),
         interpret=INTERPRET,
-        name="tiles",
-    )(wave, *[pinned_to_vmem(array) for array in (column, mine, other)])
-
-
-def terms(tiles, block, line):
+        name=name,
+    )(wave, *[pinned_to_vmem(array) for array in arrays], *after)
+
+
+def make_own(wave, column, panel_rows):
+    return make_tiles(own_kernel, wave, [column, panel_rows], (2,), "own")
+
+
+def make_rest(place, wave, column, mine, other, before):
+    kernel = functools.partial(rest_kernel, place)
+    return make_tiles(kernel, wave, [column, mine, other], (2, 3), "rest", (before,))
+
+
+def terms(place, tiles, block, line):
+    own, _ = square_place(place)
     total = None
-    for source in range(block.shape[0]):
-        upper = block[source, line]
+    for step in range(block.shape[0]):
+        upper = block[jnp.bitwise_xor(own, step), line]
         lower = jnp.concatenate([-upper[:, LANES:], upper[:, :LANES]], axis=1)
         stacked = jnp.concatenate([upper, lower], axis=0)
-        term = jnp.dot(tiles[source, 0], stacked, preferred_element_type=F32)
+        term = jnp.dot(tiles[step][0, 0], stacked, preferred_element_type=F32)
         total = term if total is None else total + term
     return total
 
 
-def near_kernel(tiles, near, token, out):
-    out[0] = terms(tiles, near, pl.program_id(0))
-
-
-def far_kernel(tiles, far, held, out):
+def near_kernel(place, a, b, c, d, near, token, out):
+    out[0] = terms(place, (a, b, c, d), near, pl.program_id(0))
+
+
+def far_kernel(place, a, b, c, d, far, held, out):
     parts, _, share, columns = out.shape
-    total = held[0] + terms(tiles, far, pl.program_id(0))
+    total = held[0] + terms(place, (a, b, c, d), far, pl.program_id(0))
     out[:, 0] = total.astype(BF16).reshape(parts, share, columns)
 
 
-def make_near(tiles, near, token):
-    chunks, lines, points, depth = tiles.shape
+def tile_specs(half, points, depth):
+    specs = [pl.BlockSpec((1, 1, points, depth), lambda l: (half, l, 0, 0))]
+    for step in range(3):
+        at = half * 3 + step
+        specs.append(pl.BlockSpec((1, 1, points, depth), lambda l, at=at: (at, l, 0, 0)))
+    return specs
+
+
+def make_near(place, own, rest, near, token):
+    _, lines, points, depth = own.shape
     columns = near.shape[3]
-    vmem = pl.BlockSpec(memory_space=pltpu.VMEM)
     return pl.pallas_call(
-        near_kernel,
+        functools.partial(near_kernel, place),
         out_shape=jax.ShapeDtypeStruct((lines, points, columns), F32),
         grid=(lines,),
-        in_specs=[
-            pl.BlockSpec((chunks // 2, 1, points, depth), lambda l: (0, l, 0, 0)),
-            vmem,
-            vmem,
-        ],
+        in_specs=tile_specs(0, points, depth)
+        + [pl.BlockSpec(memory_space=pltpu.VMEM), pl.BlockSpec(memory_space=pl.ANY)],
         out_specs=pl.BlockSpec((1, points, columns), lambda l: (l, 0, 0)),
-        cost_estimate=cost(lines * chunks * points * depth * columns, 7 << 20),
+        cost_estimate=cost(8 * lines * points * depth * columns, 7 << 20),
         interpret=INTERPRET,
         name="near",
-    )(tiles, pinned_to_vmem(near), pinned_to_vmem(token))
-
-
-def make_far(tiles, far, held, parts):
-    chunks, lines, points, depth = tiles.shape
+    )(own, rest, rest, rest, pinned_to_vmem(near), token)
+
+
+def make_far(place, own, rest, far, held, parts):
+    _, lines, points, depth = own.shape
     columns = far.shape[3]
     return pl.pallas_call(
-        far_kernel,
+        functools.partial(far_kernel, place),
         out_shape=jax.ShapeDtypeStruct((parts, lines, points // parts, columns), BF16),
         grid=(lines,),
-        in_specs=[
-            pl.BlockSpec((chunks // 2, 1, points, depth), lambda l: (1, l, 0, 0)),
+        in_specs=tile_specs(1, points, depth)
+        + [
             pl.BlockSpec(memory_space=pltpu.VMEM),
             pl.BlockSpec((1, points, columns), lambda l: (l, 0, 0)),
         ],
         out_specs=pl.BlockSpec((parts, 1, points // parts, columns), lambda l: (0, l, 0, 0)),
-        cost_estimate=cost(lines * chunks * points * depth * columns, 8 << 20),
+        cost_estimate=cost(8 * lines * points * depth * columns, 8 << 20),
         interpret=INTERPRET,
         name="far",
-    )(tiles, pinned_to_vmem(far), held)
+    )(own, rest, rest, rest, pinned_to_vmem(far), held)
 
 
 def level_kernel(rows, beside, out):
@@ -364,8 +422,8 @@
     return call(fold_kernel, out, [], [table], "fold")
 
 
-def exchange(array, axes):
-    return lax.all_to_all(array, axes, 0, 0, tiled=True)
+def exchange(array, axes, groups=None):
+    return lax.all_to_all(array, axes, 0, 0, tiled=True, axis_index_groups=groups)
 
 
 def shards(forces, response, panel_plane, panel_area, field_points, wavenumber):
@@ -379,18 +437,22 @@
         place, forces, panel_plane, area, field_points, lax.axis_size(DEPTH)
     )
     column = exchange(column, DEPTH)
-    mine = exchange(make_spread(column, panel_rows, lax.axis_size(("x", "y"))), ("x", "y"))
+    mine = exchange(make_spread(column, panel_rows, lax.axis_size("s")), "s")
+    own_tiles, token = make_own(wavenumber, column, panel_rows)
+    mine, column, token = lax.optimization_barrier((mine, column, token))
     other = lax.ppermute(mine, "c", SWAP)
-    velocity, energy = make_velocity(place, mine, other, response, lax.axis_size("x"))
-    energy, column, tile_mine, tile_other = lax.optimization_barrier(
-        (energy, column, mine, other)
-    )
-    near = exchange(velocity, "x")
-    tiles, token = make_tiles(place, wavenumber, column, tile_mine, tile_other)
+    velocity, energy = make_velocity(place, mine, other, response, len(PAIRS))
+    energy, column, tile_mine, tile_other, token = lax.optimization_barrier(
+        (energy, column, mine, other, token)
+    )
+    near = exchange(velocity, "s", SQUARES)
+    rest_tiles, token = make_rest(place, wavenumber, column, tile_mine, tile_other, token)
     near, token = lax.optimization_barrier((near, token))
     far = lax.ppermute(near, "c", SWAP)
-    partial = make_far(tiles, far, make_near(tiles, near, token), lax.axis_size("y"))
-    level = make_level(exchange(partial, "y"), rows)
+    held = make_near(place, own_tiles, rest_tiles, near, token)
+    partial = make_far(place, own_tiles, rest_tiles, far, held, len(PAIRS))
+    beside = exchange(partial, "s", SHIFTED)
+    level = make_level(beside, rows)
     column = exchange(level, DEPTH)
     pressure, sums = make_finish(wavenumber, column, energy, lax.axis_size(LEVEL))
     sums = make_fold(exchange(sums, LEVEL), lax.axis_size(DEPTH))
@@ -403,7 +465,7 @@
 
 
 def solution(mesh):
-    grid = Mesh(np.asarray(mesh.devices).reshape(4, 4, 4, 4, 2), SURF + FIELD)
+    grid = Mesh(np.asarray(mesh.devices).reshape(16, 4, 4, 2), SURF + FIELD)
     return jax.shard_map(
         shards,
         mesh=grid,

time: 158 us -> 159 us (level)
  blocking collectives: 95 us -> 80.9 us
  starting transfers between devices: 17.2 us -> 23.9 us
  waiting for transfers between devices: 14.5 us -> 20.9 us
  Pallas kernels: 28.3 us -> 31 us
    all_to_all x5 -> x4, blocking collectives: 95 us -> 80.9 us  [exchange(): lax.all_to_all(array, axes, 0, 0, tiled=True, axis_index_groups=groups)]
    all_to_all x2 -> x3, starting transfers between devices: 8.56 us -> 15.5 us  [exchange(): lax.all_to_all(array, axes, 0, 0, tiled=True, axis_index_groups=groups)]
    all_to_all x2 -> x3, waiting for transfers between devices: 12.9 us -> 19.2 us  [exchange(): lax.all_to_all(array, axes, 0, 0, tiled=True, axis_index_groups=groups)]
    pallas_call x3 -> x4, Pallas kernels: 23.1 us -> 25 us  [the longest x2 14.8 us: make_tiles(): pl.pallas_call(kernel, out_shape=(jax.ShapeDtypeStruct((steps, lines, poi...]
  transfers between devices with their start and end apart: 4 -> 5, of which waited for: 3 -> 4; matrix products, arithmetic and copies ran while one was open for 0% -> 0% of each run, Pallas kernels for 11% -> 13%
where the time goes in v4:
time: 159 us
  blocking collectives  80.9 us (51%)
  Pallas kernels  31 us (19%)
  starting transfers between devices  23.9 us (15%)
  waiting for transfers between devices  20.9 us (13%)
    all_to_all x4, blocking collectives, exchange(): lax.all_to_all(array, axes, 0, 0, tiled=True, axis_index_groups=groups)  80.9 us
    all_to_all x3, waiting for transfers between devices, exchange(): lax.all_to_all(array, axes, 0, 0, tiled=True, axis_index_groups=groups)  19.2 us
    all_to_all x3, starting transfers between devices, exchange(): lax.all_to_all(array, axes, 0, 0, tiled=True, axis_index_groups=groups)  15.5 us
    pallas_call x2, Pallas kernels, make_tiles(): pl.pallas_call(kernel, out_shape=(jax.ShapeDtypeStruct((steps, lines, poi...  14.8 us
    pallas_call x6, Pallas kernels, call(): pl.pallas_call(kernel, out_shape=results, in_specs=[pl.BlockSpec(memory_s...  6.03 us
    ppermute x1, starting transfers between devices, shards(): other = lax.ppermute(mine, 'c', SWAP)  5.27 us
    pallas_call x1, Pallas kernels, make_far(): pl.pallas_call(functools.partial(far_kernel, place), out_shape=jax.ShapeD...  5.13 us
    pallas_call x1, Pallas kernels, make_near(): pl.pallas_call(functools.partial(near_kernel, place), out_shape=jax.Shape...  5 us
  transfers between devices with their start and end apart: 5, of which 4 were waited for; matrix products, arithmetic and copies ran while one was open for 0% of the time, Pallas kernels for 13%

profile of v4, /device:TPU:1, one launch (start us, length us, event | category | flops | bytes accessed | tf_op | source)
XLA Modules:
  0.0 158.6 jit_solution(8244465226881429347)
XLA Ops:
  0.6 0.8 start.1
  1.5 27.1 %all_to_all.35.column = bf16[16,16,128]{2,1,0:T(8,128)(2,1)S(1)} all-to-all(bf16[16,16,128]{2,1,0:T(8,128)(2,1)S(1)} %get-tuple-element.22), channel_id=1, replica_groups=mesh['s'=16,'zl'=4,'zh'=4,'c'=2] {'zh','zl'}, dimensions={0} | all-to-all | bytes 131072 | tf_op jit(solution)/shard_map/all_to_all | solution.py:426
  28.6 0.9 spread.1
  29.5 6.8 %all-to-all-start.1 = ((bf16[16,144,128]{2,1,0:T(8,128)(2,1)}), bf16[16,144,128]{2,1,0:T(8,128)(2,1)S(1)}, u32[]{:S(2)}, u32[]{:S(2)}) async-start(bf16[16,144,128]{2,1,0:T(8,128)(2,1)} %spread.1), calls=%async_computation.1 | async-start | bytes 1179648 | tf_op jit(solution)/shard_map/all_to_all | solution.py:426
  36.2 4.7 %own.1 = (bf16[2,4,512,256]{3,2,1,0:T(8,128)(2,1)}, f32[8,128]{1,0:T(8,128)}) custom-call(f32[4]{0:T(128)} %wave.5, bf16[16,16,128]{2,1,0:T(8,128)(2,1)S(1)} %all_to_all.35.column, bf16[2,16,128]{2,1,0:T(8,128)(2,1)S(1)} %get-tuple-element.23.panel_rows), custom_call_target="tpu_custom_call" | custom-call | flops 2000000000 | bytes 2097152 | tf_op jit(solution)/shard_map/own/pallas_call | solution.py:264
  40.9 5.1 %all-to-all-done.1.mine = bf16[16,144,128]{2,1,0:T(8,128)(2,1)S(1)} async-done(((bf16[16,144,128]{2,1,0:T(8,128)(2,1)}), bf16[16,144,128]{2,1,0:T(8,128)(2,1)S(1)}, u32[]{:S(2)}, u32[]{:S(2)}) %all-to-all-start.1) | async-done | bytes 589856 | tf_op jit(solution)/shard_map/all_to_all | solution.py:426
  46.0 5.3 %collective-permute-start = (bf16[16,144,128]{2,1,0:T(8,128)(2,1)S(1)}, bf16[16,144,128]{2,1,0:T(8,128)(2,1)S(1)}, u32[]{:S(2)}, u32[]{:S(2)}) collective-permute-start(bf16[16,144,128]{2,1,0:T(8,128)(2,1)S(1)} %all-to-all-done.1.mine), channel_id=1, source_target_pairs={{0,1},{1,0},{2,3},{3,2},{4,5},{5,4},{6,7},{7,6},{8,9},{9,8},{10,11... | collective-permute-start | bytes 1769480 | tf_op jit(solution)/shard_map/ppermute | solution.py:443
  51.3 1.6 %collective-permute-done.other = bf16[16,144,128]{2,1,0:T(8,128)(2,1)S(1)} collective-permute-done((bf16[16,144,128]{2,1,0:T(8,128)(2,1)S(1)}, bf16[16,144,128]{2,1,0:T(8,128)(2,1)S(1)}, u32[]{:S(2)}, u32[]{:S(2)}) %collective-permute-start) | collective-permute-done | bytes 589856 | tf_op jit(solution)/shard_map/ppermute | solution.py:443
  52.9 2.8 %velocity.1 = (bf16[4,4,128,256]{3,2,1,0:T(8,128)(2,1)}, f32[4,128]{1,0:T(4,128)S(1)}) custom-call(bf16[16,144,128]{2,1,0:T(8,128)(2,1)S(1)} %all-to-all-done.1.mine, bf16[16,144,128]{2,1,0:T(8,128)(2,1)S(1)} %collective-permute-done.other, bf16[4,2,128,512]{3,2,1,0:T(8,128)(2,1)} %response.1), custom_call_target="tpu_custom_call" | custom-call | flops 268435456 | bytes 3145728 | tf_op jit(solution)/shard_map/velocity/pallas_call | solution.py:60
  55.7 3.5 %all-to-all-start.2 = ((bf16[4,4,128,256]{3,2,1,0:T(8,128)(2,1)}), bf16[4,4,128,256]{3,2,1,0:T(8,128)(2,1)S(1)}, u32[]{:S(2)}, u32[]{:S(2)}) async-start(bf16[4,4,128,256]{3,2,1,0:T(8,128)(2,1)} %get-tuple-element.35), calls=%async_computation.2 | async-start | bytes 2097152 | tf_op jit(solution)/shard_map/all_to_all | solution.py:426
  59.2 10.2 %rest.1 = (bf16[6,4,512,256]{3,2,1,0:T(8,128)(2,1)}, f32[8,128]{1,0:T(8,128)}) custom-call(f32[4]{0:T(128)} %wave.5, bf16[16,16,128]{2,1,0:T(8,128)(2,1)S(1)} %all_to_all.35.column, bf16[16,144,128]{2,1,0:T(8,128)(2,1)S(1)} %all-to-all-done.1.mine, bf16[16,144,128]{2,1,0:T(8,128)(2,1)S(1)} %collective-permute-done.other, f32[8,128]{1,0:T(8,128)} %get-tuple-element.33.before), custom_call_target="tpu_custom_call" | custom-call | flops 6000000000 | bytes 6291456 | tf_op jit(solution)/shard_map/rest/pallas_call | solution.py:264
  69.4 3.1 %all-to-all-done.2.near = bf16[4,4,128,256]{3,2,1,0:T(8,128)(2,1)S(1)} async-done(((bf16[4,4,128,256]{3,2,1,0:T(8,128)(2,1)}), bf16[4,4,128,256]{3,2,1,0:T(8,128)(2,1)S(1)}, u32[]{:S(2)}, u32[]{:S(2)}) %all-to-all-start.2) | async-done | bytes 1048608 | tf_op jit(solution)/shard_map/all_to_all | solution.py:426
  72.5 3.1 %collective-permute-start.1 = (bf16[4,4,128,256]{3,2,1,0:T(8,128)(2,1)S(1)}, bf16[4,4,128,256]{3,2,1,0:T(8,128)(2,1)S(1)}, u32[]{:S(2)}, u32[]{:S(2)}) collective-permute-start(bf16[4,4,128,256]{3,2,1,0:T(8,128)(2,1)S(1)} %all-to-all-done.2.near), channel_id=1, source_target_pairs={{0,1},{1,0},{2,3},{3,2},{4,5},{5,4},{6,7},{7,6},{8,9},{9,8},{10,11... | collective-permute-start | bytes 3145736 | tf_op jit(solution)/shard_map/ppermute | solution.py:451
  75.6 5.0 %near.1.held = f32[4,512,256]{2,1,0:T(8,128)} custom-call(bf16[2,4,512,256]{3,2,1,0:T(8,128)(2,1)} %get-tuple-element.24.a, bf16[6,4,512,256]{3,2,1,0:T(8,128)(2,1)} %get-tuple-element.34.b.c.d, bf16[6,4,512,256]{3,2,1,0:T(8,128)(2,1)} %get-tuple-element.34.b.c.d, bf16[6,4,512,256]{3,2,1,0:T(8,128)(2,1)} %get-tuple-element.34.b.c.d, ...), custom_call_target="tpu_custom_call" | custom-call | flops 1073741824 | bytes 7340032 | tf_op jit(solution)/shard_map/near/pallas_call | solution.py:330
  80.6 0.0 collective-permute-done.1.far
  80.6 5.1 %far.1 = bf16[4,4,128,256]{3,2,1,0:T(8,128)(2,1)} custom-call(bf16[2,4,512,256]{3,2,1,0:T(8,128)(2,1)} %get-tuple-element.24.a, bf16[6,4,512,256]{3,2,1,0:T(8,128)(2,1)} %get-tuple-element.34.b.c.d, bf16[6,4,512,256]{3,2,1,0:T(8,128)(2,1)} %get-tuple-element.34.b.c.d, bf16[6,4,512,256]{3,2,1,0:T(8,128)(2,1)} %get-tuple-element.34.b.c.d, ...), custom_call_target="tpu_custom_call" | custom-call | flops 1073741824 | bytes 8388608 | tf_op jit(solution)/shard_map/far/pallas_call | solution.py:346
  85.8 18.3 %all_to_all.36.beside = bf16[4,4,128,256]{3,2,1,0:T(8,128)(2,1)S(1)} all-to-all(bf16[4,4,128,256]{3,2,1,0:T(8,128)(2,1)} %far.1), channel_id=1, replica_groups={{480,384,96,0},{416,448,32,64},{224,128,352,256},{160,192,288,320},{481..., dimensions={0} | all-to-all | bytes 2097152 | tf_op jit(solution)/shard_map/all_to_all | solution.py:426
  104.0 0.1 level.1
  104.2 15.7 %all_to_all.37.column = bf16[16,32,256]{2,1,0:T(8,128)(2,1)S(1)} all-to-all(bf16[16,32,256]{2,1,0:T(8,128)(2,1)S(1)} %level.1), channel_id=1, replica_groups=mesh['s'=16,'zl'=4,'zh'=4,'c'=2] {'zh','zl'}, dimensions={0} | all-to-all | bytes 524288 | tf_op jit(solution)/shard_map/all_to_all | solution.py:426
  119.9 0.7 finish.1
  120.6 19.9 %all_to_all.38.table = f32[32,8,128]{2,1,0:T(8,128)S(1)} all-to-all(f32[32,8,128]{2,1,0:T(8,128)S(1)} %get-tuple-element.41), channel_id=1, replica_groups=mesh['s'=16,'zl'=4,'zh'=4,'c'=2] {'s','c'}, dimensions={0} | all-to-all | bytes 262144 | tf_op jit(solution)/shard_map/all_to_all | solution.py:426
  140.5 0.7 fold.1
  141.1 5.2 %all-to-all-start.6 = ((f32[16,8,128]{2,1,0:T(8,128)}), f32[16,8,128]{2,1,0:T(8,128)S(1)}, u32[]{:S(2)}, u32[]{:S(2)}) async-start(f32[16,8,128]{2,1,0:T(8,128)} %fold.1), calls=%async_computation.6 | async-start | bytes 131072 | tf_op jit(solution)/shard_map/all_to_all | solution.py:426
  146.4 0.6 copy.10
  147.0 11.0 %all-to-all-done.6 = f32[16,8,128]{2,1,0:T(8,128)S(1)} async-done(((f32[16,8,128]{2,1,0:T(8,128)}), f32[16,8,128]{2,1,0:T(8,128)S(1)}, u32[]{:S(2)}, u32[]{:S(2)}) %all-to-all-start.6) | async-done | bytes 65568 | tf_op jit(solution)/shard_map/all_to_all | solution.py:426
  158.0 0.6 add_divide_fusion
  (1 shorter events, 0.0 us)
Async XLA Ops:
  29.5 16.5 %all-to-all-start.1 = ((bf16[16,144,128]{2,1,0:T(8,128)(2,1)}), bf16[16,144,128]{2,1,0:T(8,128)(2,1)S(1)}, u32[]{:S(2)}, u32[]{:S(2)}) async-start(bf16[16,144,128]{2,1,0:T(8,128)(2,1)} %spread.1), calls=%async_computation.1 | async-start | bytes 1179648 | tf_op jit(solution)/shard_map/all_to_all | solution.py:426
  46.0 6.9 %collective-permute-start = (bf16[16,144,128]{2,1,0:T(8,128)(2,1)S(1)}, bf16[16,144,128]{2,1,0:T(8,128)(2,1)S(1)}, u32[]{:S(2)}, u32[]{:S(2)}) collective-permute-start(bf16[16,144,128]{2,1,0:T(8,128)(2,1)S(1)} %all-to-all-done.1.mine), channel_id=1, source_target_pairs={{0,1},{1,0},{2,3},{3,2},{4,5},{5,4},{6,7},{7,6},{8,9},{9,8},{10,11... | collective-permute-start | bytes 1769480 | tf_op jit(solution)/shard_map/ppermute | solution.py:443
  55.7 16.8 %all-to-all-start.2 = ((bf16[4,4,128,256]{3,2,1,0:T(8,128)(2,1)}), bf16[4,4,128,256]{3,2,1,0:T(8,128)(2,1)S(1)}, u32[]{:S(2)}, u32[]{:S(2)}) async-start(bf16[4,4,128,256]{3,2,1,0:T(8,128)(2,1)} %get-tuple-element.35), calls=%async_computation.2 | async-start | bytes 2097152 | tf_op jit(solution)/shard_map/all_to_all | solution.py:426
  72.5 8.1 %collective-permute-start.1 = (bf16[4,4,128,256]{3,2,1,0:T(8,128)(2,1)S(1)}, bf16[4,4,128,256]{3,2,1,0:T(8,128)(2,1)S(1)}, u32[]{:S(2)}, u32[]{:S(2)}) collective-permute-start(bf16[4,4,128,256]{3,2,1,0:T(8,128)(2,1)S(1)} %all-to-all-done.2.near), channel_id=1, source_target_pairs={{0,1},{1,0},{2,3},{3,2},{4,5},{5,4},{6,7},{7,6},{8,9},{9,8},{10,11... | collective-permute-start | bytes 3145736 | tf_op jit(solution)/shard_map/ppermute | solution.py:451
  141.1 16.8 %all-to-all-start.6 = ((f32[16,8,128]{2,1,0:T(8,128)}), f32[16,8,128]{2,1,0:T(8,128)S(1)}, u32[]{:S(2)}, u32[]{:S(2)}) async-start(f32[16,8,128]{2,1,0:T(8,128)} %fold.1), calls=%async_computation.6 | async-start | bytes 131072 | tf_op jit(solution)/shard_map/all_to_all | solution.py:426

commit v5 on v4

v5 whole, which is shorter than its diff:
```python
import functools
import math

import jax
import jax.numpy as jnp
import numpy as np
from jax import lax
from jax.experimental import pallas as pl
from jax.experimental.pallas import tpu as pltpu
from jax.sharding import Mesh, PartitionSpec as P

SURF = ("s", "zl")
FIELD = ("zh", "c")
DEPTH = ("zh", "zl")
LEVEL = ("s", "c")
SWAP = [(0, 1), (1, 0)]
LANES = 128
STRIP = 32
SIDE = 4
GRID = ("s", "zl", "zh", "c")


def rings(first):
    groups = []
    for zl in range(SIDE):
        for zh in range(SIDE):
            for core in range(2):
                for fixed in range(SIDE):
                    chips = [
                        moving * SIDE + fixed if core == first else fixed * SIDE + moving
                        for moving in range(SIDE)
                    ]
                    groups.append([((chip * SIDE + zl) * SIDE + zh) * 2 + core for chip in chips])
    return groups


GATHER = rings(0)
REDUCE = rings(1)
GROUP = 16
BF16 = jnp.bfloat16
F32 = jnp.float32
INTERPRET = False


def fitted(function, count):
    top = 0.0625
    nodes = 0.5 * top * (1.0 - np.cos(np.pi * (np.arange(count) + 0.5) / count))
    powers = np.vander(nodes, count, increasing=True)
    return [float(value) for value in np.linalg.solve(powers, function(np.sqrt(nodes)))]


SINE = fitted(lambda b: np.sin(2.0 * np.pi * b) / b, 5)
COSINE = fitted(lambda b: np.cos(2.0 * np.pi * b), 5)


def polynomial(coefficients, u):
    total = u * coefficients[-1] + coefficients[-2]
    for value in coefficients[-3::-1]:
        total = total * u + value
    return total


def call(kernel, out, scalars, arrays, name, scratch=(), cost=None, pinned=9):
    single = not isinstance(out, (list, tuple))
    shapes = (out,) if single else tuple(out)
    if INTERPRET:
        results = tuple(jax.ShapeDtypeStruct(s.shape, s.dtype) for s in shapes)
    else:
        results = tuple(pltpu.VMEM(s.shape, s.dtype) for s in shapes)
        arrays = [
            pltpu.with_memory_space_constraint(array, pltpu.VMEM) if index < pinned else array
            for index, array in enumerate(arrays)
        ]
    outs = pl.pallas_call(
        kernel,
        out_shape=results,
        in_specs=[pl.BlockSpec(memory_space=pltpu.SMEM)] * len(scalars)
        + [
            pl.BlockSpec(memory_space=pltpu.VMEM) if index < pinned else pl.BlockSpec()
            for index in range(len(arrays))
        ],
        out_specs=tuple(pl.BlockSpec(memory_space=pltpu.VMEM) for _ in shapes),
        scratch_shapes=list(scratch),
        cost_estimate=cost,
        interpret=INTERPRET,
        name=name,
    )(*scalars, *arrays)
    return outs[0] if single else outs


def cost(flops, moved):
    return pl.CostEstimate(flops=flops, bytes_accessed=moved, transcendentals=0)


def thirds_of(row):
    high = row.astype(BF16).astype(F32)
    middle = (row - high).astype(BF16).astype(F32)
    return [high, middle, row - high - middle]


def start_kernel(place, forces, panel_plane, panel_area, field_points, out, panel_rows):
    zh, core, zl = (place(axis) for axis in ("zh", "c", "zl"))
    x, y = lax.div(place("s"), SIDE), lax.rem(place("s"), SIDE)
    along_y = field_points[:, pl.ds(pl.multiple_of(x * LANES, LANES), LANES)]
    piece = lax.broadcasted_iota(jnp.int32, (3, LANES), 1) // STRIP
    along_x = jnp.zeros((3, LANES), F32)
    for index in range(SIDE):
        shift = lax.rem(index + SIDE - y, SIDE) * STRIP
        moved = pltpu.roll(field_points[:, index * LANES : (index + 1) * LANES], shift, 1)
        along_x = jnp.where(piece == index, moved, along_x)
    point = []
    for block in (
        jnp.where(core == 0, along_y, along_x),
        jnp.where(core == 0, along_x, along_y),
    ):
        row = block[2:3]
        for coordinate in (0, 1):
            row = jnp.where(zl == coordinate, block[coordinate : coordinate + 1], row)
        point += thirds_of(row)
    point = jnp.concatenate(point + [jnp.zeros((2, LANES), F32)], axis=0)
    force = forces[zh, core].astype(F32)
    chunk = jnp.concatenate([force, point], axis=0).astype(BF16)
    for copy in range(out.shape[0]):
        out[copy] = chunk
    for half in range(2):
        field = zh * 2 + lax.rem(core + half, 2)
        lane = pl.multiple_of(field * LANES, LANES)
        rows = thirds_of(panel_plane[0:1, pl.ds(lane, LANES)])
        rows += thirds_of(panel_plane[1:2, pl.ds(lane, LANES)])
        rows += thirds_of(panel_area[pl.ds(field, 1), :])
        rows = jnp.concatenate(rows + [jnp.zeros((GROUP - 9, LANES), F32)], axis=0)
        panel_rows[half] = rows.astype(BF16)


def make_start(place, forces, panel_plane, panel_area, field_points, copies):
    out = (
        jax.ShapeDtypeStruct((copies, GROUP, LANES), BF16),
        jax.ShapeDtypeStruct((2, GROUP, LANES), BF16),
    )
    arrays = [forces, panel_plane, panel_area, field_points]
    return call(functools.partial(start_kernel, place), out, [], arrays, "start", pinned=0)


def spread_kernel(column, panel_rows, out):
    rows = column[:, 0:8, :].astype(F32).reshape(-1, LANES).astype(BF16)
    rows = jnp.concatenate([rows, panel_rows[0]], axis=0)
    for copy in range(out.shape[0]):
        out[copy] = rows


def make_spread(column, panel_rows, copies):
    rows = column.shape[0] * 8 + GROUP
    out = jax.ShapeDtypeStruct((copies, rows, LANES), BF16)
    return call(spread_kernel, out, [], [column, panel_rows], "spread")


def velocity_kernel(place, mine, other, response, keep, give, energy):
    core = place("c")
    lines = response.shape[0]
    depth = response.shape[3] // mine.shape[0]
    for line in range(lines):
        rows = slice(line * depth, (line + 1) * depth)
        a = mine[:, rows, :].reshape(-1, LANES)
        b = other[:, rows, :].reshape(-1, LANES)
        real = jnp.where(core == 0, a, b)
        imag = jnp.where(core == 0, b, a)
        upper = jnp.concatenate([real, imag], axis=1)
        lower = jnp.concatenate([-imag, real], axis=1)
        total = jnp.dot(response[line, 0], upper, preferred_element_type=F32)
        total = total + jnp.dot(response[line, 1], lower, preferred_element_type=F32)
        rounded = total.astype(BF16)
        half, at = divmod(line, lines // 2)

        @pl.when(core == half)
        def _():
            keep[at] = rounded

        @pl.when(core != half)
        def _():
            give[at] = rounded

        wide = rounded.astype(F32)
        squares = jnp.sum(wide * wide, axis=0, keepdims=True)
        energy[line : line + 1, :] = squares[:, :LANES] + squares[:, LANES:]


def make_velocity(place, mine, other, response):
    lines, _, own, channels = response.shape
    half = jax.ShapeDtypeStruct((lines // 2, own, 2 * LANES), BF16)
    out = (half, half, jax.ShapeDtypeStruct((lines, LANES), F32))
    work = cost(8 * lines * own * channels * LANES, 3 << 20)
    kernel = functools.partial(velocity_kernel, place)
    arrays = [mine, other, response]
    return call(kernel, out, [], arrays, "velocity", cost=work, pinned=2)


def pack_kernel(keep, got, out):
    for copy in range(out.shape[0]):
        out[copy, 0] = keep[...]
        out[copy, 1] = got[...]


def make_pack(keep, got):
    out = jax.ShapeDtypeStruct((SIDE, 2) + keep.shape, BF16)
    return call(pack_kernel, out, [], [keep, got], "pack")


def ring_place(place):
    x, y = lax.div(place("s"), SIDE), lax.rem(place("s"), SIDE)
    first = place("c") == 0
    return jnp.where(first, x, y), jnp.where(first, y, x * SIDE), jnp.where(first, SIDE, 1)


def set_points(column, partner, token, px, py, pz):
    for half, (array, base) in enumerate(((column, 8), (partner, 11))):
        for slot in range(4):
            for coordinate, target in enumerate((px, py, pz)):
                part = array[slot * 4 + coordinate].astype(F32)
                row = part[base : base + 1] + part[base + 1 : base + 2] + part[base + 2 : base + 3]
                if coordinate == 2:
                    row = row * row
                block = jnp.broadcast_to(row, (LANES, LANES)).T
                for piece in range(SIDE):
                    start = (piece * 2 + half) * LANES + slot * STRIP
                    target[start : start + STRIP, :] = block[piece * STRIP : (piece + 1) * STRIP, :]
    token[...] = px[0:8, :]


def own_kernel(place, wave, column, partner, panel_rows, out, token, px, py, pz):
    @pl.when(pl.program_id(0) == 0)
    def _():
        set_points(column, partner, token, px, py, pz)

    fill_tiles(place, wave, panel_rows[pl.program_id(0)].astype(F32), out, px, py, pz)


def rest_kernel(place, wave, column, partner, mine, other, before, out, token, px, py, pz):
    last = mine.shape[1] - GROUP
    half, step = pl.program_id(0), pl.program_id(1)

    @pl.when((half == 0) & (step == 0))
    def _():
        set_points(column, partner, token, px, py, pz)

    own, origin, stride = ring_place(place)
    at = origin + stride * jnp.bitwise_xor(own, step + 1)
    thirds = jnp.where(
        half == 0,
        mine[at, last : last + GROUP, :].astype(F32),
        other[at, last : last + GROUP, :].astype(F32),
    )
    fill_tiles(place, wave, thirds, out, px, py, pz)


def fill_tiles(place, wave, thirds, out, px, py, pz):
    lines = out.shape[1]
    across = thirds[0:1] + thirds[1:2] + thirds[2:3]
    along = thirds[3:4] + thirds[4:5] + thirds[5:6]
    area = thirds[6:7] + thirds[7:8] + thirds[8:9]
    turns = [wave[place("c") * lines + line] * (0.5 / math.pi) for line in range(lines)]

    def strip(index, carry):
        rows = pl.ds(pl.multiple_of(index * STRIP, STRIP), STRIP)
        dx = px[rows, :] - across
        dy = py[rows, :] - along
        distance = jnp.sqrt(dx * dx + dy * dy + pz[rows, :])
        gain = area / distance
        opposite = -gain
        for line in range(lines):
            turn = distance * turns[line]
            turn = turn - jnp.round(turn)
            b = 0.25 - jnp.abs(turn)
            u = b * b
            cosine = polynomial(SINE, u) * b
            sine = polynomial(COSINE, u)
            signed = jnp.where(turn < 0.0, opposite, gain)
            out[0, line, rows, 0:LANES] = (signed * sine).astype(BF16)
            out[0, line, rows, LANES : 2 * LANES] = (gain * cosine).astype(BF16)
        return carry

    lax.fori_loop(0, out.shape[2] // STRIP, strip, 0)


def pinned_to_vmem(array):
    return array if INTERPRET else pltpu.with_memory_space_constraint(array, pltpu.VMEM)


def make_tiles(kernel, wave, arrays, grid, name, after=()):
    points = 8 * LANES
    lines = wave.shape[0] // 2
    vmem = pl.BlockSpec(memory_space=pltpu.VMEM)
    steps = math.prod(grid)
    inner = grid[1] if len(grid) == 2 else 1
    return pl.pallas_call(
        kernel,
        out_shape=(
            jax.ShapeDtypeStruct((steps, lines, points, 2 * LANES), BF16),
            jax.ShapeDtypeStruct((8, LANES), F32),
        ),
        grid=grid,
        in_specs=[pl.BlockSpec(memory_space=pltpu.SMEM)]
        + [vmem] * len(arrays)
        + [pl.BlockSpec(memory_space=pl.ANY)] * len(after),
        out_specs=(
            pl.BlockSpec(
                (1, lines, points, 2 * LANES),
                lambda h, i=0: (h * inner + i, 0, 0, 0),
            ),
            pl.BlockSpec((8, LANES), lambda *_: (0, 0)),
        ),
        scratch_shapes=[pltpu.VMEM((points, LANES), F32)] * 3,
        cost_estimate=cost(steps * 1_000_000_000, steps << 20),
        interpret=INTERPRET,
        name=name,
    )(wave, *[pinned_to_vmem(array) for array in arrays], *after)


def make_own(place, wave, column, partner, panel_rows):
    kernel = functools.partial(own_kernel, place)
    return make_tiles(kernel, wave, [column, partner, panel_rows], (2,), "own")


def make_rest(place, wave, column, partner, mine, other, before):
    kernel = functools.partial(rest_kernel, place)
    arrays = [column, partner, mine, other]
    return make_tiles(kernel, wave, arrays, (2, 3), "rest", (before,))


def partial_kernel(place, *refs):
    tiles, near, out = refs[:8], refs[8], refs[-1]
    line = pl.program_id(0)
    own, _, _ = ring_place(place)
    total = None
    for half in range(2):
        for step in range(SIDE):
            upper = near[jnp.bitwise_xor(own, step), half, line]
            lower = jnp.concatenate([-upper[:, LANES:], upper[:, :LANES]], axis=1)
            stacked = jnp.concatenate([upper, lower], axis=0)
            tile = tiles[half * SIDE + step][0, 0]
            term = jnp.dot(tile, stacked, preferred_element_type=F32)
            total = term if total is None else total + term
    parts, _, share, columns = out.shape
    out[:, 0] = total.astype(BF16).reshape(parts, share, columns)


def make_partial(place, own, rest, near):
    _, lines, points, depth = own.shape
    columns = near.shape[-1]
    step_rows = points // 2
    share = points // SIDE
    specs = []
    for half in range(2):
        for step in range(SIDE):
            at = half if step == 0 else half * 3 + step - 1
            specs.append(
                pl.BlockSpec((1, 1, step_rows, depth), lambda l, i, at=at: (at, l, i, 0))
            )
    return pl.pallas_call(
        functools.partial(partial_kernel, place),
        out_shape=jax.ShapeDtypeStruct((SIDE, lines, share, columns), BF16),
        grid=(lines, 2),
        in_specs=specs + [pl.BlockSpec(memory_space=pltpu.VMEM)],
        out_specs=pl.BlockSpec((2, 1, share, columns), lambda l, i: (i, l, 0, 0)),
        cost_estimate=cost(16 * lines * points * depth * columns, 10 << 20),
        interpret=INTERPRET,
        name="partial",
    )(*(([own] + [rest] * 3) * 2), pinned_to_vmem(near))


def level_kernel(rows, beside, out):
    levels = []
    for line in range(beside.shape[1]):
        total = beside[0, line].astype(F32)
        for source in range(1, beside.shape[0]):
            total = total + beside[source, line].astype(F32)
        share = total.shape[0] // 2
        for half in range(2):
            part = total[half * share : (half + 1) * share]
            levels.append(part.reshape(-1, rows, total.shape[1]))
    out[...] = jnp.concatenate(levels, axis=1).astype(BF16)


def make_level(beside, rows):
    _, lines, share, columns = beside.shape
    out = jax.ShapeDtypeStruct((share // (2 * rows), lines * 2 * rows, columns), BF16)
    return call(functools.partial(level_kernel, rows), out, [], [beside], "level")


def finish_kernel(place, wave, column, energy, keep, give, sums):
    lines = energy.shape[0]
    core = place("c")
    total = column[0].astype(F32)
    for source in range(1, column.shape[0]):
        total = total + column[source].astype(F32)
    half = lines // 2
    share = total.shape[0] // half
    rows = share // 2
    parts = [
        total[line * share : (line + 1) * share] * (wave[core * half + line] * (0.5 / math.pi))
        for line in range(half)
    ]
    rounded = jnp.concatenate(parts, axis=0).astype(BF16)
    wide = rounded.astype(F32)
    for line in range(half):
        start = line * share
        keep[line * rows : (line + 1) * rows, :] = wide[start : start + rows].astype(BF16)
        give[line * rows : (line + 1) * rows, :] = wide[start + rows : start + share].astype(BF16)
    wide = wide * wide
    both = wide[:, :LANES] + wide[:, LANES:]
    power = [
        jnp.sum(both[line * share : (line + 1) * share], axis=0, keepdims=True)
        for line in range(half)
    ]
    nothing = jnp.zeros_like(power[0])
    power = [jnp.where(core == line // half, power[line % half], nothing) for line in range(lines)]
    table = jnp.concatenate([energy[...]] + power, axis=0)
    for copy in range(sums.shape[0]):
        sums[copy] = table


def make_finish(place, wave, column, energy, copies):
    lines, cases = energy.shape
    _, rows, columns = column.shape
    half = jax.ShapeDtypeStruct((rows // 2, columns), BF16)
    out = (half, half, jax.ShapeDtypeStruct((copies, 2 * lines, cases), F32))
    kernel = functools.partial(finish_kernel, place)
    return call(kernel, out, [wave], [column, energy], "finish")


def fold_kernel(table, out):
    total = table[0]
    for source in range(1, table.shape[0]):
        total = total + table[source]
    for copy in range(out.shape[0]):
        out[copy] = total


def make_fold(table, copies):
    out = jax.ShapeDtypeStruct((copies,) + table.shape[1:], F32)
    return call(fold_kernel, out, [], [table], "fold")


def exchange(array, axes, groups=None):
    return lax.all_to_all(array, axes, 0, 0, tiled=True, axis_index_groups=groups)


def shards(forces, response, panel_plane, panel_area, field_points, wavenumber):
    lines, _, channels, cases = forces.shape
    own = response.shape[2]
    rows = field_points.shape[1] // lax.axis_size(SURF)
    place = lax.axis_index

    area = panel_area.reshape(-1, own)
    column, panel_rows = make_start(
        place, forces, panel_plane, area, field_points, lax.axis_size(DEPTH)
    )
    column = exchange(column, DEPTH)
    mine = exchange(make_spread(column, panel_rows, lax.axis_size("s")), "s")
    partner = lax.ppermute(column, "c", SWAP)
    own_tiles, token = make_own(place, wavenumber, column, partner, panel_rows)
    mine, column, partner, token = lax.optimization_barrier((mine, column, partner, token))
    other = lax.ppermute(mine, "c", SWAP)
    keep, give, energy = make_velocity(place, mine, other, response)
    near = exchange(make_pack(keep, lax.ppermute(give, "c", SWAP)), GRID, GATHER)
    energy, column, partner, tile_mine, tile_other, token = lax.optimization_barrier(
        (energy, column, partner, mine, other, token)
    )
    rest_tiles, _ = make_rest(
        place, wavenumber, column, partner, tile_mine, tile_other, token
    )
    partial = make_partial(place, own_tiles, rest_tiles, near)
    level = make_level(exchange(partial, GRID, REDUCE), rows)
    column = exchange(level, DEPTH)
    keep, give, sums = make_finish(place, wavenumber, column, energy, lax.axis_size(LEVEL))
    got = lax.ppermute(give, "c", SWAP)
    sums = make_fold(exchange(sums, LEVEL), lax.axis_size(DEPTH))
    sums = jnp.sum(exchange(sums, DEPTH), axis=0)
    point_total = field_points.shape[1] * lax.axis_size(FIELD)
    panel_total = own * lax.axis_size(SURF + FIELD)
    efficiency = sums[lines:] / point_total / (sums[:lines] / panel_total + 1e-06)
    first = lax.axis_index("c") == 0
    pressure = jnp.concatenate([jnp.where(first, keep, got), jnp.where(first, got, keep)], axis=0)
    pressure = pressure.reshape(lines, rows, 2, cases).transpose(1, 0, 2, 3)
    return (pressure, efficiency)


def solution(mesh):
    grid = Mesh(np.asarray(mesh.devices).reshape(16, 4, 4, 2), SURF + FIELD)
    return jax.shard_map(
        shards,
        mesh=grid,
        in_specs=(
            P(None, None, SURF, None),
            P(None, None, SURF + FIELD, None),
            P(None, SURF),
            P(SURF),
            P(None, FIELD),
            P(),
        ),
        out_specs=(P(FIELD + SURF, None, None, None), P()),
        check_vma=False,
    )
```

time: 159 us -> 153 us (0.962)
  blocking collectives: 80.9 us -> 56.3 us
  starting transfers between devices: 23.9 us -> 40.3 us
  local copies, waits for them, and re-layouts: 0.62 us -> 2.3 us
    all_to_all x4 -> x3, blocking collectives: 80.9 us -> 56.3 us  [exchange(): lax.all_to_all(array, axes, 0, 0, tiled=True, axis_index_groups=groups)]
    all_to_all x3 -> x4, starting transfers between devices: 15.5 us -> 27.3 us  [exchange(): lax.all_to_all(array, axes, 0, 0, tiled=True, axis_index_groups=groups)]
    ppermute x1 -> x3, starting transfers between devices: 3.13 us -> 8.73 us  [the longest x1 4.3 us: shards(): partner = lax.ppermute(column, 'c', SWAP)]
    pallas_call x2 -> x1, Pallas kernels: 10.1 us -> 6.19 us  [make_partial(): pl.pallas_call(functools.partial(partial_kernel, place), out_shape=jax.Sh...]
    pallas_call x2, Pallas kernels: 14.8 us -> 18 us  [make_tiles(): pl.pallas_call(kernel, out_shape=(jax.ShapeDtypeStruct((steps, lines, poi...]
    all_to_all x3 -> x4, waiting for transfers between devices: 19.2 us -> 16.5 us  [exchange(): lax.all_to_all(array, axes, 0, 0, tiled=True, axis_index_groups=groups)]
    ppermute x1 -> x3, waiting for transfers between devices: 0.01 us -> 1.85 us  [the longest x1 0.96 us: shards(): lax.ppermute(give, 'c', SWAP)]
    unnamed x0 -> x8, local copies, waits for them, and re-layouts: none -> 1.68 us
  transfers between devices with their start and end apart: 5 -> 8, of which waited for: 4 -> 5; matrix products, arithmetic and copies ran while one was open for 0% -> 0% of each run, Pallas kernels for 13% -> 12%
where the time goes in v5:
time: 153 us; the launch traced here: 152 us
  blocking collectives  56.3 us (37%)
  starting transfers between devices  40.3 us (26%)
  Pallas kernels  31.7 us (21%)
  waiting for transfers between devices  19.9 us (13%)
  local copies, waits for them, and re-layouts  2.3 us (2%)
    all_to_all x3, blocking collectives, exchange(): lax.all_to_all(array, axes, 0, 0, tiled=True, axis_index_groups=groups)  56.3 us
    all_to_all x4, starting transfers between devices, exchange(): lax.all_to_all(array, axes, 0, 0, tiled=True, axis_index_groups=groups)  27.3 us
    pallas_call x2, Pallas kernels, make_tiles(): pl.pallas_call(kernel, out_shape=(jax.ShapeDtypeStruct((steps, lines, poi...  18 us
    all_to_all x4, waiting for transfers between devices, exchange(): lax.all_to_all(array, axes, 0, 0, tiled=True, axis_index_groups=groups)  16.5 us
    pallas_call x7, Pallas kernels, call(): pl.pallas_call(kernel, out_shape=results, in_specs=[pl.BlockSpec(memory_s...  7.47 us
    pallas_call x1, Pallas kernels, make_partial(): pl.pallas_call(functools.partial(partial_kernel, place), out_shape=jax.Sh...  6.19 us
    ppermute x1, starting transfers between devices, shards(): partner = lax.ppermute(column, 'c', SWAP)  4.3 us
    ppermute x1, starting transfers between devices, shards(): other = lax.ppermute(mine, 'c', SWAP)  4.29 us
  transfers between devices with their start and end apart: 8, of which 5 were waited for; matrix products, arithmetic and copies ran while one was open for 0% of the time, Pallas kernels for 12%

profile of v5, /device:TPU:1, one launch (start us, length us, event | category | flops | bytes accessed | tf_op | source)
XLA Modules:
  0.0 151.9 jit_solution(3573407234037606412)
XLA Ops:
  0.6 0.8 start.1
  1.5 27.1 %all_to_all.35.column = bf16[16,16,128]{2,1,0:T(8,128)(2,1)S(1)} all-to-all(bf16[16,16,128]{2,1,0:T(8,128)(2,1)S(1)} %get-tuple-element.23), channel_id=1, replica_groups=mesh['s'=16,'zl'=4,'zh'=4,'c'=2] {'zh','zl'}, dimensions={0} | all-to-all | bytes 131072 | tf_op jit(solution)/shard_map/all_to_all | solution.py:444
  28.6 0.9 spread.1
  29.5 6.8 %all-to-all-start.1 = ((bf16[16,144,128]{2,1,0:T(8,128)(2,1)}), bf16[16,144,128]{2,1,0:T(8,128)(2,1)S(1)}, u32[]{:S(2)}, u32[]{:S(2)}) async-start(bf16[16,144,128]{2,1,0:T(8,128)(2,1)} %spread.1), calls=%async_computation.1 | async-start | bytes 1179648 | tf_op jit(solution)/shard_map/all_to_all | solution.py:444
  36.2 4.3 %collective-permute-start = (bf16[16,16,128]{2,1,0:T(8,128)(2,1)S(1)}, bf16[16,16,128]{2,1,0:T(8,128)(2,1)S(1)}, u32[]{:S(2)}, u32[]{:S(2)}) collective-permute-start(bf16[16,16,128]{2,1,0:T(8,128)(2,1)S(1)} %all_to_all.35.column), channel_id=1, source_target_pairs={{0,1},{1,0},{2,3},{3,2},{4,5},{5,4},{6,7},{7,6},{8,9},{9,8},{10,11... | collective-permute-start | bytes 196616 | tf_op jit(solution)/shard_map/ppermute | solution.py:459
  40.5 0.9 collective-permute-done.partner
  41.4 5.6 %own.1 = (bf16[2,2,1024,256]{3,2,1,0:T(8,128)(2,1)}, f32[8,128]{1,0:T(8,128)}) custom-call(f32[4]{0:T(128)} %wave.5, bf16[16,16,128]{2,1,0:T(8,128)(2,1)S(1)} %all_to_all.35.column, bf16[16,16,128]{2,1,0:T(8,128)(2,1)S(1)} %collective-permute-done.partner, bf16[2,16,128]{2,1,0:T(8,128)(2,1)S(1)} %get-tuple-element.24.panel_rows), custom_call_target="tpu_custom_call" | custom-call | flops 2000000000 | bytes 2097152 | tf_op jit(solution)/shard_map/own/pallas_call | solution.py:294
  47.0 0.0 all-to-all-done.1.mine
  47.0 4.3 %collective-permute-start.1 = (bf16[16,144,128]{2,1,0:T(8,128)(2,1)S(1)}, bf16[16,144,128]{2,1,0:T(8,128)(2,1)S(1)}, u32[]{:S(2)}, u32[]{:S(2)}) collective-permute-start(bf16[16,144,128]{2,1,0:T(8,128)(2,1)S(1)} %all-to-all-done.1.mine), channel_id=1, source_target_pairs={{0,1},{1,0},{2,3},{3,2},{4,5},{5,4},{6,7},{7,6},{8,9},{9,8},{10,11... | collective-permute-start | bytes 1769480 | tf_op jit(solution)/shard_map/ppermute | solution.py:462
  51.3 1.6 %collective-permute-done.1.other = bf16[16,144,128]{2,1,0:T(8,128)(2,1)S(1)} collective-permute-done((bf16[16,144,128]{2,1,0:T(8,128)(2,1)S(1)}, bf16[16,144,128]{2,1,0:T(8,128)(2,1)S(1)}, u32[]{:S(2)}, u32[]{:S(2)}) %collective-permute-start.1) | collective-permute-done | bytes 589856 | tf_op jit(solution)/shard_map/ppermute | solution.py:462
  52.9 2.4 %velocity.1 = (bf16[2,128,256]{2,1,0:T(8,128)(2,1)S(1)}, bf16[2,128,256]{2,1,0:T(8,128)(2,1)S(1)}, f32[4,128]{1,0:T(4,128)S(1)}) custom-call(bf16[16,144,128]{2,1,0:T(8,128)(2,1)S(1)} %all-to-all-done.1.mine, bf16[16,144,128]{2,1,0:T(8,128)(2,1)S(1)} %collective-permute-done.1.other, bf16[4,2,128,512]{3,2,1,0:T(8,128)(2,1)} %response.1), custom_call_target="tpu_custom_call" | custom-call | flops 268435456 | bytes 3145728 | tf_op jit(solution)/shard_map/velocity/pallas_call | solution.py:74
  55.3 2.3 %collective-permute-start.2 = (bf16[2,128,256]{2,1,0:T(8,128)(2,1)S(1)}, bf16[2,128,256]{2,1,0:T(8,128)(2,1)S(1)}, u32[]{:S(2)}, u32[]{:S(2)}) collective-permute-start(bf16[2,128,256]{2,1,0:T(8,128)(2,1)S(1)} %get-tuple-element.39), channel_id=1, source_target_pairs={{0,1},{1,0},{2,3},{3,2},{4,5},{5,4},{6,7},{7,6},{8,9},{9,8},{10,11... | collective-permute-start | bytes 393224 | tf_op jit(solution)/shard_map/ppermute | solution.py:464
  57.6 1.0 collective-permute-done.2.got
  58.6 1.1 pack.1
  59.7 3.5 %all-to-all-start.2 = ((bf16[4,2,2,128,256]{4,3,2,1,0:T(8,128)(2,1)}), bf16[4,2,2,128,256]{4,3,2,1,0:T(8,128)(2,1)S(1)}, u32[]{:S(2)}, u32[]{:S(2)}) async-start(bf16[4,2,2,128,256]{4,3,2,1,0:T(8,128)(2,1)} %pack.1), calls=%async_computation.2 | async-start | bytes 2097152 | tf_op jit(solution)/shard_map/all_to_all | solution.py:444
  63.2 0.8 copy-done.1
  64.1 0.8 copy-done.3
  64.9 12.5 %rest.1 = (bf16[6,2,1024,256]{3,2,1,0:T(8,128)(2,1)}, f32[8,128]{1,0:T(8,128)}) custom-call(f32[4]{0:T(128)} %wave.5, bf16[16,16,128]{2,1,0:T(8,128)(2,1)S(1)} %copy-done.1, bf16[16,16,128]{2,1,0:T(8,128)(2,1)S(1)} %copy-done.3, bf16[16,144,128]{2,1,0:T(8,128)(2,1)S(1)} %all-to-all-done.1.mine, bf16[16,144,128]{2,1,0:T(8,128)(2,1)S(1)} %collective-permute-done.1.other, ...), custom_call_target="tpu_custom_call" | custom-call | flops 6000000000 | bytes 6291456 | tf_op jit(solution)/shard_map/rest/pallas_call | solution.py:294
  77.4 0.0 all-to-all-done.2.refs_8_
  77.4 6.2 %partial.1 = bf16[4,2,256,256]{3,2,1,0:T(8,128)(2,1)} custom-call(bf16[2,2,1024,256]{3,2,1,0:T(8,128)(2,1)} %get-tuple-element.25.refs_0_.refs_4_, bf16[6,2,1024,256]{3,2,1,0:T(8,128)(2,1)} %get-tuple-element.37.refs_1_.refs_2_.refs_3_.refs_5_.refs_6_.refs_7_, bf16[6,2,1024,256]{3,2,1,0:T(8,128)(2,1)} %get-tuple-element.37.refs_1_.refs_2_.refs_3_.refs_5_.refs_6_.refs_7_, ...), custom_call_target="tpu_custom_call" | custom-call | flops 2147483648 | bytes 10485760 | tf_op jit(solution)/shard_map/partial/pallas_call | solution.py:358
  83.6 13.5 %all_to_all.36.beside = bf16[4,2,256,256]{3,2,1,0:T(8,128)(2,1)S(1)} all-to-all(bf16[4,2,256,256]{3,2,1,0:T(8,128)(2,1)} %partial.1), channel_id=1, replica_groups={{0,32,64,96},{128,160,192,224},{256,288,320,352},{384,416,448,480},{1,1..., dimensions={0} | all-to-all | bytes 2097152 | tf_op jit(solution)/shard_map/all_to_all | solution.py:444
  97.1 0.1 level.1
  97.2 15.7 %all_to_all.37.column = bf16[16,32,256]{2,1,0:T(8,128)(2,1)S(1)} all-to-all(bf16[16,32,256]{2,1,0:T(8,128)(2,1)S(1)} %level.1), channel_id=1, replica_groups=mesh['s'=16,'zl'=4,'zh'=4,'c'=2] {'zh','zl'}, dimensions={0} | all-to-all | bytes 524288 | tf_op jit(solution)/shard_map/all_to_all | solution.py:444
  112.9 1.4 finish.1
  114.3 12.0 %all-to-all-start.5 = ((f32[32,8,128]{2,1,0:T(8,128)}), f32[32,8,128]{2,1,0:T(8,128)S(1)}, u32[]{:S(2)}, u32[]{:S(2)}) async-start(f32[32,8,128]{2,1,0:T(8,128)} %get-tuple-element.43), calls=%async_computation.5 | async-start | bytes 262144 | tf_op jit(solution)/shard_map/all_to_all | solution.py:444
  126.3 2.1 %collective-permute-start.3 = (bf16[16,256]{1,0:T(8,128)(2,1)S(1)}, bf16[16,256]{1,0:T(8,128)(2,1)S(1)}, u32[]{:S(2)}, u32[]{:S(2)}) collective-permute-start(bf16[16,256]{1,0:T(8,128)(2,1)S(1)} %get-tuple-element.42), channel_id=1, source_target_pairs={{0,1},{1,0},{2,3},{3,2},{4,5},{5,4},{6,7},{7,6},{8,9},{9,8},{10,11... | collective-permute-start | bytes 24584 | tf_op jit(solution)/shard_map/ppermute | solution.py:475
  128.4 5.5 %all-to-all-done.5.table = f32[32,8,128]{2,1,0:T(8,128)S(1)} async-done(((f32[32,8,128]{2,1,0:T(8,128)}), f32[32,8,128]{2,1,0:T(8,128)S(1)}, u32[]{:S(2)}, u32[]{:S(2)}) %all-to-all-start.5) | async-done | bytes 131104 | tf_op jit(solution)/shard_map/all_to_all | solution.py:444
  134.0 0.7 fold.1
  134.6 5.1 %all-to-all-start.6 = ((f32[16,8,128]{2,1,0:T(8,128)}), f32[16,8,128]{2,1,0:T(8,128)S(1)}, u32[]{:S(2)}, u32[]{:S(2)}) async-start(f32[16,8,128]{2,1,0:T(8,128)} %fold.1), calls=%async_computation.6 | async-start | bytes 131072 | tf_op jit(solution)/shard_map/all_to_all | solution.py:444
  139.7 0.6 copy.10
  140.3 10.9 %all-to-all-done.6 = f32[16,8,128]{2,1,0:T(8,128)S(1)} async-done(((f32[16,8,128]{2,1,0:T(8,128)}), f32[16,8,128]{2,1,0:T(8,128)S(1)}, u32[]{:S(2)}, u32[]{:S(2)}) %all-to-all-start.6) | async-done | bytes 65568 | tf_op jit(solution)/shard_map/all_to_all | solution.py:444
  151.3 0.6 add_divide_fusion
  (10 shorter events, 0.0 us)
Async XLA Ops:
  28.6 24.3 %copy-start = (bf16[16,16,128]{2,1,0:T(8,128)(2,1)}, bf16[16,16,128]{2,1,0:T(8,128)(2,1)S(1)}, u32[]{:S(2)}) copy-start(bf16[16,16,128]{2,1,0:T(8,128)(2,1)S(1)} %all_to_all.35.column) | copy-start | bytes 196612
  29.5 17.5 %all-to-all-start.1 = ((bf16[16,144,128]{2,1,0:T(8,128)(2,1)}), bf16[16,144,128]{2,1,0:T(8,128)(2,1)S(1)}, u32[]{:S(2)}, u32[]{:S(2)}) async-start(bf16[16,144,128]{2,1,0:T(8,128)(2,1)} %spread.1), calls=%async_computation.1 | async-start | bytes 1179648 | tf_op jit(solution)/shard_map/all_to_all | solution.py:444
  36.2 5.2 %collective-permute-start = (bf16[16,16,128]{2,1,0:T(8,128)(2,1)S(1)}, bf16[16,16,128]{2,1,0:T(8,128)(2,1)S(1)}, u32[]{:S(2)}, u32[]{:S(2)}) collective-permute-start(bf16[16,16,128]{2,1,0:T(8,128)(2,1)S(1)} %all_to_all.35.column), channel_id=1, source_target_pairs={{0,1},{1,0},{2,3},{3,2},{4,5},{5,4},{6,7},{7,6},{8,9},{9,8},{10,11... | collective-permute-start | bytes 196616 | tf_op jit(solution)/shard_map/ppermute | solution.py:459
  41.4 9.9 %copy-start.2 = (bf16[16,16,128]{2,1,0:T(8,128)(2,1)}, bf16[16,16,128]{2,1,0:T(8,128)(2,1)S(1)}, u32[]{:S(2)}) copy-start(bf16[16,16,128]{2,1,0:T(8,128)(2,1)S(1)} %collective-permute-done.partner) | copy-start | bytes 196612
  47.0 5.9 %collective-permute-start.1 = (bf16[16,144,128]{2,1,0:T(8,128)(2,1)S(1)}, bf16[16,144,128]{2,1,0:T(8,128)(2,1)S(1)}, u32[]{:S(2)}, u32[]{:S(2)}) collective-permute-start(bf16[16,144,128]{2,1,0:T(8,128)(2,1)S(1)} %all-to-all-done.1.mine), channel_id=1, source_target_pairs={{0,1},{1,0},{2,3},{3,2},{4,5},{5,4},{6,7},{7,6},{8,9},{9,8},{10,11... | collective-permute-start | bytes 1769480 | tf_op jit(solution)/shard_map/ppermute | solution.py:462
  55.3 3.3 %collective-permute-start.2 = (bf16[2,128,256]{2,1,0:T(8,128)(2,1)S(1)}, bf16[2,128,256]{2,1,0:T(8,128)(2,1)S(1)}, u32[]{:S(2)}, u32[]{:S(2)}) collective-permute-start(bf16[2,128,256]{2,1,0:T(8,128)(2,1)S(1)} %get-tuple-element.39), channel_id=1, source_target_pairs={{0,1},{1,0},{2,3},{3,2},{4,5},{5,4},{6,7},{7,6},{8,9},{9,8},{10,11... | collective-permute-start | bytes 393224 | tf_op jit(solution)/shard_map/ppermute | solution.py:464
  59.7 17.7 %all-to-all-start.2 = ((bf16[4,2,2,128,256]{4,3,2,1,0:T(8,128)(2,1)}), bf16[4,2,2,128,256]{4,3,2,1,0:T(8,128)(2,1)S(1)}, u32[]{:S(2)}, u32[]{:S(2)}) async-start(bf16[4,2,2,128,256]{4,3,2,1,0:T(8,128)(2,1)} %pack.1), calls=%async_computation.2 | async-start | bytes 2097152 | tf_op jit(solution)/shard_map/all_to_all | solution.py:444
  63.2 0.8 copy-start.1
  64.1 0.8 copy-start.3
  114.3 19.7 %all-to-all-start.5 = ((f32[32,8,128]{2,1,0:T(8,128)}), f32[32,8,128]{2,1,0:T(8,128)S(1)}, u32[]{:S(2)}, u32[]{:S(2)}) async-start(f32[32,8,128]{2,1,0:T(8,128)} %get-tuple-element.43), calls=%async_computation.5 | async-start | bytes 262144 | tf_op jit(solution)/shard_map/all_to_all | solution.py:444
  126.3 13.4 %collective-permute-start.3 = (bf16[16,256]{1,0:T(8,128)(2,1)S(1)}, bf16[16,256]{1,0:T(8,128)(2,1)S(1)}, u32[]{:S(2)}, u32[]{:S(2)}) collective-permute-start(bf16[16,256]{1,0:T(8,128)(2,1)S(1)} %get-tuple-element.42), channel_id=1, source_target_pairs={{0,1},{1,0},{2,3},{3,2},{4,5},{5,4},{6,7},{7,6},{8,9},{9,8},{10,11... | collective-permute-start | bytes 24584 | tf_op jit(solution)/shard_map/ppermute | solution.py:475
  134.6 16.7 %all-to-all-start.6 = ((f32[16,8,128]{2,1,0:T(8,128)}), f32[16,8,128]{2,1,0:T(8,128)S(1)}, u32[]{:S(2)}, u32[]{:S(2)}) async-start(f32[16,8,128]{2,1,0:T(8,128)} %fold.1), calls=%async_computation.6 | async-start | bytes 131072 | tf_op jit(solution)/shard_map/all_to_all | solution.py:444

commit v6 on v5

--- a/solution.py
+++ b/solution.py
@@ -260,11 +260,13 @@
     turns = [wave[place("c") * lines + line] * (0.5 / math.pi) for line in range(lines)]
 
     def strip(index, carry):
-        rows = pl.ds(pl.multiple_of(index * STRIP, STRIP), STRIP)
+        rows = pl.ds(pl.multiple_of(index * 64, 64), 64)
         dx = px[rows, :] - across
         dy = py[rows, :] - along
-        distance = jnp.sqrt(dx * dx + dy * dy + pz[rows, :])
-        gain = area / distance
+        square = dx * dx + dy * dy + pz[rows, :]
+        inverse = lax.rsqrt(square)
+        distance = square * inverse
+        gain = area * inverse
         opposite = -gain
         for line in range(lines):
             turn = distance * turns[line]
@@ -278,14 +280,14 @@
             out[0, line, rows, LANES : 2 * LANES] = (gain * cosine).astype(BF16)
         return carry
 
-    lax.fori_loop(0, out.shape[2] // STRIP, strip, 0)
+    lax.fori_loop(0, out.shape[2] // 64, strip, 0)
 
 
 def pinned_to_vmem(array):
     return array if INTERPRET else pltpu.with_memory_space_constraint(array, pltpu.VMEM)
 
 
-def make_tiles(kernel, wave, arrays, grid, name, after=()):
+def make_tiles(kernel, wave, columns, arrays, grid, name, after=()):
     points = 8 * LANES
     lines = wave.shape[0] // 2
     vmem = pl.BlockSpec(memory_space=pltpu.VMEM)
@@ -299,6 +301,7 @@
         ),
         grid=grid,
         in_specs=[pl.BlockSpec(memory_space=pltpu.SMEM)]
+        + [pl.BlockSpec(columns[0].shape, lambda *_: (0, 0, 0))] * 2
         + [vmem] * len(arrays)
         + [pl.BlockSpec(memory_space=pl.ANY)] * len(after),
         out_specs=(
@@ -312,18 +315,18 @@
         cost_estimate=cost(steps * 1_000_000_000, steps << 20),
         interpret=INTERPRET,
         name=name,
-    )(wave, *[pinned_to_vmem(array) for array in arrays], *after)
+    )(wave, *columns, *[pinned_to_vmem(array) for array in arrays], *after)
 
 
 def make_own(place, wave, column, partner, panel_rows):
     kernel = functools.partial(own_kernel, place)
-    return make_tiles(kernel, wave, [column, partner, panel_rows], (2,), "own")
+    return make_tiles(kernel, wave, [column, partner], [panel_rows], (2,), "own")
 
 
 def make_rest(place, wave, column, partner, mine, other, before):
     kernel = functools.partial(rest_kernel, place)
-    arrays = [column, partner, mine, other]
-    return make_tiles(kernel, wave, arrays, (2, 3), "rest", (before,))
+    arrays = [mine, other]
+    return make_tiles(kernel, wave, [column, partner], arrays, (2, 3), "rest", (before,))
 
 
 def partial_kernel(place, *refs):

time: 153 us -> 150 us (0.980)
  Pallas kernels: 31.7 us -> 29.9 us
    pallas_call x2, Pallas kernels: 18 us -> 16.2 us  [make_tiles(): pl.pallas_call(kernel, out_shape=(jax.ShapeDtypeStruct((steps, lines, poi...]
  transfers between devices with their start and end apart: 8 -> 8, of which waited for: 5 -> 5; matrix products, arithmetic and copies ran while one was open for 0% -> 0% of each run, Pallas kernels for 12% -> 11%
where the time goes in v6:
time: 150 us; the launch traced here: 149 us
  blocking collectives  56.3 us (38%)
  starting transfers between devices  40 us (27%)
  Pallas kernels  29.9 us (20%)
  waiting for transfers between devices  19.9 us (13%)
    all_to_all x3, blocking collectives, exchange(): lax.all_to_all(array, axes, 0, 0, tiled=True, axis_index_groups=groups)  56.3 us
    all_to_all x4, starting transfers between devices, exchange(): lax.all_to_all(array, axes, 0, 0, tiled=True, axis_index_groups=groups)  27.3 us
    all_to_all x4, waiting for transfers between devices, exchange(): lax.all_to_all(array, axes, 0, 0, tiled=True, axis_index_groups=groups)  16.5 us
    pallas_call x2, Pallas kernels, make_tiles(): pl.pallas_call(kernel, out_shape=(jax.ShapeDtypeStruct((steps, lines, poi...  16.2 us
    pallas_call x7, Pallas kernels, call(): pl.pallas_call(kernel, out_shape=results, in_specs=[pl.BlockSpec(memory_s...  7.47 us
    pallas_call x1, Pallas kernels, make_partial(): pl.pallas_call(functools.partial(partial_kernel, place), out_shape=jax.Sh...  6.22 us
    ppermute x1, starting transfers between devices, shards(): partner = lax.ppermute(column, 'c', SWAP)  4.3 us
    ppermute x1, starting transfers between devices, shards(): other = lax.ppermute(mine, 'c', SWAP)  4.04 us
  transfers between devices with their start and end apart: 8, of which 5 were waited for; matrix products, arithmetic and copies ran while one was open for 0% of the time, Pallas kernels for 11%

profile of v6, /device:TPU:1, one launch (start us, length us, event | category | flops | bytes accessed | tf_op | source)
XLA Modules:
  0.0 148.7 jit_solution(4471909776708571993)
XLA Ops:
  0.6 0.8 start.1
  1.5 27.1 %all_to_all.35.column = bf16[16,16,128]{2,1,0:T(8,128)(2,1)S(1)} all-to-all(bf16[16,16,128]{2,1,0:T(8,128)(2,1)S(1)} %get-tuple-element.23), channel_id=1, replica_groups=mesh['s'=16,'zl'=4,'zh'=4,'c'=2] {'zh','zl'}, dimensions={0} | all-to-all | bytes 131072 | tf_op jit(solution)/shard_map/all_to_all | solution.py:447
  28.6 0.9 spread.1
  29.5 6.8 %all-to-all-start.1 = ((bf16[16,144,128]{2,1,0:T(8,128)(2,1)}), bf16[16,144,128]{2,1,0:T(8,128)(2,1)S(1)}, u32[]{:S(2)}, u32[]{:S(2)}) async-start(bf16[16,144,128]{2,1,0:T(8,128)(2,1)} %spread.1), calls=%async_computation.1 | async-start | bytes 1179648 | tf_op jit(solution)/shard_map/all_to_all | solution.py:447
  36.2 4.3 %collective-permute-start = (bf16[16,16,128]{2,1,0:T(8,128)(2,1)S(1)}, bf16[16,16,128]{2,1,0:T(8,128)(2,1)S(1)}, u32[]{:S(2)}, u32[]{:S(2)}) collective-permute-start(bf16[16,16,128]{2,1,0:T(8,128)(2,1)S(1)} %all_to_all.35.column), channel_id=1, source_target_pairs={{0,1},{1,0},{2,3},{3,2},{4,5},{5,4},{6,7},{7,6},{8,9},{9,8},{10,11... | collective-permute-start | bytes 196616 | tf_op jit(solution)/shard_map/ppermute | solution.py:462
  40.5 0.9 collective-permute-done.partner
  41.4 0.6 copy-done.1
  42.1 5.2 %own.1 = (bf16[2,2,1024,256]{3,2,1,0:T(8,128)(2,1)}, f32[8,128]{1,0:T(8,128)}) custom-call(f32[4]{0:T(128)} %wave.5, bf16[16,16,128]{2,1,0:T(8,128)(2,1)} %copy-done, bf16[16,16,128]{2,1,0:T(8,128)(2,1)} %copy-done.1, bf16[2,16,128]{2,1,0:T(8,128)(2,1)S(1)} %get-tuple-element.24.panel_rows), custom_call_target="tpu_custom_call" | custom-call | flops 2000000000 | bytes 2097152 | tf_op jit(solution)/shard_map/own/pallas_call | solution.py:296
  47.2 0.0 all-to-all-done.1.mine
  47.2 4.0 %collective-permute-start.1 = (bf16[16,144,128]{2,1,0:T(8,128)(2,1)S(1)}, bf16[16,144,128]{2,1,0:T(8,128)(2,1)S(1)}, u32[]{:S(2)}, u32[]{:S(2)}) collective-permute-start(bf16[16,144,128]{2,1,0:T(8,128)(2,1)S(1)} %all-to-all-done.1.mine), channel_id=1, source_target_pairs={{0,1},{1,0},{2,3},{3,2},{4,5},{5,4},{6,7},{7,6},{8,9},{9,8},{10,11... | collective-permute-start | bytes 1769480 | tf_op jit(solution)/shard_map/ppermute | solution.py:465
  51.3 1.6 %collective-permute-done.1.other = bf16[16,144,128]{2,1,0:T(8,128)(2,1)S(1)} collective-permute-done((bf16[16,144,128]{2,1,0:T(8,128)(2,1)S(1)}, bf16[16,144,128]{2,1,0:T(8,128)(2,1)S(1)}, u32[]{:S(2)}, u32[]{:S(2)}) %collective-permute-start.1) | collective-permute-done | bytes 589856 | tf_op jit(solution)/shard_map/ppermute | solution.py:465
  52.9 2.4 %velocity.1 = (bf16[2,128,256]{2,1,0:T(8,128)(2,1)S(1)}, bf16[2,128,256]{2,1,0:T(8,128)(2,1)S(1)}, f32[4,128]{1,0:T(4,128)S(1)}) custom-call(bf16[16,144,128]{2,1,0:T(8,128)(2,1)S(1)} %all-to-all-done.1.mine, bf16[16,144,128]{2,1,0:T(8,128)(2,1)S(1)} %collective-permute-done.1.other, bf16[4,2,128,512]{3,2,1,0:T(8,128)(2,1)} %response.1), custom_call_target="tpu_custom_call" | custom-call | flops 268435456 | bytes 3145728 | tf_op jit(solution)/shard_map/velocity/pallas_call | solution.py:74
  55.3 2.3 %collective-permute-start.2 = (bf16[2,128,256]{2,1,0:T(8,128)(2,1)S(1)}, bf16[2,128,256]{2,1,0:T(8,128)(2,1)S(1)}, u32[]{:S(2)}, u32[]{:S(2)}) collective-permute-start(bf16[2,128,256]{2,1,0:T(8,128)(2,1)S(1)} %get-tuple-element.39), channel_id=1, source_target_pairs={{0,1},{1,0},{2,3},{3,2},{4,5},{5,4},{6,7},{7,6},{8,9},{9,8},{10,11... | collective-permute-start | bytes 393224 | tf_op jit(solution)/shard_map/ppermute | solution.py:467
  57.6 1.0 collective-permute-done.2.got
  58.6 1.1 pack.1
  59.7 3.5 %all-to-all-start.2 = ((bf16[4,2,2,128,256]{4,3,2,1,0:T(8,128)(2,1)}), bf16[4,2,2,128,256]{4,3,2,1,0:T(8,128)(2,1)S(1)}, u32[]{:S(2)}, u32[]{:S(2)}) async-start(bf16[4,2,2,128,256]{4,3,2,1,0:T(8,128)(2,1)} %pack.1), calls=%async_computation.2 | async-start | bytes 2097152 | tf_op jit(solution)/shard_map/all_to_all | solution.py:447
  63.2 11.0 %rest.1 = (bf16[6,2,1024,256]{3,2,1,0:T(8,128)(2,1)}, f32[8,128]{1,0:T(8,128)}) custom-call(f32[4]{0:T(128)} %wave.5, bf16[16,16,128]{2,1,0:T(8,128)(2,1)} %copy-done, bf16[16,16,128]{2,1,0:T(8,128)(2,1)} %copy-done.1, bf16[16,144,128]{2,1,0:T(8,128)(2,1)S(1)} %all-to-all-done.1.mine, bf16[16,144,128]{2,1,0:T(8,128)(2,1)S(1)} %collective-permute-done.1.other, ...), custom_call_target="tpu_custom_call" | custom-call | flops 6000000000 | bytes 6291456 | tf_op jit(solution)/shard_map/rest/pallas_call | solution.py:296
  74.2 0.0 all-to-all-done.2.refs_8_
  74.2 6.2 %partial.1 = bf16[4,2,256,256]{3,2,1,0:T(8,128)(2,1)} custom-call(bf16[2,2,1024,256]{3,2,1,0:T(8,128)(2,1)} %get-tuple-element.25.refs_0_.refs_4_, bf16[6,2,1024,256]{3,2,1,0:T(8,128)(2,1)} %get-tuple-element.37.refs_1_.refs_2_.refs_3_.refs_5_.refs_6_.refs_7_, bf16[6,2,1024,256]{3,2,1,0:T(8,128)(2,1)} %get-tuple-element.37.refs_1_.refs_2_.refs_3_.refs_5_.refs_6_.refs_7_, ...), custom_call_target="tpu_custom_call" | custom-call | flops 2147483648 | bytes 10485760 | tf_op jit(solution)/shard_map/partial/pallas_call | solution.py:361
  80.5 13.5 %all_to_all.36.beside = bf16[4,2,256,256]{3,2,1,0:T(8,128)(2,1)S(1)} all-to-all(bf16[4,2,256,256]{3,2,1,0:T(8,128)(2,1)} %partial.1), channel_id=1, replica_groups={{0,32,64,96},{128,160,192,224},{256,288,320,352},{384,416,448,480},{1,1..., dimensions={0} | all-to-all | bytes 2097152 | tf_op jit(solution)/shard_map/all_to_all | solution.py:447
  94.0 0.1 level.1
  94.1 15.7 %all_to_all.37.column = bf16[16,32,256]{2,1,0:T(8,128)(2,1)S(1)} all-to-all(bf16[16,32,256]{2,1,0:T(8,128)(2,1)S(1)} %level.1), channel_id=1, replica_groups=mesh['s'=16,'zl'=4,'zh'=4,'c'=2] {'zh','zl'}, dimensions={0} | all-to-all | bytes 524288 | tf_op jit(solution)/shard_map/all_to_all | solution.py:447
  109.8 1.4 finish.1
  111.2 11.9 %all-to-all-start.5 = ((f32[32,8,128]{2,1,0:T(8,128)}), f32[32,8,128]{2,1,0:T(8,128)S(1)}, u32[]{:S(2)}, u32[]{:S(2)}) async-start(f32[32,8,128]{2,1,0:T(8,128)} %get-tuple-element.43), calls=%async_computation.5 | async-start | bytes 262144 | tf_op jit(solution)/shard_map/all_to_all | solution.py:447
  123.1 2.1 %collective-permute-start.3 = (bf16[16,256]{1,0:T(8,128)(2,1)S(1)}, bf16[16,256]{1,0:T(8,128)(2,1)S(1)}, u32[]{:S(2)}, u32[]{:S(2)}) collective-permute-start(bf16[16,256]{1,0:T(8,128)(2,1)S(1)} %get-tuple-element.42), channel_id=1, source_target_pairs={{0,1},{1,0},{2,3},{3,2},{4,5},{5,4},{6,7},{7,6},{8,9},{9,8},{10,11... | collective-permute-start | bytes 24584 | tf_op jit(solution)/shard_map/ppermute | solution.py:478
  125.3 5.5 %all-to-all-done.5.table = f32[32,8,128]{2,1,0:T(8,128)S(1)} async-done(((f32[32,8,128]{2,1,0:T(8,128)}), f32[32,8,128]{2,1,0:T(8,128)S(1)}, u32[]{:S(2)}, u32[]{:S(2)}) %all-to-all-start.5) | async-done | bytes 131104 | tf_op jit(solution)/shard_map/all_to_all | solution.py:447
  130.8 0.7 fold.1
  131.5 5.1 %all-to-all-start.6 = ((f32[16,8,128]{2,1,0:T(8,128)}), f32[16,8,128]{2,1,0:T(8,128)S(1)}, u32[]{:S(2)}, u32[]{:S(2)}) async-start(f32[16,8,128]{2,1,0:T(8,128)} %fold.1), calls=%async_computation.6 | async-start | bytes 131072 | tf_op jit(solution)/shard_map/all_to_all | solution.py:447
  136.5 0.0 collective-permute-done.3
  136.6 0.6 copy.10
  137.2 10.9 %all-to-all-done.6 = f32[16,8,128]{2,1,0:T(8,128)S(1)} async-done(((f32[16,8,128]{2,1,0:T(8,128)}), f32[16,8,128]{2,1,0:T(8,128)S(1)}, u32[]{:S(2)}, u32[]{:S(2)}) %all-to-all-start.6) | async-done | bytes 65568 | tf_op jit(solution)/shard_map/all_to_all | solution.py:447
  148.1 0.6 add_divide_fusion
  (6 shorter events, 0.0 us)
Async XLA Ops:
  28.6 12.9 %copy-start = (bf16[16,16,128]{2,1,0:T(8,128)(2,1)}, bf16[16,16,128]{2,1,0:T(8,128)(2,1)S(1)}, u32[]{:S(2)}) copy-start(bf16[16,16,128]{2,1,0:T(8,128)(2,1)S(1)} %all_to_all.35.column) | copy-start | bytes 196612
  29.5 17.8 %all-to-all-start.1 = ((bf16[16,144,128]{2,1,0:T(8,128)(2,1)}), bf16[16,144,128]{2,1,0:T(8,128)(2,1)S(1)}, u32[]{:S(2)}, u32[]{:S(2)}) async-start(bf16[16,144,128]{2,1,0:T(8,128)(2,1)} %spread.1), calls=%async_computation.1 | async-start | bytes 1179648 | tf_op jit(solution)/shard_map/all_to_all | solution.py:447
  36.2 5.2 %collective-permute-start = (bf16[16,16,128]{2,1,0:T(8,128)(2,1)S(1)}, bf16[16,16,128]{2,1,0:T(8,128)(2,1)S(1)}, u32[]{:S(2)}, u32[]{:S(2)}) collective-permute-start(bf16[16,16,128]{2,1,0:T(8,128)(2,1)S(1)} %all_to_all.35.column), channel_id=1, source_target_pairs={{0,1},{1,0},{2,3},{3,2},{4,5},{5,4},{6,7},{7,6},{8,9},{9,8},{10,11... | collective-permute-start | bytes 196616 | tf_op jit(solution)/shard_map/ppermute | solution.py:462
  41.4 0.6 copy-start.1
  47.2 5.7 %collective-permute-start.1 = (bf16[16,144,128]{2,1,0:T(8,128)(2,1)S(1)}, bf16[16,144,128]{2,1,0:T(8,128)(2,1)S(1)}, u32[]{:S(2)}, u32[]{:S(2)}) collective-permute-start(bf16[16,144,128]{2,1,0:T(8,128)(2,1)S(1)} %all-to-all-done.1.mine), channel_id=1, source_target_pairs={{0,1},{1,0},{2,3},{3,2},{4,5},{5,4},{6,7},{7,6},{8,9},{9,8},{10,11... | collective-permute-start | bytes 1769480 | tf_op jit(solution)/shard_map/ppermute | solution.py:465
  55.3 3.3 %collective-permute-start.2 = (bf16[2,128,256]{2,1,0:T(8,128)(2,1)S(1)}, bf16[2,128,256]{2,1,0:T(8,128)(2,1)S(1)}, u32[]{:S(2)}, u32[]{:S(2)}) collective-permute-start(bf16[2,128,256]{2,1,0:T(8,128)(2,1)S(1)} %get-tuple-element.39), channel_id=1, source_target_pairs={{0,1},{1,0},{2,3},{3,2},{4,5},{5,4},{6,7},{7,6},{8,9},{9,8},{10,11... | collective-permute-start | bytes 393224 | tf_op jit(solution)/shard_map/ppermute | solution.py:467
  59.7 14.5 %all-to-all-start.2 = ((bf16[4,2,2,128,256]{4,3,2,1,0:T(8,128)(2,1)}), bf16[4,2,2,128,256]{4,3,2,1,0:T(8,128)(2,1)S(1)}, u32[]{:S(2)}, u32[]{:S(2)}) async-start(bf16[4,2,2,128,256]{4,3,2,1,0:T(8,128)(2,1)} %pack.1), calls=%async_computation.2 | async-start | bytes 2097152 | tf_op jit(solution)/shard_map/all_to_all | solution.py:447
  111.2 19.6 %all-to-all-start.5 = ((f32[32,8,128]{2,1,0:T(8,128)}), f32[32,8,128]{2,1,0:T(8,128)S(1)}, u32[]{:S(2)}, u32[]{:S(2)}) async-start(f32[32,8,128]{2,1,0:T(8,128)} %get-tuple-element.43), calls=%async_computation.5 | async-start | bytes 262144 | tf_op jit(solution)/shard_map/all_to_all | solution.py:447
  123.1 13.4 %collective-permute-start.3 = (bf16[16,256]{1,0:T(8,128)(2,1)S(1)}, bf16[16,256]{1,0:T(8,128)(2,1)S(1)}, u32[]{:S(2)}, u32[]{:S(2)}) collective-permute-start(bf16[16,256]{1,0:T(8,128)(2,1)S(1)} %get-tuple-element.42), channel_id=1, source_target_pairs={{0,1},{1,0},{2,3},{3,2},{4,5},{5,4},{6,7},{7,6},{8,9},{9,8},{10,11... | collective-permute-start | bytes 24584 | tf_op jit(solution)/shard_map/ppermute | solution.py:478
  131.5 16.7 %all-to-all-start.6 = ((f32[16,8,128]{2,1,0:T(8,128)}), f32[16,8,128]{2,1,0:T(8,128)S(1)}, u32[]{:S(2)}, u32[]{:S(2)}) async-start(f32[16,8,128]{2,1,0:T(8,128)} %fold.1), calls=%async_computation.6 | async-start | bytes 131072 | tf_op jit(solution)/shard_map/all_to_all | solution.py:447
